TPU v7x, 32 devices: a whole 2x2x4 slice. The times are simulated.
32 devices in a mesh: row: 8 (over y, x, core), col: 4 (over z).
Axes of the slice: x: 2, y: 2, z: 4, core: 2. Of those that a mesh axis runs over, the one named last changes fastest.
Arguments:
- inputs: bfloat16 [4096, 2048], P('col', 'row'), may hold values from -6 to 6
- cotangent: bfloat16 [4096, 2048], P('col', 'row'), may hold values from -6 to 6
- seq_blocks: int32 [4], replicated, may hold values from 1 to 12, 16 in all
- first_gain: float32 [2048], P('row'), may hold values from 0.5 to 1.5
- first_shift: float32 [2048], P('row'), may hold values from -1.75 to 1.75
- w_query: bfloat16 [2048, 2048], P('row', 'col'), may hold values from -0.125 to 0.125
- b_query: float32 [2048], P('col'), may hold values from -3 to 3
- w_keyval: bfloat16 [2048, 256], P('row', 'col'), may hold values from -0.125 to 0.125
- b_value: float32 [128], replicated, may hold values from -0.3125 to 0.3125
- w_out: bfloat16 [2048, 2048], P('col', 'row'), may hold values from -2 to 2
- b_out: float32 [2048], P('row'), may hold values from -3 to 3
- second_gain: float32 [2048], P('row'), may hold values from 0.5 to 1.5
- second_shift: float32 [2048], P('row'), may hold values from -1.75 to 1.75
- w_up: bfloat16 [2048, 8192], P('row', 'col'), may hold values from -0.125 to 0.125
- b_up: float32 [8192], P('col'), may hold values from -3 to 3
- w_down: bfloat16 [8192, 2048], P('col', 'row'), may hold values from -0.125 to 0.125
- b_down: float32 [2048], P('row'), may hold values from -3 to 3
Outputs:
- block_output: bfloat16 [4096, 2048], P('col', 'row')
- grad_inputs: float32 [4096, 2048], P('col', 'row')
- grad_first_gain: float32 [2048], P('row')
- grad_first_shift: float32 [2048], P('row')
- grad_w_query: float32 [2048, 2048], P('row', 'col')
- grad_b_query: float32 [2048], P('col')
- grad_w_keyval: float32 [2048, 256], P('row', 'col')
- grad_b_value: float32 [128], replicated
- grad_w_out: float32 [2048, 2048], P('col', 'row')
- grad_b_out: float32 [2048], P('row')
- grad_second_gain: float32 [2048], P('row')
- grad_second_shift: float32 [2048], P('row')
- grad_w_up: float32 [2048, 8192], P('row', 'col')
- grad_b_up: float32 [8192], P('col')
- grad_w_down: float32 [8192, 2048], P('col', 'row')
- grad_b_down: float32 [2048], P('row')
Inputs may be any that keep to these rules, and one draw needn't show every extreme that they name: seq_blocks sums to 16, and its largest entry is exactly 12.
All inputs are finite; a program needn't handle non-finite values.
Results may differ from a plain program's by a relative error of at most 0.033.
Values may be sent and summed in bfloat16 or wider, within the bound.
No kernel may reach another device: no remote copies, remote signals or barrier semaphores. Data moves between devices by JAX's collectives and lax.ppermute only.
A program may use at most 320 MiB of HBM per device.

v0:
```python
from functools import partial

import jax
import jax.numpy as jnp
from jax import lax
from jax.sharding import PartitionSpec as P

BLK = 256
BQ = 512


EPSILON = 1e-05
NEGATIVE = -1e30


def spread_cols(value):
    return lax.all_gather(value, "col", axis=0, tiled=True)


def spread_rows(value):
    return lax.all_gather(value, "row", axis=0, tiled=True)


def fold_rows(maker, count):
    return lax.psum_scatter(
        maker(jnp.int32(0), count * lax.axis_size("row")).astype(jnp.bfloat16),
        "row",
        scatter_dimension=0,
        tiled=True,
    ).astype(jnp.float32)


def fold_cols(maker, count):
    return lax.psum_scatter(
        maker(jnp.int32(0), count * lax.axis_size("col")).astype(jnp.bfloat16),
        "col",
        scatter_dimension=0,
        tiled=True,
    ).astype(jnp.float32)


def feature_total(values):
    return lax.psum(values, "row")


def contract_first(left, right):
    return lax.dot_general(
        left, right, (((0,), (0,)), ((), ())), preferred_element_type=jnp.float32
    )


def contract_last(left, right):
    return lax.dot_general(
        left, right, (((1,), (1,)), ((), ())), preferred_element_type=jnp.float32
    )


def column_sums(values):
    return jnp.dot(
        jnp.ones((values.shape[0],), values.dtype), values, preferred_element_type=jnp.float32
    )


def place_slice(vector, length, index):
    return lax.dynamic_update_slice_in_dim(
        jnp.zeros((length,), jnp.float32), vector, index * vector.shape[0], 0
    )


def take_slice(vector, index, count):
    return lax.dynamic_slice_in_dim(vector, index * count, count, 0)


def norm_forward(inputs, width):
    mean = feature_total(jnp.sum(inputs, 1)) / width
    centred = inputs - mean[:, None]
    variance = feature_total(jnp.sum(centred * centred, 1)) / width
    scale = lax.rsqrt(variance + EPSILON)
    return ((inputs - mean[:, None]) * scale[:, None], scale)


def norm_backward(grad_out, normed, scale, gain, width):
    grad_normed = grad_out * gain[None, :]
    sum_plain, sum_cross = feature_total(
        (jnp.sum(grad_normed, 1), jnp.sum(grad_normed * normed, 1))
    )
    grad_in = scale[:, None] * (
        grad_normed - sum_plain[:, None] / width - normed * (sum_cross[:, None] / width)
    )
    return (grad_in, jnp.sum(grad_out * normed, 0), jnp.sum(grad_out, 0))


def sequence_ends(seq_blocks):
    ends = jnp.cumsum(seq_blocks) * BLK
    return (ends - seq_blocks * BLK, ends)


def sequence_index(positions, ends):
    return jnp.sum((positions[:, None] >= ends[None, :]).astype(jnp.int32), 1)


def block_allowed(query_pos, key_pos, ends):
    same = sequence_index(query_pos, ends)[:, None] == sequence_index(key_pos, ends)[None, :]
    return same & ((key_pos // BLK)[None, :] <= (query_pos // BLK)[:, None])


def key_range(query_first, span, starts, ends):
    owner = jnp.sum((query_first >= ends).astype(jnp.int32))
    key_low = jnp.sum(jnp.where(jnp.arange(ends.shape[0], dtype=jnp.int32) == owner, starts, 0))
    return (key_low // span, (query_first + span - 1) // span + 1)


def attend_forward(queries, key_values, row_first, seq_blocks, head_dim):
    rows_here = queries.shape[0]
    heads_here = queries.shape[1] // head_dim
    span = min(BQ, rows_here)
    starts, ends = sequence_ends(seq_blocks)
    scale = head_dim ** (-0.5)
    offsets = jnp.arange(span, dtype=jnp.int32)
    cores = []
    sums_log = []
    for index in range(rows_here // span):
        query_first = row_first + index * span
        query_pos = query_first + offsets
        block_query = queries[index * span : (index + 1) * span].reshape(span, heads_here, head_dim)

        def visit(position, state, query_pos=query_pos, block_query=block_query):
            running_max, running_sum, accum = state
            key_first = position * span
            block_kv = lax.dynamic_slice_in_dim(key_values, key_first, span, 0)
            allowed = block_allowed(query_pos, key_first + offsets, ends)[None]
            scores = (
                jnp.einsum(
                    "qhd,kd->hqk",
                    block_query,
                    block_kv[:, :head_dim],
                    preferred_element_type=jnp.float32,
                )
                * scale
            )
            scores = jnp.where(allowed, scores, NEGATIVE)
            new_max = jnp.maximum(running_max, jnp.max(scores, 2))
            factor = jnp.exp(running_max - new_max)
            weights = jnp.where(allowed, jnp.exp(scores - new_max[:, :, None]), 0.0)
            running_sum = running_sum * factor + jnp.sum(weights, 2)
            accum = accum * factor[:, :, None] + jnp.einsum(
                "hqk,kd->hqd",
                weights.astype(jnp.bfloat16),
                block_kv[:, head_dim:],
                preferred_element_type=jnp.float32,
            )
            return (new_max, running_sum, accum)

        key_low, key_high = key_range(query_first, span, starts, ends)
        initial = (
            jnp.full((heads_here, span), NEGATIVE, jnp.float32),
            jnp.zeros((heads_here, span), jnp.float32),
            jnp.zeros((heads_here, span, head_dim), jnp.float32),
        )
        running_max, running_sum, accum = lax.fori_loop(key_low, key_high, visit, initial)
        core = accum / running_sum[:, :, None]
        cores.append(jnp.transpose(core, (1, 0, 2)).reshape(span, heads_here * head_dim))
        sums_log.append(running_max + jnp.log(running_sum))
    return (jnp.concatenate(cores, 0), jnp.concatenate(sums_log, 1))


def attend_backward(queries, key_values, core, grad_low, sums_log, row_first, seq_blocks, head_dim):
    rows_here = queries.shape[0]
    heads_here = queries.shape[1] // head_dim
    span = min(BQ, rows_here)
    starts, ends = sequence_ends(seq_blocks)
    scale = head_dim ** (-0.5)
    offsets = jnp.arange(span, dtype=jnp.int32)
    delta_all = jnp.transpose(
        jnp.sum((grad_low.astype(jnp.float32) * core).reshape(rows_here, heads_here, head_dim), 2)
    )
    grad_keys = jnp.zeros((key_values.shape[0], 2 * head_dim), jnp.float32)
    grad_blocks = []
    for index in range(rows_here // span):
        query_first = row_first + index * span
        query_pos = query_first + offsets
        block_query = queries[index * span : (index + 1) * span].reshape(span, heads_here, head_dim)
        block_grad = grad_low[index * span : (index + 1) * span].reshape(span, heads_here, head_dim)
        block_log = sums_log[:, index * span : (index + 1) * span]
        block_delta = delta_all[:, index * span : (index + 1) * span]

        def visit(
            position,
            state,
            query_pos=query_pos,
            block_query=block_query,
            block_grad=block_grad,
            block_log=block_log,
            block_delta=block_delta,
        ):
            grad_query, grad_kv = state
            key_first = position * span
            block_kv = lax.dynamic_slice_in_dim(key_values, key_first, span, 0)
            allowed = block_allowed(query_pos, key_first + offsets, ends)[None]
            scores = (
                jnp.einsum(
                    "qhd,kd->hqk",
                    block_query,
                    block_kv[:, :head_dim],
                    preferred_element_type=jnp.float32,
                )
                * scale
            )
            probs = jnp.where(allowed, jnp.exp(scores - block_log[:, :, None]), 0.0)
            grad_probs = jnp.einsum(
                "qhd,kd->hqk",
                block_grad,
                block_kv[:, head_dim:],
                preferred_element_type=jnp.float32,
            )
            grad_scores = (probs * (grad_probs - block_delta[:, :, None])).astype(jnp.bfloat16)
            grad_query = (
                grad_query
                + jnp.einsum(
                    "hqk,kd->qhd",
                    grad_scores,
                    block_kv[:, :head_dim],
                    preferred_element_type=jnp.float32,
                )
                * scale
            )
            key_part = (
                jnp.einsum(
                    "hqk,qhd->kd", grad_scores, block_query, preferred_element_type=jnp.float32
                )
                * scale
            )
            value_part = jnp.einsum(
                "hqk,qhd->kd",
                probs.astype(jnp.bfloat16),
                block_grad,
                preferred_element_type=jnp.float32,
            )
            current = lax.dynamic_slice_in_dim(grad_kv, key_first, span, 0)
            grad_kv = lax.dynamic_update_slice_in_dim(
                grad_kv, current + jnp.concatenate([key_part, value_part], 1), key_first, 0
            )
            return (grad_query, grad_kv)

        key_low, key_high = key_range(query_first, span, starts, ends)
        initial = (jnp.zeros((span, heads_here, head_dim), jnp.float32), grad_keys)
        grad_query, grad_keys = lax.fori_loop(key_low, key_high, visit, initial)
        grad_blocks.append(grad_query.reshape(span, heads_here * head_dim))
    return (jnp.concatenate(grad_blocks, 0), grad_keys)


def body(
    inputs,
    cotangent,
    seq_blocks,
    first_gain,
    first_shift,
    w_query,
    b_query,
    w_keyval,
    b_value,
    w_out,
    b_out,
    second_gain,
    second_shift,
    w_up,
    b_up,
    w_down,
    b_down,
):
    row_index = lax.axis_index("row")
    col_index = lax.axis_index("col")
    tokens_col = inputs.shape[0]
    feature_rows = inputs.shape[1]
    width = feature_rows * lax.axis_size("row")
    total_tokens = tokens_col * lax.axis_size("col")
    rows_here = total_tokens // lax.axis_size("row")
    head_dim = b_value.shape[0]
    query_cols = w_query.shape[1]
    heads_here = query_cols // head_dim
    up_cols = w_up.shape[1]
    residual = inputs.astype(jnp.float32)
    normed_first, scale_first = norm_forward(residual, width)
    first_in = (normed_first * first_gain + first_shift).astype(jnp.bfloat16)
    first_all = spread_cols(first_in)
    joint_weight = jnp.concatenate([w_query, w_keyval], 1)

    def project_joint(begin, count):
        return jnp.dot(first_all, joint_weight, preferred_element_type=jnp.float32)

    joint = fold_rows(project_joint, rows_here)
    queries = (joint[:, :query_cols] + b_query).astype(jnp.bfloat16)
    keyval_part = joint[:, query_cols:].astype(jnp.bfloat16)
    keyval_rows = lax.all_gather(keyval_part, "col", axis=1, tiled=True)
    keyval_all = lax.all_gather(keyval_rows, "row", axis=0, tiled=True)
    row_first = row_index * rows_here
    core, sums_log = attend_forward(queries, keyval_all, row_first, seq_blocks, head_dim)
    attn_in = (core + jnp.tile(b_value, heads_here)).astype(jnp.bfloat16)
    attn_all = spread_rows(attn_in)

    def project_out(begin, count):
        return jnp.dot(attn_all, w_out, preferred_element_type=jnp.float32)

    middle = residual + fold_cols(project_out, tokens_col) + b_out
    normed_second, scale_second = norm_forward(middle, width)
    second_in = (normed_second * second_gain + second_shift).astype(jnp.bfloat16)
    second_all = spread_cols(second_in)

    def project_up(begin, count):
        return jnp.dot(second_all, w_up, preferred_element_type=jnp.float32)

    pre = fold_rows(project_up, rows_here) + b_up
    gelu_value, gelu_back = jax.vjp(partial(jax.nn.gelu, approximate=True), pre)
    hidden = gelu_value.astype(jnp.bfloat16)
    hidden_all = spread_rows(hidden)

    def project_down(begin, count):
        return jnp.dot(
            lax.dynamic_slice_in_dim(hidden_all, begin, count, 0),
            w_down,
            preferred_element_type=jnp.float32,
        )

    block_output = (middle + fold_cols(project_down, tokens_col) + b_down).astype(jnp.bfloat16)
    grad_all = spread_cols(cotangent)
    grad_w_down = contract_first(hidden_all, grad_all)
    grad_b_down = column_sums(grad_all)

    def back_down(begin, count):
        return contract_last(grad_all, w_down)

    grad_hidden = fold_rows(back_down, rows_here)
    grad_pre_low = gelu_back(grad_hidden)[0].astype(jnp.bfloat16)
    grad_pre_all = spread_rows(grad_pre_low)
    grad_w_up = contract_first(second_all, grad_pre_all)

    def back_up(begin, count):
        return contract_last(grad_pre_all, w_up)

    grad_second = fold_cols(back_up, tokens_col)
    up_partial = column_sums(grad_pre_low)
    grad_mid_norm, second_gain_part, second_shift_part = norm_backward(
        grad_second, normed_second, scale_second, second_gain, width
    )
    grad_middle = cotangent.astype(jnp.float32) + grad_mid_norm
    mid_all = spread_cols(grad_middle.astype(jnp.bfloat16))
    grad_w_out = contract_first(attn_all, mid_all)
    grad_b_out = column_sums(mid_all)

    def back_out(begin, count):
        return contract_last(mid_all, w_out)

    grad_attn_low = fold_rows(back_out, rows_here).astype(jnp.bfloat16)
    value_partial = jnp.sum(
        grad_attn_low.astype(jnp.float32).reshape(rows_here, heads_here, head_dim), (0, 1)
    )
    grad_queries, grad_keyval_all = attend_backward(
        queries, keyval_all, core, grad_attn_low, sums_log, row_first, seq_blocks, head_dim
    )
    grad_keyval_rows = lax.psum_scatter(
        grad_keyval_all.astype(jnp.bfloat16), "row", scatter_dimension=0, tiled=True
    )
    grad_keyval = lax.psum_scatter(grad_keyval_rows, "col", scatter_dimension=1, tiled=True).astype(
        jnp.float32
    )
    joint_grad = jnp.concatenate(
        [grad_queries.astype(jnp.bfloat16), grad_keyval.astype(jnp.bfloat16)], 1
    )
    joint_all = spread_rows(joint_grad)
    grad_joint_weight = contract_first(first_all, joint_all)
    grad_b_query = column_sums(joint_all[:, :query_cols])

    def back_joint(begin, count):
        return contract_last(joint_all, joint_weight)

    grad_first = fold_cols(back_joint, tokens_col)
    grad_in_norm, first_gain_part, first_shift_part = norm_backward(
        grad_first, normed_first, scale_first, first_gain, width
    )
    grad_inputs = grad_middle + grad_in_norm
    totals = lax.psum(
        (
            place_slice(first_gain_part, width, row_index),
            place_slice(first_shift_part, width, row_index),
            place_slice(second_gain_part, width, row_index),
            place_slice(second_shift_part, width, row_index),
            value_partial,
            place_slice(up_partial, up_cols * lax.axis_size("col"), col_index),
        ),
        ("row", "col"),
    )
    return (
        block_output,
        grad_inputs,
        take_slice(totals[0], row_index, feature_rows),
        take_slice(totals[1], row_index, feature_rows),
        grad_joint_weight[:, :query_cols],
        grad_b_query,
        grad_joint_weight[:, query_cols:],
        totals[4],
        grad_w_out,
        grad_b_out,
        take_slice(totals[2], row_index, feature_rows),
        take_slice(totals[3], row_index, feature_rows),
        grad_w_up,
        take_slice(totals[5], col_index, up_cols),
        grad_w_down,
        grad_b_down,
    )


def solution(mesh):
    placed = (
        P("col", "row"),
        P("col", "row"),
        P(),
        P("row"),
        P("row"),
        P("row", "col"),
        P("col"),
        P("row", "col"),
        P(),
        P("col", "row"),
        P("row"),
        P("row"),
        P("row"),
        P("row", "col"),
        P("col"),
        P("col", "row"),
        P("row"),
    )
    return jax.shard_map(
        body,
        mesh=mesh,
        in_specs=placed,
        out_specs=(
            P("col", "row"),
            P("col", "row"),
            P("row"),
            P("row"),
            P("row", "col"),
            P("col"),
            P("row", "col"),
            P(),
            P("col", "row"),
            P("row"),
            P("row"),
            P("row"),
            P("row", "col"),
            P("col"),
            P("col", "row"),
            P("row"),
        ),
        check_vma=False,
    )
```

profile of v0, /device:TPU:0, one launch (start us, length us, event | category | flops | bytes accessed | tf_op | source)
XLA Modules:
  0.0 1399.9 jit_solution(16788110946598439833)
XLA Ops:
  8.6 15.2 %psum.98 = f32[1024]{0:T(1024)S(1)} all-reduce(f32[1024]{0:T(1024)S(1)} %convert_reduce_fusion.6), channel_id=1, replica_groups=mesh['row'=8,'col'=4] {'row'}, use_global_device_ids=true, to_apply=%region_4.0 | all-reduce | flops 1024 | bytes 8192 | tf_op jit(solution)/shard_map/psum | solution.py:43
  40.1 44.3 %all-gather.10.cloned.1.call-done = bf16[4096,256]{1,0:T(8,128)(2,1)} async-done(((bf16[1024,256]{1,0:T(8,128)(2,1)}), bf16[4096,256]{1,0:T(8,128)(2,1)}) %all-gather.10.cloned.1.call-update) | async-done | bytes 2097168 | tf_op jit(solution)/shard_map/all_gather | solution.py:17
  89.6 52.6 %reduce-scatter.11.cloned.1.call-done = bf16[512,576]{0,1:T(8,128)(2,1)} async-done(((bf16[4096,576]{0,1:T(8,128)(2,1)}), bf16[512,576]{0,1:T(8,128)(2,1)}) %reduce-scatter.11.cloned.1.call-update) | async-done | bytes 589840 | tf_op jit(solution)/shard_map/reduce_scatter | solution.py:25
  143.0 14.6 %all_gather.31 = bf16[512,256]{0,1:T(8,128)(2,1)} all-gather(bf16[512,64]{0,1:T(8,128)(2,1)S(1)} %slice.62), channel_id=1, replica_groups=mesh['row'=8,'col'=4] {'col'}, dimensions={1}, use_global_device_ids=true | all-gather | bytes 327680 | tf_op jit(solution)/shard_map/all_gather | solution.py:294
  164.0 22.5 %all-gather.12.cloned.1.call-done = bf16[4096,256]{0,1:T(8,128)(2,1)} async-done(((bf16[512,256]{0,1:T(8,128)(2,1)}), bf16[4096,256]{0,1:T(8,128)(2,1)}) %all-gather.12.cloned.1.call-update) | async-done | bytes 2097168 | tf_op jit(solution)/shard_map/all_gather | solution.py:295
  198.1 67.4 %all-gather.14.cloned.1.call-done = bf16[4096,512]{1,0:T(8,128)(2,1)} async-done(((bf16[512,512]{1,0:T(8,128)(2,1)}), bf16[4096,512]{1,0:T(8,128)(2,1)}) %all-gather.14.cloned.1.call-update) | async-done | bytes 4194320 | tf_op jit(solution)/shard_map/all_gather | solution.py:21
  270.9 43.2 %reduce-scatter.13.cloned.1.call-done = bf16[1024,256]{1,0:T(8,128)(2,1)} async-done(((bf16[4096,256]{1,0:T(8,128)(2,1)}), bf16[1024,256]{1,0:T(8,128)(2,1)}) %reduce-scatter.13.cloned.1.call-update) | async-done | bytes 524304 | tf_op jit(solution)/shard_map/reduce_scatter | solution.py:34
  315.3 13.2 psum.100
  345.1 15.2 %all-gather.20.cloned.1.call-done = bf16[4096,256]{1,0:T(8,128)(2,1)} async-done(((bf16[1024,256]{1,0:T(8,128)(2,1)}), bf16[4096,256]{1,0:T(8,128)(2,1)}) %all-gather.20.cloned.1.call-update) | async-done | bytes 2097168 | tf_op jit(solution)/shard_map/all_gather | solution.py:17
  372.9 34.1 %all-gather.16.cloned.1.call-done = bf16[4096,256]{1,0:T(8,128)(2,1)} async-done(((bf16[1024,256]{1,0:T(8,128)(2,1)}), bf16[4096,256]{1,0:T(8,128)(2,1)}) %all-gather.16.cloned.1.call-update) | async-done | bytes 2097168 | tf_op jit(solution)/shard_map/all_gather | solution.py:17
  417.5 108.1 %reduce-scatter.19.cloned.1.call-done = bf16[512,2048]{1,0:T(8,128)(2,1)} async-done(((bf16[4096,2048]{1,0:T(8,128)(2,1)}), bf16[512,2048]{1,0:T(8,128)(2,1)}) %reduce-scatter.19.cloned.1.call-update) | async-done | bytes 2097168 | tf_op jit(solution)/shard_map/reduce_scatter | solution.py:25
  525.6 119.8 %reduce-scatter.15.cloned.1.call-done = bf16[512,2048]{1,0:T(8,128)(2,1)} async-done(((bf16[4096,2048]{1,0:T(8,128)(2,1)}), bf16[512,2048]{1,0:T(8,128)(2,1)}) %reduce-scatter.15.cloned.1.call-update) | async-done | bytes 2097168 | tf_op jit(solution)/shard_map/reduce_scatter | solution.py:25
  652.5 89.1 %all-gather.22.cloned.1.call-done = bf16[4096,2048]{1,0:T(8,128)(2,1)} async-done(((bf16[512,2048]{1,0:T(8,128)(2,1)}), bf16[4096,2048]{1,0:T(8,128)(2,1)}) %all-gather.22.cloned.1.call-update) | async-done | bytes 16777232 | tf_op jit(solution)/shard_map/all_gather | solution.py:21
  763.0 70.3 %all-gather.18.cloned.1.call-done = bf16[4096,2048]{1,0:T(8,128)(2,1)} async-done(((bf16[512,2048]{1,0:T(8,128)(2,1)}), bf16[4096,2048]{1,0:T(8,128)(2,1)}) %all-gather.18.cloned.1.call-update) | async-done | bytes 16777232 | tf_op jit(solution)/shard_map/all_gather | solution.py:21
  845.2 33.9 %reduce-scatter.21.cloned.1.call-done = bf16[1024,256]{1,0:T(8,128)(2,1)} async-done(((bf16[4096,256]{1,0:T(8,128)(2,1)}), bf16[1024,256]{1,0:T(8,128)(2,1)}) %reduce-scatter.21.cloned.1.call-update) | async-done | bytes 524304 | tf_op jit(solution)/shard_map/reduce_scatter | solution.py:34
  880.9 13.9 all-reduce.2
  894.8 29.5 %reduce-scatter.17.cloned.1.call-done = bf16[1024,256]{1,0:T(8,128)(2,1)} async-done(((bf16[4096,256]{1,0:T(8,128)(2,1)}), bf16[1024,256]{1,0:T(8,128)(2,1)}) %reduce-scatter.17.cloned.1.call-update) | async-done | bytes 524304 | tf_op jit(solution)/shard_map/reduce_scatter | solution.py:34
  927.2 45.0 %all-gather.24.cloned.1.call-done = bf16[4096,256]{1,0:T(8,128)(2,1)} async-done(((bf16[1024,256]{1,0:T(8,128)(2,1)}), bf16[4096,256]{1,0:T(8,128)(2,1)}) %all-gather.24.cloned.1.call-update) | async-done | bytes 2097168 | tf_op jit(solution)/shard_map/all_gather | solution.py:17
  977.2 50.0 %reduce-scatter.23.cloned.1.call-done = bf16[512,512]{1,0:T(8,128)(2,1)} async-done(((bf16[4096,512]{1,0:T(8,128)(2,1)}), bf16[512,512]{1,0:T(8,128)(2,1)}) %reduce-scatter.23.cloned.1.call-update) | async-done | bytes 524304 | tf_op jit(solution)/shard_map/reduce_scatter | solution.py:25
  1047.4 89.3 %reduce-scatter.25.cloned.1.call-done = bf16[512,256]{0,1:T(8,128)(2,1)} async-done(((bf16[4096,256]{0,1:T(8,128)(2,1)}), bf16[512,256]{0,1:T(8,128)(2,1)}) %reduce-scatter.25.cloned.1.call-update) | async-done | bytes 262160 | tf_op jit(solution)/shard_map/reduce_scatter | solution.py:360
  1136.8 22.0 %reduce-scatter.27.cloned.1.call-done = bf16[512,64]{0,1:T(8,128)(2,1)} async-done(((bf16[512,256]{0,1:T(8,128)(2,1)}), bf16[512,64]{0,1:T(8,128)(2,1)}) %reduce-scatter.27.cloned.1.call-update) | async-done | bytes 65552 | tf_op jit(solution)/shard_map/reduce_scatter | solution.py:363
  1165.4 33.7 %all-gather.26.cloned.1.call-done = bf16[4096,576]{0,1:T(8,128)(2,1)} async-done(((bf16[512,576]{0,1:T(8,128)(2,1)}), bf16[4096,576]{0,1:T(8,128)(2,1)}) %all-gather.26.cloned.1.call-update) | async-done | bytes 4718608 | tf_op jit(solution)/shard_map/all_gather | solution.py:21
  1250.1 13.5 all-reduce.1
  1267.4 117.6 %all-reduce.5.cloned.1.call-done = (f32[2048]{0:T(1024)}, f32[2048]{0:T(1024)}, f32[128]{0:T(128)}, f32[2048]{0:T(1024)}, f32[2048]{0:T(1024)}, /*index=5*/f32[8192]{0:T(1024)}) async-done(((f32[2048]{0:T(1024)}, f32[2048]{0:T(1024)}, f32[128]{0:T(128)}, f32[2048]{0:T(1024)}, f32[2048]{0:T(1024)}, /*index=5*/f32[8192]{0:T(1024)}), (f32[2048]{0:T(1024)}, f32[2048]{0:T(1024)}, f32[128]{0:T(128)}, ...) | async-done | bytes 66064 | tf_op jit(solution)/shard_map/psum | solution.py:381
  (209 shorter events, 240.2 us)
Async XLA Ops:
  7.2 399.8 %copy-start = (bf16[256,2048]{1,0:T(8,128)(2,1)S(1)}, bf16[256,2048]{1,0:T(8,128)(2,1)}, u32[]{:S(2)}) copy-start(bf16[256,2048]{1,0:T(8,128)(2,1)} %param.34) | copy-start | bytes 3145732
  7.2 77.2 %all-gather.10.cloned.1.call-start = ((), (), s32[]{:S(2)}) async-start(), calls=%async_computation.10 | async-start | bytes 2621440 | tf_op jit(solution)/shard_map/all_gather | solution.py:17
  39.2 103.0 %reduce-scatter.11.cloned.1.call-start = ((), (), s32[]{:S(2)}) async-start(), calls=%async_computation.11 | async-start | bytes 5308416 | tf_op jit(solution)/shard_map/reduce_scatter | solution.py:25
  89.6 96.9 %all-gather.12.cloned.1.call-start = ((), (), s32[]{:S(2)}) async-start(), calls=%async_computation.12 | async-start | bytes 2359296 | tf_op jit(solution)/shard_map/all_gather | solution.py:295
  157.7 107.8 %all-gather.14.cloned.1.call-start = ((), (), s32[]{:S(2)}) async-start(), calls=%async_computation.13 | async-start | bytes 4718592 | tf_op jit(solution)/shard_map/all_gather | solution.py:21
  198.0 116.0 %reduce-scatter.13.cloned.1.call-start = ((), (), s32[]{:S(2)}) async-start(), calls=%async_computation.14 | async-start | bytes 2621440 | tf_op jit(solution)/shard_map/reduce_scatter | solution.py:34
  270.3 90.1 %all-gather.20.cloned.1.call-start = ((), (), s32[]{:S(2)}) async-start(), calls=%async_computation.19 | async-start | bytes 2621440 | tf_op jit(solution)/shard_map/all_gather | solution.py:17
  270.8 136.2 %all-gather.16.cloned.1.call-start = ((), (), s32[]{:S(2)}) async-start(), calls=%async_computation.15 | async-start | bytes 2621440 | tf_op jit(solution)/shard_map/all_gather | solution.py:17
  344.8 180.8 %reduce-scatter.19.cloned.1.call-start = ((), (), s32[]{:S(2)}) async-start(), calls=%async_computation.20 | async-start | bytes 18874368 | tf_op jit(solution)/shard_map/reduce_scatter | solution.py:25
  372.9 272.5 %reduce-scatter.15.cloned.1.call-start = ((), (), s32[]{:S(2)}) async-start(), calls=%async_computation.16 | async-start | bytes 18874368 | tf_op jit(solution)/shard_map/reduce_scatter | solution.py:25
  417.4 228.0 %copy-start.22 = (f32[2048]{0:T(1024)S(1)}, f32[2048]{0:T(1024)}, u32[]{:S(2)}) copy-start(f32[2048]{0:T(1024)} %param.35) | copy-start | bytes 24580
  417.4 324.2 %all-gather.22.cloned.1.call-start = ((), (), s32[]{:S(2)}) async-start(), calls=%async_computation.21 | async-start | bytes 18874368 | tf_op jit(solution)/shard_map/all_gather | solution.py:21
  651.7 181.5 %all-gather.18.cloned.1.call-start = ((), (), s32[]{:S(2)}) async-start(), calls=%async_computation.17 | async-start | bytes 18874368 | tf_op jit(solution)/shard_map/all_gather | solution.py:21
  652.5 226.6 %reduce-scatter.21.cloned.1.call-start = ((), (), s32[]{:S(2)}) async-start(), calls=%async_computation.22 | async-start | bytes 2621440 | tf_op jit(solution)/shard_map/reduce_scatter | solution.py:34
  751.4 172.9 %copy-start.7 = (bf16[1024,256]{1,0:T(8,128)(2,1)S(1)}, bf16[1024,256]{1,0:T(8,128)(2,1)}, u32[]{:S(2)}) copy-start(bf16[1024,256]{1,0:T(8,128)(2,1)} %param.22) | copy-start | bytes 1572868
  751.4 172.8 %copy-start.24 = (f32[256]{0:T(256)S(1)}, f32[256]{0:T(256)}, u32[]{:S(2)}) copy-start(f32[256]{0:T(256)} %param.37) | copy-start | bytes 3076
  751.4 172.8 %reduce-scatter.17.cloned.1.call-start = ((), (), s32[]{:S(2)}) async-start(), calls=%async_computation.18 | async-start | bytes 2621440 | tf_op jit(solution)/shard_map/reduce_scatter | solution.py:34
  845.1 127.0 %all-gather.24.cloned.1.call-start = ((), (), s32[]{:S(2)}) async-start(), calls=%async_computation.23 | async-start | bytes 2621440 | tf_op jit(solution)/shard_map/all_gather | solution.py:17
  927.1 100.1 %reduce-scatter.23.cloned.1.call-start = ((), (), s32[]{:S(2)}) async-start(), calls=%async_computation.24 | async-start | bytes 4718592 | tf_op jit(solution)/shard_map/reduce_scatter | solution.py:25
  977.1 159.6 %reduce-scatter.25.cloned.1.call-start = ((), (), s32[]{:S(2)}) async-start(), calls=%async_computation.25 | async-start | bytes 2359296 | tf_op jit(solution)/shard_map/reduce_scatter | solution.py:360
  1047.3 111.5 %reduce-scatter.27.cloned.1.call-start = ((), (), s32[]{:S(2)}) async-start(), calls=%async_computation.26 | async-start | bytes 327680 | tf_op jit(solution)/shard_map/reduce_scatter | solution.py:363
  1136.7 62.3 %all-gather.26.cloned.1.call-start = ((), (), s32[]{:S(2)}) async-start(), calls=%async_computation.27 | async-start | bytes 5308416 | tf_op jit(solution)/shard_map/all_gather | solution.py:21
  1160.5 87.8 %reduce-scatter.29.cloned.1.call-start = ((), (), s32[]{:S(2)}) async-start(), calls=%async_computation.28 | async-start | bytes 2621440 | tf_op jit(solution)/shard_map/reduce_scatter | solution.py:34
  1204.6 180.4 %all-reduce.5.cloned.1.call-start = ((), (), s32[]{:S(2)}) async-start(), calls=%async_computation.29 | async-start | bytes 132096 | tf_op jit(solution)/shard_map/psum | solution.py:381
  (26 other events, 1365.5 us)
Sparse Core Ops, SparseCore 0:
  39.3 45.0 all-gather.9
  89.7 52.4 reduce-scatter.10
  157.8 28.6 all-gather.11
  198.1 67.3 all-gather.13
  270.4 43.6 reduce-scatter.12
  315.5 44.8 all-gather.19
  362.5 44.4 all-gather.15
  410.6 114.9 reduce-scatter.18
  529.2 116.1 reduce-scatter.14
  651.9 89.7 all-gather.21
  743.5 89.7 all-gather.17
  835.4 43.6 reduce-scatter.20
  881.4 42.8 reduce-scatter.16
  927.3 44.8 all-gather.23
  977.2 49.9 reduce-scatter.22
  1047.4 89.2 reduce-scatter.24
  1138.8 19.9 reduce-scatter.26
  1161.1 37.8 all-gather.25
  1204.7 43.6 reduce-scatter.28
  1264.9 120.0 all-reduce.4
where the time goes:
time: 1410 us; the launch traced here: 1400 us
  waiting for transfers between devices  1090 us (77%)
  matrix products  117 us (8%)
  blocking collectives  94.7 us (7%)
  other arithmetic  41.7 us (3%)
  local copies, waits for them, and re-layouts  21.8 us (2%)
  between operations  17.8 us (1%)
    reduce_scatter x4, waiting for transfers between devices, fold_rows(): lax.psum_scatter(maker(jnp.int32(0), count * lax.axis_size('row')).astype...  331 us
    all_gather x4, waiting for transfers between devices, spread_rows(): return lax.all_gather(value, 'row', axis=0, tiled=True)  260 us
    all_gather x4, waiting for transfers between devices, spread_cols(): return lax.all_gather(value, 'col', axis=0, tiled=True)  139 us
    psum x1, waiting for transfers between devices, body(): lax.psum((place_slice(first_gain_part, width, row_index), place_slice(fir...  118 us
    reduce_scatter x4, waiting for transfers between devices, fold_cols(): lax.psum_scatter(maker(jnp.int32(0), count * lax.axis_size('col')).astype...  111 us
    reduce_scatter x1, waiting for transfers between devices, body(): lax.psum_scatter(grad_keyval_all.astype(jnp.bfloat16), 'row', scatter_dim...  89.3 us
    psum x6, blocking collectives, feature_total(): return lax.psum(values, 'row')  80.1 us
    dot_general x4, matrix products, contract_last(): lax.dot_general(left, right, (((1,), (1,)), ((), ())), preferred_element_...  32.7 us
  transfers between devices with their start and end apart: 20, of which 20 were waited for; matrix products, arithmetic and copies ran while one was open for 7% of the time, Pallas kernels for 0%

commit v1 on v0

v1 whole, which is shorter than its diff:
```python
from functools import partial

import jax
import jax.numpy as jnp
from jax import lax
from jax.experimental import pallas as pl
from jax.experimental.pallas import tpu as pltpu
from jax.sharding import PartitionSpec as P

BLK = 256
EPSILON = 1e-05
NEGATIVE = -1e30
LOG2E = 1.4426950408889634
F32 = jnp.float32
BF16 = jnp.bfloat16


def barrier(*values):
    return lax.optimization_barrier(values)


def col_parts(value):
    count = lax.axis_size("col")
    return [
        lax.ppermute(value, "col", [(i, (i + step) % count) for i in range(count)])
        for step in range(1, count)
    ]


def col_join(value, parts):
    count = lax.axis_size("col")
    me = lax.axis_index("col")
    out = jnp.zeros((count,) + value.shape, value.dtype)
    out = lax.dynamic_update_index_in_dim(out, value, me, 0)
    for step, part in enumerate(parts, 1):
        out = lax.dynamic_update_index_in_dim(out, part, lax.rem(me - step + count, count), 0)
    return out


def col_send(pieces):
    count = lax.axis_size("col")
    me = lax.axis_index("col")
    low = pieces.astype(BF16)
    out = [lax.dynamic_index_in_dim(low, me, 0, keepdims=False)]
    for step in range(1, count):
        part = lax.dynamic_index_in_dim(low, lax.rem(me + step, count), 0, keepdims=False)
        out.append(
            lax.ppermute(part, "col", [(i, (i + step) % count) for i in range(count)])
        )
    return out


def add_up(parts):
    return sum(part.astype(F32) for part in parts)


def exchange_rows(pieces):
    return lax.all_to_all(pieces.astype(BF16), "row", 0, 0)


def total(pieces):
    return jnp.sum(pieces.astype(F32), 0)


def swap(value, bit):
    count = lax.axis_size("row")
    return lax.ppermute(value, "row", [(i, i ^ bit) for i in range(count)])


def chip_bits():
    bits = []
    bit = 2
    while bit < lax.axis_size("row"):
        bits.append(bit)
        bit *= 2
    return bits


def row_place(other):
    apart = jnp.bitwise_xor(lax.axis_index("row"), other)
    return (apart & 1) * (lax.axis_size("row") // 2) + (apart >> 1)


def in_row_order(pieces, axis):
    count = pieces.shape[0]
    return jnp.concatenate(
        [
            lax.dynamic_index_in_dim(pieces, row_place(a), 0, keepdims=False)
            for a in range(count)
        ],
        axis,
    )


def row_gather(value):
    half = value.shape[-1] // 2
    bits = chip_bits()
    orders = (bits, bits[::-1])
    held = [{0: value[..., :half]}, {0: value[..., half:]}]
    for step in range(len(bits)):
        keys = [sorted(h) for h in held]
        got = yield [
            swap(jnp.stack([h[k] for k in ks]), order[step])
            for h, ks, order in zip(held, keys, orders)
        ]
        for h, ks, order, new in zip(held, keys, orders, got):
            h.update({k ^ order[step]: new[n] for n, k in enumerate(ks)})
    own = jnp.stack([jnp.concatenate([held[0][k], held[1][k]], -1) for k in sorted(held[0])])
    (other,) = yield [swap(own, 1)]
    return own, other


def row_scatter(mine, theirs):
    got = yield [swap(part, 1) for part in theirs]
    bits = chip_bits()
    orders = (bits[::-1], bits)
    held = []
    for part, new in zip(mine, got):
        both = part + new.astype(F32)
        held.append({2 * k: both[k] for k in range(both.shape[0])})
    for step in range(len(bits)):
        keeps = [sorted(k for k in h if not k & order[step]) for h, order in zip(held, orders)]
        got = yield [
            swap(jnp.stack([h[k ^ order[step]] for k in keep]).astype(BF16), order[step])
            for h, keep, order in zip(held, keeps, orders)
        ]
        held = [
            {k: h[k] + new[n].astype(F32) for n, k in enumerate(keep)}
            for h, keep, new in zip(held, keeps, got)
        ]
    return [h[0] for h in held]


def advance(steps, arrived):
    try:
        return steps.send(list(arrived))
    except StopIteration as stop:
        return {"done": stop.value}


def finish(steps, arrived):
    while True:
        arrived = advance(steps, list(barrier(*arrived)))
        if isinstance(arrived, dict):
            return arrived["done"]


def in_parts(vector, count):
    parts = []
    for _ in range(count):
        low = lax.reduce_precision(vector, 8, 7)
        parts.append(low.astype(BF16))
        vector = vector - low
    return jnp.stack(parts)


def padded(rows_array, multiple):
    short = -rows_array.shape[0] % multiple
    return jnp.pad(rows_array, ((0, short), (0, 0)))


def norm_kernel(
    me_ref, mine_ref, theirs_ref, mine_vec, theirs_vec, mine_own, theirs_own,
    first_ref, own_ref, vector_ref,
    *, width
):
    half = mine_ref.shape[0]
    features = mine_ref.shape[2]
    places = [(mine_ref, mine_vec, mine_own, 2 * k, k) for k in range(half)]
    places += [(theirs_ref, theirs_vec, theirs_own, 2 * k + 1, k) for k in range(half)]
    me = me_ref[0]

    def columns(apart):
        return pl.ds(pl.multiple_of(jnp.bitwise_xor(me, apart) * features, features), features)

    @pl.when(pl.program_id(0) == 0)
    def _():
        for _, vec, own, apart, k in places:
            stack = vec[k].astype(F32)
            vector_ref[:, columns(apart)] = stack[0:8] + stack[8:16] + stack[16:24]
            own_ref[:, columns(apart)] = own[k]

    sums = sum(jnp.sum(ref[k].astype(F32), 1, keepdims=True) for ref, _, _, _, k in places)
    mean = sums / width
    squares = jnp.zeros_like(mean)
    for ref, _, _, _, k in places:
        centred = ref[k].astype(F32) - mean
        squares = squares + jnp.sum(centred * centred, 1, keepdims=True)
    scale = lax.rsqrt(squares / width + EPSILON)
    for ref, vec, _, apart, k in places:
        stack = vec[k].astype(F32)
        both = stack[0:8] + stack[8:16] + stack[16:24]
        normed = (ref[k].astype(F32) - mean) * scale
        first_ref[:, columns(apart)] = (normed * both[0:1] + both[1:2]).astype(BF16)


def norm_gathered(mine, theirs, tokens, span):
    rows = lax.axis_size("row")
    half, _, features = mine.shape
    width = features * rows
    me = jnp.full((1,), lax.axis_index("row"), jnp.int32)
    block = pl.BlockSpec((half, BLK, features), lambda i, _: (0, i, 0))
    vec = pl.BlockSpec((half, 32, features), lambda i, _: (0, tokens // 32, 0))
    own = pl.BlockSpec((half, span, features), lambda i, m: (0, m[0], 0))
    return pl.pallas_call(
        partial(norm_kernel, width=width),
        out_shape=(
            jax.ShapeDtypeStruct((tokens, width), BF16),
            jax.ShapeDtypeStruct((span, width), BF16),
            jax.ShapeDtypeStruct((8, width), F32),
        ),
        grid_spec=pltpu.PrefetchScalarGridSpec(
            num_scalar_prefetch=1,
            grid=(tokens // BLK,),
            in_specs=[block, block, vec, vec, own, own],
            out_specs=(
                pl.BlockSpec((BLK, width), lambda i, _: (i, 0)),
                pl.BlockSpec((span, width), lambda i, _: (0, 0)),
                pl.BlockSpec((8, width), lambda i, _: (0, 0)),
            ),
        ),
        name="norm_gathered",
    )(me, mine, theirs, mine, theirs, mine, theirs)


def stacked_heads(block, head_dim):
    count = block.shape[1] // head_dim
    return jnp.concatenate([block[:, h * head_dim : (h + 1) * head_dim] for h in range(count)], 0)


def dot_last(left, right):
    return lax.dot_general(left, right, (((1,), (1,)), ((), ())), preferred_element_type=F32)


def dot_first(left, right):
    return lax.dot_general(left, right, (((0,), (0,)), ((), ())), preferred_element_type=F32)


def dot_plain(left, right):
    return lax.dot_general(left, right, (((1,), (0,)), ((), ())), preferred_element_type=F32)


def key_pieces(kb, me, per_col, per_block, half):
    col = lax.div(kb, per_col)
    first = lax.rem(kb, per_col) * per_block
    places = []
    for t in range(per_block):
        apart = jnp.bitwise_xor(first + t, me)
        places.append((apart & 1) * half + lax.shift_right_logical(apart, 1))
    return col, places


def forward_kernel(
    low_ref, high_ref, me_ref, q_ref, kv_ref, bias_ref, out_ref, log_ref, low_out_ref, acc_ref, top_ref, sum_ref,
    *, head_dim, per_col, per_block, span
):
    chunk = pl.program_id(0)
    q = stacked_heads(q_ref[...], head_dim)
    rows = q.shape[0]
    acc_ref[...] = jnp.zeros_like(acc_ref)
    top_ref[...] = jnp.full_like(top_ref, NEGATIVE)
    sum_ref[...] = jnp.zeros_like(sum_ref)
    factor = head_dim ** (-0.5) * LOG2E

    def visit(kb, carry):
        col, places = key_pieces(kb, me_ref[0], per_col, per_block, kv_ref.shape[0] // 2)
        at = pl.ds(pl.multiple_of(col * span, span), span)
        kv = jnp.concatenate([kv_ref[place, at, :] for place in places], 0)
        scores = dot_last(kv[:, :head_dim], q) * factor
        old = top_ref[...]
        new = jnp.maximum(old, jnp.max(scores, 0, keepdims=True))
        weights = jnp.exp2(scores - new)
        decay = jnp.exp2(old - new)
        top_ref[...] = new
        sum_ref[...] = sum_ref[...] * decay + jnp.sum(weights, 0, keepdims=True)
        acc_ref[...] = acc_ref[...] * decay + dot_first(kv[:, head_dim:], weights.astype(BF16))
        return carry

    lax.fori_loop(low_ref[chunk], high_ref[chunk], visit, 0)
    out = acc_ref[...] / sum_ref[...]
    out_ref[0] = out
    for h in range(rows // BLK):
        low_out_ref[:, h * head_dim : (h + 1) * head_dim] = (
            jnp.transpose(out[:, h * BLK : (h + 1) * BLK]) + bias_ref[...]
        ).astype(BF16)
    log_ref[0] = top_ref[...] + jnp.log2(sum_ref[...])


def backward_kernel(
    low_ref, high_ref, me_ref, q_ref, grad_ref, out_ref, log_ref, kv_ref, gq_ref, gk_mine, gk_theirs, gv_mine, gv_theirs,
    gk_acc, gv_acc, gq_acc,
    *, head_dim, per_col, per_block, span
):
    chunk = pl.program_id(0)

    @pl.when(chunk == 0)
    def _():
        gk_acc[...] = jnp.zeros_like(gk_acc)
        gv_acc[...] = jnp.zeros_like(gv_acc)

    q = stacked_heads(q_ref[...], head_dim)
    grad = stacked_heads(grad_ref[...], head_dim)
    scale = head_dim ** (-0.5)
    log = log_ref[0]
    delta = jnp.sum(out_ref[0] * jnp.transpose(grad.astype(F32)), 0, keepdims=True)
    gq_acc[...] = jnp.zeros_like(gq_acc)

    def visit(kb, carry):
        col, places = key_pieces(kb, me_ref[0], per_col, per_block, kv_ref.shape[0] // 2)
        at = pl.ds(pl.multiple_of(col * span, span), span)
        kv = jnp.concatenate([kv_ref[place, at, :] for place in places], 0)
        keys, vals = kv[:, :head_dim], kv[:, head_dim:]
        scores = dot_last(keys, q) * (scale * LOG2E)
        probs = jnp.exp2(scores - log)
        grad_probs = dot_last(vals, grad)
        grad_scores = (probs * (grad_probs - delta)).astype(BF16)
        gq_acc[...] += dot_first(keys, grad_scores)
        gk = dot_plain(grad_scores, q)
        gv = dot_plain(probs.astype(BF16), grad)
        for t, place in enumerate(places):
            gk_acc[place, at, :] += gk[t * span : (t + 1) * span]
            gv_acc[place, at, :] += gv[t * span : (t + 1) * span]
        return carry

    lax.fori_loop(low_ref[chunk], high_ref[chunk], visit, 0)
    gq = gq_acc[...] * scale
    for h in range(q.shape[0] // BLK):
        gq_ref[:, h * head_dim : (h + 1) * head_dim] = jnp.transpose(
            gq[:, h * BLK : (h + 1) * BLK]
        ).astype(BF16)

    @pl.when(chunk == pl.num_programs(0) - 1)
    def _():
        half = gk_mine.shape[0]
        gk_mine[...] = gk_acc[:half] * scale
        gk_theirs[...] = (gk_acc[half:] * scale).astype(BF16)
        gv_mine[...] = gv_acc[:half]
        gv_theirs[...] = gv_acc[half:].astype(BF16)


def attention_calls(seq_blocks, tokens_col, span, head_dim, query_cols):
    rows, cols = lax.axis_size("row"), lax.axis_size("col")
    per_col, per_block = tokens_col // BLK, BLK // span
    heads = query_cols // head_dim
    me = lax.axis_index("row")
    ends = jnp.cumsum(seq_blocks)
    blocks = lax.axis_index("col") * per_col + jnp.arange(per_col, dtype=jnp.int32)
    owner = jnp.sum((blocks[:, None] >= ends[None, :]).astype(jnp.int32), 1)
    starts = ends - seq_blocks
    low = jnp.sum(
        jnp.where(owner[:, None] == jnp.arange(ends.shape[0])[None, :], starts[None, :], 0), 1
    ).astype(jnp.int32)
    scalars = (low, (blocks + 1).astype(jnp.int32), jnp.full((1,), me, jnp.int32))
    sizes = dict(head_dim=head_dim, per_col=per_col, per_block=per_block, span=span)
    chunk_rows = pl.BlockSpec((BLK, query_cols), lambda c, *_: (c, 0))
    whole_kv = pl.BlockSpec((rows, cols * span, 2 * head_dim), lambda c, *_: (0, 0, 0))
    half_kv = pl.BlockSpec((rows // 2, cols * span, head_dim), lambda c, *_: (0, 0, 0))
    turned = pl.BlockSpec((1, head_dim, heads * BLK), lambda c, *_: (c, 0, 0))
    logs = pl.BlockSpec((1, 1, heads * BLK), lambda c, *_: (c, 0, 0))
    bias = pl.BlockSpec((1, head_dim), lambda c, *_: (0, 0))
    shape = jax.ShapeDtypeStruct

    def forward(queries, key_values, bias_value):
        return pl.pallas_call(
            partial(forward_kernel, **sizes),
            out_shape=(
                shape((per_col, head_dim, heads * BLK), F32),
                shape((per_col, 1, heads * BLK), F32),
                shape((tokens_col, query_cols), BF16),
            ),
            grid_spec=pltpu.PrefetchScalarGridSpec(
                num_scalar_prefetch=3,
                grid=(per_col,),
                in_specs=[chunk_rows, whole_kv, bias],
                out_specs=(turned, logs, chunk_rows),
                scratch_shapes=[
                    pltpu.VMEM((head_dim, heads * BLK), F32),
                    pltpu.VMEM((1, heads * BLK), F32),
                    pltpu.VMEM((1, heads * BLK), F32),
                ],
            ),
            name="attend_forward",
        )(*scalars, queries, key_values, bias_value)

    def backward(queries, grad_low, out, log, key_values):
        return pl.pallas_call(
            partial(backward_kernel, **sizes),
            out_shape=(
                shape((tokens_col, query_cols), BF16),
                shape((rows // 2, cols * span, head_dim), F32),
                shape((rows // 2, cols * span, head_dim), BF16),
                shape((rows // 2, cols * span, head_dim), F32),
                shape((rows // 2, cols * span, head_dim), BF16),
            ),
            grid_spec=pltpu.PrefetchScalarGridSpec(
                num_scalar_prefetch=3,
                grid=(per_col,),
                in_specs=[chunk_rows, chunk_rows, turned, logs, whole_kv],
                out_specs=(chunk_rows, half_kv, half_kv, half_kv, half_kv),
                scratch_shapes=[
                    pltpu.VMEM((rows, cols * span, head_dim), F32),
                    pltpu.VMEM((rows, cols * span, head_dim), F32),
                    pltpu.VMEM((head_dim, heads * BLK), F32),
                ],
            ),
            name="attend_backward",
        )(*scalars, queries, grad_low, out, log, key_values)

    return forward, backward


def norm_forward(values):
    mean = jnp.mean(values, 1, keepdims=True)
    centred = values - mean
    scale = lax.rsqrt(jnp.mean(centred * centred, 1, keepdims=True) + EPSILON)
    return centred * scale, scale


def norm_backward(grad_out, normed, scale, gain):
    grad_normed = grad_out * gain
    plain = jnp.mean(grad_normed, 1, keepdims=True)
    cross = jnp.mean(grad_normed * normed, 1, keepdims=True)
    grad_in = scale * (grad_normed - plain - normed * cross)
    return grad_in, jnp.sum(grad_out * normed, 0), jnp.sum(grad_out, 0)


def body(
    inputs,
    cotangent,
    seq_blocks,
    first_gain,
    first_shift,
    w_query,
    b_query,
    w_keyval,
    b_value,
    w_out,
    b_out,
    second_gain,
    second_shift,
    w_up,
    b_up,
    w_down,
    b_down,
):
    rows, cols = lax.axis_size("row"), lax.axis_size("col")
    row, col = lax.axis_index("row"), lax.axis_index("col")
    tokens_col, features = inputs.shape
    width = features * rows
    span = tokens_col // rows
    head_dim = b_value.shape[0]
    kv_cols = w_keyval.shape[1]
    head_cols = w_query.shape[1]
    query_cols = head_cols * cols // rows
    heads_each = head_cols // query_cols

    up_cols = w_up.shape[1]

    vectors = jnp.stack([first_gain, first_shift, b_out, second_gain, second_shift, b_down])
    vectors = in_parts(padded(vectors, 8), 3).reshape(24, features)
    steps_x = row_gather(jnp.concatenate([inputs, padded(vectors, 32)], 0))
    fly_x = next(steps_x)
    kv_local = w_keyval.reshape(-1, query_cols)
    fly_kv = col_parts(kv_local)
    fly_x, fly_kv = barrier(fly_x, fly_kv)

    fly_x = advance(steps_x, fly_x)
    kv_strip = jnp.transpose(
        col_join(kv_local, fly_kv).reshape(cols, features, kv_cols), (1, 0, 2)
    ).reshape(features, cols * kv_cols)
    steps_kv = row_gather(kv_strip)
    fly_kv = next(steps_kv)
    query_local = jnp.transpose(w_query.reshape(features, heads_each, query_cols), (1, 0, 2))
    fly_q = col_parts(query_local)
    bias_local = b_query.reshape(heads_each, query_cols)
    fly_bias = col_parts(bias_local)
    fly_x, fly_kv = barrier(fly_x, fly_kv)

    w_up_late, _ = barrier(w_up, fly_x)
    w_up_all = lax.all_gather(w_up_late, "row", axis=0, tiled=True)

    fly_x = advance(steps_x, fly_x)
    fly_kv = advance(steps_kv, fly_kv)
    w_out_late, _ = barrier(w_out, fly_bias)
    fly_out = col_parts(w_out_late)
    fly_x, fly_kv = barrier(fly_x, fly_kv)

    fly_kv = advance(steps_kv, fly_kv)
    cot_late, _ = barrier(cotangent, fly_x)
    cot_own = lax.all_to_all(cot_late, "row", 0, 1, tiled=True)
    mine, theirs = finish(steps_x, fly_x)
    first_all, own_low, vectors = norm_gathered(mine, theirs, tokens_col, span)
    gain1, shift1, bias_out, gain2, shift2, bias_down = (vectors[k : k + 1] for k in range(6))
    first_all, own_low, fly_kv, fly_q, fly_bias, cot_own = barrier(
        first_all, own_low, fly_kv, fly_q, fly_bias, cot_own
    )

    w_kv_all = in_row_order(jnp.concatenate(finish(steps_kv, fly_kv), 0), 0)
    own = own_low.astype(F32)
    first_low = lax.dynamic_slice_in_dim(first_all, row * span, span, 0)
    kv_own = dot_plain(first_low, w_kv_all).astype(BF16)
    fly_kv = col_parts(kv_own)
    query_flat = col_join(query_local, fly_q).reshape(rows, features, query_cols)
    w_query_row = exchange_rows(query_flat)
    bias_query = lax.dynamic_slice(
        col_join(bias_local, fly_bias), (row // heads_each, row % heads_each, 0), (1, 1, query_cols)
    ).reshape(1, query_cols)
    fly_kv, w_query_row = barrier(fly_kv, w_query_row)
    steps_kv = row_gather(col_join(kv_own, fly_kv).reshape(cols * span, -1))
    fly_kv = next(steps_kv)
    w_out_all = lax.all_gather(
        col_join(w_out, fly_out).reshape(cols * head_cols, features), "row", axis=1, tiled=True
    )
    queries = (dot_plain(first_all, w_query_row.reshape(width, query_cols)) + bias_query).astype(
        BF16
    )
    fly_kv, queries = barrier(fly_kv, queries)
    fly_cot = col_parts(cot_own)
    kv_all = jnp.concatenate(finish(steps_kv, advance(steps_kv, fly_kv)), 0)
    queries, kv_all, w_up_all = barrier(queries, kv_all, w_up_all)

    attend, attend_back = attention_calls(seq_blocks, tokens_col, span, head_dim, query_cols)
    core_turned, logs, attn_low = attend(queries, kv_all, b_value[None, :])
    attn_own = lax.all_to_all(attn_low, "row", 0, 1, tiled=True)
    attn_own, w_out_all, fly_cot = barrier(attn_own, w_out_all, fly_cot)
    w_down_late, _ = barrier(w_down, w_out_all)
    w_down_all = lax.all_gather(w_down_late, "row", axis=1, tiled=True)
    middle = own + dot_plain(attn_own, w_out_all) + bias_out

    normed2, scale2 = norm_forward(middle)
    second_low = (normed2 * gain2 + shift2).astype(BF16)
    fly_second = col_parts(second_low)
    query_strip = jnp.transpose(query_flat, (1, 0, 2)).reshape(features, rows * query_cols)
    query_strip, _ = barrier(query_strip, w_down_all)
    w_query_all = lax.all_gather(query_strip, "row", axis=0, tiled=True)
    cot_all = col_join(cot_own, fly_cot).reshape(cols * span, width)
    fly_second, cot_all, w_down_all = barrier(fly_second, cot_all, w_down_all)
    second_all = col_join(second_low, fly_second).reshape(cols * span, width)
    grad_hidden = dot_last(cot_all, w_down_all)
    pre = dot_plain(second_all, w_up_all) + b_up
    gelu_value, gelu_back = jax.vjp(partial(jax.nn.gelu, approximate=True), pre)
    hidden = gelu_value.astype(BF16)
    grad_pre = gelu_back(grad_hidden)[0].astype(BF16)
    fly_second = col_send(dot_last(grad_pre, w_up_all).reshape(cols, span, width))
    down_part = dot_first(hidden, cot_all).astype(BF16)
    up_part = dot_first(second_all, grad_pre).astype(BF16)
    grad_w_down = lax.psum_scatter(down_part, "row", scatter_dimension=1, tiled=True).astype(F32)
    grad_w_up = lax.psum_scatter(up_part, "row", scatter_dimension=0, tiled=True).astype(F32)
    fly_second, _, _, w_query_all = barrier(fly_second, down_part, up_part, w_query_all)

    grad_in2, gain2_part, shift2_part = norm_backward(add_up(fly_second), normed2, scale2, gain2)
    grad_middle = cot_own.astype(F32) + grad_in2
    mid_low = grad_middle.astype(BF16)
    grad_attn_own = dot_last(mid_low, w_out_all).astype(BF16)
    grad_attn = lax.all_to_all(grad_attn_own, "row", 1, 0, tiled=True)
    steps_mid = row_gather(mid_low)
    fly_mid = next(steps_mid)
    late_hidden, _ = barrier(hidden, mid_low)
    out_part = dot_plain(late_hidden, w_down_all).astype(BF16)
    grad_attn, fly_mid, out_part = barrier(grad_attn, fly_mid, out_part)
    fly_mid = advance(steps_mid, fly_mid)
    fly_block = col_send(out_part.reshape(cols, span, width))

    grad_queries, key_mine, key_theirs, value_mine, value_theirs = attend_back(
        queries, grad_attn, core_turned, logs, kv_all
    )
    grad_queries, key_theirs, value_theirs, fly_mid = barrier(
        grad_queries, key_theirs, value_theirs, fly_mid
    )

    steps_kv = row_scatter([key_mine, value_mine], [key_theirs, value_theirs])
    fly_kv = next(steps_kv)
    queries_own = lax.all_to_all(grad_queries, "row", 0, 1, tiled=True)
    fly_mid = advance(steps_mid, fly_mid)
    query_part = dot_first(first_all, grad_queries).astype(BF16)
    fly_kv, fly_mid, query_part = barrier(fly_kv, fly_mid, query_part)
    fly_kv = advance(steps_kv, fly_kv)
    mid_mine, mid_theirs = finish(steps_mid, fly_mid)
    attn_tokens = attn_low.reshape(rows, span, query_cols)
    apart = [2 * k for k in range(rows // 2)]

    def attn_rows(offset):
        return jnp.concatenate(
            [
                lax.dynamic_index_in_dim(attn_tokens, row ^ (p + offset), 0, keepdims=False)
                for p in apart
            ],
            0,
        )

    out_part = (
        dot_first(mid_mine.reshape(-1, width), attn_rows(0))
        + dot_first(mid_theirs.reshape(-1, width), attn_rows(1))
    ).astype(BF16)
    query_bias = padded(in_parts(jnp.sum(grad_queries.astype(F32), 0), 2), 16)
    up_bias = in_parts(jnp.sum(grad_pre.astype(F32), 0), 2).reshape(-1, query_cols)
    up_rows = up_bias.shape[0]
    extra = jnp.concatenate([query_bias, padded(up_bias, 16)], 0)
    fly_kv, queries_own, out_part = barrier(fly_kv, queries_own, out_part)
    fly_kv = advance(steps_kv, fly_kv)
    first_part = dot_last(queries_own, w_query_all)
    weights = exchange_rows(
        jnp.concatenate(
            [
                query_part.reshape(rows, features, query_cols),
                out_part.reshape(rows, features, query_cols),
                jnp.broadcast_to(extra[None], (rows,) + extra.shape),
            ],
            1,
        )
    )
    fly_kv, fly_block, first_part = barrier(fly_kv, fly_block, first_part)
    kv_group = jnp.concatenate(finish(steps_kv, fly_kv), -1)
    fly_kv = col_send(kv_group.reshape(cols, span, -1))
    out_own = (middle + add_up(fly_block) + bias_down).astype(BF16)
    fly_kv, weights = barrier(fly_kv, weights)

    both = 2 * features + 16
    fly_weights = col_send(weights[:, :both].reshape(cols, heads_each, both, query_cols))
    up_total = total(weights[:, both : both + up_rows]).reshape(2, up_cols)
    kv_mine = add_up(fly_kv).astype(BF16)
    grad_first = first_part + dot_last(kv_mine, w_kv_all)
    kv_part = dot_first(first_low, kv_mine).astype(BF16)
    normed1, scale1 = norm_forward(own)
    grad_in1, gain1_part, shift1_part = norm_backward(grad_first, normed1, scale1, gain1)
    feature_parts = jnp.stack(
        [
            gain1_part,
            shift1_part,
            gain2_part,
            shift2_part,
            jnp.sum(mid_low.astype(F32), 0),
            jnp.sum(cot_own.astype(F32), 0),
        ]
    )
    value_part = jnp.sum(grad_attn_own.astype(F32).reshape(-1, head_dim), 0)
    value_rows = jnp.broadcast_to(
        jnp.pad(in_parts(value_part, 2), ((0, 0), (0, features - head_dim)))[None],
        (rows, 2, features),
    )
    feature_rows = jnp.transpose(
        in_parts(feature_parts, 2).reshape(12, rows, features), (1, 0, 2)
    )
    grad_low = jnp.transpose(
        (grad_middle + grad_in1).astype(BF16).reshape(span, rows, features), (1, 0, 2)
    )
    kv_wide = kv_part.reshape(rows, -1, features)
    kv_rows = kv_wide.shape[1]
    last = exchange_rows(
        jnp.concatenate(
            [
                grad_low,
                kv_wide,
                feature_rows,
                value_rows,
                jnp.zeros((rows, 2, features), BF16),
            ],
            1,
        )
    )
    block_output = lax.all_to_all(out_own, "row", 1, 0, tiled=True)
    grad_inputs = last[:, :span].reshape(tokens_col, features).astype(F32)
    kv_sum = total(last[:, span : span + kv_rows]).reshape(features, cols, kv_cols)
    grad_w_keyval = add_up(col_send(jnp.transpose(kv_sum, (1, 0, 2))))
    sums = total(last[:, span + kv_rows : span + kv_rows + 16])
    sums = add_up([sums] + col_parts(sums))
    by_feature = sums[0:6] + sums[6:12]
    grad_b_value = (sums[12] + sums[13])[:head_dim]

    weights = add_up(fly_weights)
    grad_w_query = jnp.transpose(weights[:, :features], (1, 0, 2)).reshape(features, head_cols)
    grad_w_out = jnp.transpose(weights[:, features : 2 * features], (0, 2, 1)).reshape(
        head_cols, features
    )
    grad_b_query = (weights[:, 2 * features] + weights[:, 2 * features + 1]).reshape(head_cols)
    return (
        block_output,
        grad_inputs,
        by_feature[0],
        by_feature[1],
        grad_w_query,
        grad_b_query,
        grad_w_keyval,
        grad_b_value,
        grad_w_out,
        by_feature[4],
        by_feature[2],
        by_feature[3],
        grad_w_up,
        up_total[0] + up_total[1],
        grad_w_down,
        by_feature[5],
    )


def solution(mesh):
    both, rows, cols = P("col", "row"), P("row"), P("col")
    return jax.shard_map(
        body,
        mesh=mesh,
        in_specs=(
            both, both, P(), rows, rows, P("row", "col"), cols, P("row", "col"), P(), both, rows,
            rows, rows, P("row", "col"), cols, both, rows,
        ),
        out_specs=(
            both, both, rows, rows, P("row", "col"), cols, P("row", "col"), P(), both, rows,
            rows, rows, P("row", "col"), cols, both, rows,
        ),
        check_vma=False,
    )
```

time: 1410 us -> 671 us (0.48)
  waiting for transfers between devices: 1090 us -> 268 us
  starting transfers between devices: 12.8 us -> 164 us
  blocking collectives: 94.7 us -> 0 us
  matrix products: 117 us -> 76.6 us
  local copies, waits for them, and re-layouts: 21.8 us -> 59.6 us
  Pallas kernels: 0 us -> 24.1 us
    reduce_scatter x10 -> x2, waiting for transfers between devices: 553 us -> 0.01 us  [the longest x1 0.01 us: body(): lax.psum_scatter(up_part, 'row', scatter_dimension=0, tiled=True)]
    all_gather x9 -> x4, waiting for transfers between devices: 421 us -> 64.8 us  [the longest x1 64.8 us: body(): w_down_all = lax.all_gather(w_down_late, 'row', axis=1, tiled=True)]
    ppermute x0 -> x65, waiting for transfers between devices: none -> 185 us  [the longest x15 68.4 us: col_send(): lax.ppermute(part, 'col', [(i, (i + step) % count) for i in range(count)])]
    ppermute x0 -> x65, starting transfers between devices: none -> 130 us  [the longest x15 57.1 us: col_send(): lax.ppermute(part, 'col', [(i, (i + step) % count) for i in range(count)])]
    psum x1 -> x0, waiting for transfers between devices: 118 us -> none  [body(): lax.psum((place_slice(first_gain_part, width, row_index), place_slice(fir...]
    psum x6 -> x0, blocking collectives: 80.1 us -> none  [feature_total(): return lax.psum(values, 'row')]
    dot_general x23 -> x16, matrix products: 117 us -> 76.6 us  [the longest x5 28.7 us: dot_last(): lax.dot_general(left, right, (((1,), (1,)), ((), ())), preferred_element_...]
    all_to_all x0 -> x8, starting transfers between devices: none -> 33 us  [the longest x3 13.2 us: exchange_rows(): return lax.all_to_all(pieces.astype(BF16), 'row', 0, 0)]
  transfers between devices with their start and end apart: 20 -> 79, of which waited for: 20 -> 32; matrix products, arithmetic and copies ran while one was open for 7% -> 26% of each run, Pallas kernels for 0% -> 4%
where the time goes in v1:
time: 671 us; the launch traced here: 661 us
  waiting for transfers between devices  268 us (40%)
  starting transfers between devices  164 us (24%)
  matrix products  76.6 us (11%)
  local copies, waits for them, and re-layouts  59.6 us (9%)
  other arithmetic  52.1 us (8%)
  Pallas kernels  24.1 us (4%)
  between operations  16.4 us (2%)
    ppermute x15, waiting for transfers between devices, col_send(): lax.ppermute(part, 'col', [(i, (i + step) % count) for i in range(count)])  68.4 us
    ppermute x24, waiting for transfers between devices, col_parts(): lax.ppermute(value, 'col', [(i, (i + step) % count) for i in range(count)])  67.5 us
    all_gather x1, waiting for transfers between devices, body(): w_down_all = lax.all_gather(w_down_late, 'row', axis=1, tiled=True)  64.8 us
    ppermute x15, starting transfers between devices, col_send(): lax.ppermute(part, 'col', [(i, (i + step) % count) for i in range(count)])  57.1 us
    ppermute x26, waiting for transfers between devices, swap(): return lax.ppermute(value, 'row', [(i, i ^ bit) for i in range(count)])  49.1 us
    ppermute x24, starting transfers between devices, col_parts(): lax.ppermute(value, 'col', [(i, (i + step) % count) for i in range(count)])  43 us
    ppermute x26, starting transfers between devices, swap(): return lax.ppermute(value, 'row', [(i, i ^ bit) for i in range(count)])  29.7 us
    dot_general x5, matrix products, dot_last(): lax.dot_general(left, right, (((1,), (1,)), ((), ())), preferred_element_...  28.7 us
  transfers between devices with their start and end apart: 79, of which 32 were waited for; matrix products, arithmetic and copies ran while one was open for 26% of the time, Pallas kernels for 4%

profile of v1, /device:TPU:0, one launch (start us, length us, event | category | flops | bytes accessed | tf_op | source)
XLA Modules:
  0.0 660.8 jit_solution(5808826601042458369)
XLA Ops:
  27.6 9.8 %collective-permute-done.7 = bf16[1,256,128]{1,2,0:T(8,128)(2,1)S(1)} collective-permute-done((bf16[1,256,128]{1,2,0:T(8,128)(2,1)S(1)}, bf16[1,256,128]{1,2,0:T(8,128)(2,1)S(1)}, u32[]{:S(2)}, u32[]{:S(2)}) %collective-permute-start.7) | collective-permute-done | bytes 65568 | tf_op jit(solution)/shard_map/ppermute | solution.py:67
  49.0 7.0 %collective-permute-done.27 = bf16[512,256]{1,0:T(8,128)(2,1)S(1)} collective-permute-done((bf16[512,256]{1,0:T(8,128)(2,1)S(1)}, bf16[512,256]{1,0:T(8,128)(2,1)S(1)}, u32[]{:S(2)}, u32[]{:S(2)}) %collective-permute-start.27) | collective-permute-done | bytes 262176 | tf_op jit(solution)/shard_map/ppermute | solution.py:25
  85.7 7.9 %norm_gathered.1 = (bf16[1024,2048]{1,0:T(8,128)(2,1)}, bf16[128,2048]{1,0:T(8,128)(2,1)}, f32[8,2048]{1,0:T(8,128)}) custom-call(s32[1]{0:T(128)} %bitcast.me_ref, bf16[4,1056,256]{2,1,0:T(8,128)(2,1)} %copy-done, bf16[4,1056,256]{2,1,0:T(8,128)(2,1)} %collective-permute-done.9.theirs_ref.theirs_vec.theirs_own, bf16[4,1056,256]{2,1,0:T(8,128)(2,1)} %copy-done, ...), custom_call_target="tpu_custom_call" | custom-call | tf_op jit(solution)/shard_map/norm_gathered/pallas_call | solution.py:205
  120.1 13.8 %all-to-all-done.1 = bf16[8,256,256]{2,1,0:T(8,128)(2,1)} async-done(((bf16[8,256,256]{2,1,0:T(8,128)(2,1)}), bf16[8,256,256]{2,1,0:T(8,128)(2,1)}, u32[]{:S(2)}, u32[]{:S(2)}) %all-to-all-start.1) | async-done | bytes 1048608 | tf_op jit(solution)/shard_map/all_to_all | solution.py:58
  142.9 8.7 %collective-permute-done.24 = bf16[2,512,128]{2,1,0:T(8,128)(2,1)S(1)} collective-permute-done((bf16[2,512,128]{2,1,0:T(8,128)(2,1)S(1)}, bf16[2,512,128]{2,1,0:T(8,128)(2,1)S(1)}, u32[]{:S(2)}, u32[]{:S(2)}) %collective-permute-start.24) | collective-permute-done | bytes 262176 | tf_op jit(solution)/shard_map/ppermute | solution.py:67
  165.5 6.5 attend_forward.1
  179.1 16.3 %collective-permute-done.31 = bf16[128,2048]{1,0:T(8,128)(2,1)} collective-permute-done((bf16[128,2048]{1,0:T(8,128)(2,1)S(1)}, bf16[128,2048]{1,0:T(8,128)(2,1)}, u32[]{:S(2)}, u32[]{:S(2)}) %collective-permute-start.31) | collective-permute-done | bytes 524320 | tf_op jit(solution)/shard_map/ppermute | solution.py:25
  197.7 64.8 %all-gather.9.cloned.1.call-done = bf16[2048,2048]{1,0:T(8,128)(2,1)} async-done(((bf16[2048,256]{1,0:T(8,128)(2,1)}), bf16[2048,2048]{1,0:T(8,128)(2,1)}) %all-gather.9.cloned.1.call-update) | async-done | bytes 8388624 | tf_op jit(solution)/shard_map/all_gather | solution.py:527
  278.3 8.1 %collective-permute-done.33 = bf16[128,2048]{1,0:T(8,128)(2,1)S(1)} collective-permute-done((bf16[128,2048]{1,0:T(8,128)(2,1)S(1)}, bf16[128,2048]{1,0:T(8,128)(2,1)S(1)}, u32[]{:S(2)}, u32[]{:S(2)}) %collective-permute-start.33) | collective-permute-done | bytes 524320 | tf_op jit(solution)/shard_map/ppermute | solution.py:25
  286.4 21.7 %collective-permute-done.34 = bf16[128,2048]{1,0:T(8,128)(2,1)S(1)} collective-permute-done((bf16[128,2048]{1,0:T(8,128)(2,1)S(1)}, bf16[128,2048]{1,0:T(8,128)(2,1)S(1)}, u32[]{:S(2)}, u32[]{:S(2)}) %collective-permute-start.34) | collective-permute-done | bytes 524320 | tf_op jit(solution)/shard_map/ppermute | solution.py:25
  313.0 8.9 %convert_reduce_fusion = (f32[2048]{0:T(1024)}, bf16[512,2048]{1,0:T(8,128)(2,1)S(1)}, bf16[512,2048]{1,0:T(8,128)(2,1)}) fusion(f32[512,2048]{1,0:T(8,128)S(1)} %fusion.92, f32[2048]{0:T(1024)S(1)} %copy-done.53, bf16[512,2048]{1,0:T(8,128)(2,1)S(1)} %bitcast.389, bf16[2048,2048]{1,0:T(8,128)(2,1)S(1)} %bitcast.463), kind=kOutput, calls=%fused_computation.11 | convolution fusion | flops 4321179648 | bytes 18890752 | tf_op jit(solution)/shard_map/dot_general | solution.py:232
  323.2 6.9 %convolution_convert_fusion = bf16[2048,2048]{1,0:T(8,128)(2,1)} fusion(bf16[512,2048]{1,0:T(8,128)(2,1)S(1)} %bitcast.388, bf16[512,2048]{1,0:T(8,128)(2,1)S(1)} %get-tuple-element.287), kind=kOutput, calls=%fused_computation | convolution fusion | flops 4299161600 | bytes 12582912 | tf_op jit(solution)/shard_map/dot_general | solution.py:236
  331.4 8.5 %convolution_convert_fusion.3 = bf16[512,2048]{1,0:T(8,128)(2,1)S(1)} fusion(bf16[512,2048]{1,0:T(8,128)(2,1)} %copy-done.56, bf16[2048,2048]{1,0:T(8,128)(2,1)} %all-gather.5.cloned.1.call-done), kind=kOutput, calls=%fused_computation.14 | convolution fusion | flops 4296015872 | bytes 12582912 | tf_op jit(solution)/shard_map/dot_general | solution.py:232
  341.1 12.0 %collective-permute-start.36 = (bf16[128,2048]{1,0:T(8,128)(2,1)}, bf16[128,2048]{1,0:T(8,128)(2,1)S(1)}, u32[]{:S(2)}, u32[]{:S(2)}) collective-permute-start(bf16[128,2048]{1,0:T(8,128)(2,1)} %get-tuple-element.303), channel_id=1, source_target_pairs={{0,1},{1,2},{2,3},{3,0},{4,5},{5,6},{6,7},{7,4},{8,9},{9,10},{10,1... | collective-permute-start | bytes 1572872 | tf_op jit(solution)/shard_map/ppermute | solution.py:48
  355.5 6.8 %convolution_convert_fusion.1 = bf16[2048,2048]{1,0:T(8,128)(2,1)} fusion(bf16[512,2048]{1,0:T(8,128)(2,1)S(1)} %copy-done.55, bf16[512,2048]{1,0:T(8,128)(2,1)S(1)} %bitcast.390), kind=kOutput, calls=%fused_computation.1 | convolution fusion | flops 4299161600 | bytes 12582912 | tf_op jit(solution)/shard_map/dot_general | solution.py:236
  366.9 21.3 %collective-permute-done.37 = bf16[128,2048]{1,0:T(8,128)(2,1)} collective-permute-done((bf16[128,2048]{1,0:T(8,128)(2,1)}, bf16[128,2048]{1,0:T(8,128)(2,1)}, u32[]{:S(2)}, u32[]{:S(2)}) %collective-permute-start.37) | collective-permute-done | bytes 524320 | tf_op jit(solution)/shard_map/ppermute | solution.py:48
  392.9 6.3 convolution_convert_fusion.6
  407.3 9.9 %convolution_convert_fusion.2 = bf16[512,2048]{1,0:T(8,128)(2,1)} fusion(bf16[512,2048]{1,0:T(8,128)(2,1)} %get-tuple-element.170, bf16[2048,2048]{1,0:T(8,128)(2,1)} %all-gather.9.cloned.1.call-done), kind=kOutput, calls=%fused_computation.13 | convolution fusion | flops 4296015872 | bytes 12582912 | tf_op jit(solution)/shard_map/dot_general | solution.py:240
  428.8 9.7 %attend_backward.1 = (bf16[1024,256]{1,0:T(8,128)(2,1)}, f32[4,512,128]{2,1,0:T(8,128)}, bf16[4,512,128]{2,1,0:T(8,128)(2,1)}, f32[4,512,128]{2,1,0:T(8,128)}, bf16[4,512,128]{2,1,0:T(8,128)(2,1)}) custom-call(s32[4]{0:T(128)} %select_reduce_fusion.low_ref, s32[4]{0:T(128)} %get-tuple-element.382.high_ref, s32[1]{0:T(128)} %bitcast.me_ref, ...), custom_call_target="tpu_custom_call" | custom-call | tf_op jit(solution)/shard_map/attend_backward/pallas_call | solution.py:386
  451.8 13.1 %collective-permute-start.50 = (bf16[128,2048]{1,0:T(8,128)(2,1)}, bf16[128,2048]{1,0:T(8,128)(2,1)}, u32[]{:S(2)}, u32[]{:S(2)}) collective-permute-start(bf16[128,2048]{1,0:T(8,128)(2,1)} %get-tuple-element.299), channel_id=1, source_target_pairs={{0,1},{1,2},{2,3},{3,0},{4,5},{5,6},{6,7},{7,4},{8,9},{9,10},{10,1... | collective-permute-start | bytes 1572872 | tf_op jit(solution)/shard_map/ppermute | solution.py:48
  465.0 18.8 %collective-permute-start.51 = (bf16[128,2048]{1,0:T(8,128)(2,1)}, bf16[128,2048]{1,0:T(8,128)(2,1)}, u32[]{:S(2)}, u32[]{:S(2)}) collective-permute-start(bf16[128,2048]{1,0:T(8,128)(2,1)} %get-tuple-element.298), channel_id=1, source_target_pairs={{0,2},{1,3},{2,0},{3,1},{4,6},{5,7},{6,4},{7,5},{8,10},{9,11},{10,... | collective-permute-start | bytes 1572872 | tf_op jit(solution)/shard_map/ppermute | solution.py:48
  528.2 19.5 %collective-permute-done.48 = bf16[1,512,128]{2,1,0:T(8,128)(2,1)S(1)} collective-permute-done((bf16[1,512,128]{2,1,0:T(8,128)(2,1)S(1)}, bf16[1,512,128]{2,1,0:T(8,128)(2,1)S(1)}, u32[]{:S(2)}, u32[]{:S(2)}) %collective-permute-start.48) | collective-permute-done | bytes 131104 | tf_op jit(solution)/shard_map/ppermute | solution.py:67
  567.0 8.0 %concatenate.112 = bf16[8,400,256]{2,1,0:T(8,128)(2,1)} concatenate(bf16[8,128,256]{2,1,0:T(8,128)(2,1)} %bitcast.385, bf16[8,256,256]{2,1,0:T(8,128)(2,1)S(1)} %bitcast.376, bf16[8,12,256]{2,1,0:T(8,128)(2,1)S(1)} %copy.153, bf16[8,2,256]{2,1,0:T(2,128)(2,1)S(1)} %broadcast_in_dim.191, bf16[8,2,256]{2,1,0:T(2,128)(2,1)S(1)} %broadcast_in_dim.192), dimensions={1} | concatenate | bytes 3276800 | tf_op jit(solution)/shard_map/concatenate | solution.py:650
  595.1 35.0 %collective-permute-done.60 = bf16[2,528,256]{2,1,0:T(8,128)(2,1)} collective-permute-done((bf16[2,528,256]{2,1,0:T(8,128)(2,1)S(1)}, bf16[2,528,256]{2,1,0:T(8,128)(2,1)}, u32[]{:S(2)}, u32[]{:S(2)}) %collective-permute-start.60) | collective-permute-done | bytes 540704 | tf_op jit(solution)/shard_map/ppermute | solution.py:48
  (477 shorter events, 295.0 us)
Async XLA Ops:
  7.2 157.0 %all-gather.5.cloned.1.call-start = ((), (), s32[]{:S(2)}) async-start(), calls=%async_computation.10 | async-start | bytes 9437184 | tf_op jit(solution)/shard_map/all_gather | solution.py:480
  37.4 157.9 %all-gather.7.cloned.1.call-start = ((), (), s32[]{:S(2)}) async-start(), calls=%async_computation.11 | async-start | bytes 9437184 | tf_op jit(solution)/shard_map/all_gather | solution.py:511
  70.4 28.0 %collective-permute-start.13 = (bf16[2,256,256]{1,2,0:T(8,128)(2,1)S(1)}, bf16[2,256,256]{1,2,0:T(8,128)(2,1)S(1)}, u32[]{:S(2)}, u32[]{:S(2)}) collective-permute-start(bf16[2,256,256]{1,2,0:T(8,128)(2,1)S(1)} %bitcast.411), channel_id=1, source_target_pairs={{0,1},{1,2},{2,3},{3,0},{4,5},{5,6},{6,7},{7,4},{8,9},{9,10},{10,1... | collective-permute-start | bytes 786440 | tf_op jit(solution)/shard_map/ppermute | solution.py:25
  103.7 30.2 %all-to-all-start.1 = ((bf16[8,256,256]{2,1,0:T(8,128)(2,1)}), bf16[8,256,256]{2,1,0:T(8,128)(2,1)}, u32[]{:S(2)}, u32[]{:S(2)}) async-start(bf16[8,256,256]{2,1,0:T(8,128)(2,1)} %bitcast.60), calls=%async_computation.1 | async-start | bytes 2097152 | tf_op jit(solution)/shard_map/all_to_all | solution.py:58
  158.0 37.3 %collective-permute-start.31 = (bf16[128,2048]{1,0:T(8,128)(2,1)S(1)}, bf16[128,2048]{1,0:T(8,128)(2,1)}, u32[]{:S(2)}, u32[]{:S(2)}) collective-permute-start(bf16[128,2048]{1,0:T(8,128)(2,1)S(1)} %bitcast.372), channel_id=1, source_target_pairs={{0,2},{1,3},{2,0},{3,1},{4,6},{5,7},{6,4},{7,5},{8,10},{9,11},{10,... | collective-permute-start | bytes 1572872 | tf_op jit(solution)/shard_map/ppermute | solution.py:25
  160.4 34.9 %collective-permute-start.32 = (bf16[128,2048]{1,0:T(8,128)(2,1)S(1)}, bf16[128,2048]{1,0:T(8,128)(2,1)}, u32[]{:S(2)}, u32[]{:S(2)}) collective-permute-start(bf16[128,2048]{1,0:T(8,128)(2,1)S(1)} %bitcast.373), channel_id=1, source_target_pairs={{0,3},{1,0},{2,1},{3,2},{4,7},{5,4},{6,5},{7,6},{8,11},{9,8},{10,9... | collective-permute-start | bytes 1572872 | tf_op jit(solution)/shard_map/ppermute | solution.py:25
  179.0 83.4 %all-gather.9.cloned.1.call-start = ((), (), s32[]{:S(2)}) async-start(), calls=%async_computation.12 | async-start | bytes 9437184 | tf_op jit(solution)/shard_map/all_gather | solution.py:527
  195.4 192.8 %all-gather.11.cloned.1.call-start = ((), (), s32[]{:S(2)}) async-start(), calls=%async_computation.13 | async-start | bytes 9437184 | tf_op jit(solution)/shard_map/all_gather | solution.py:535
  262.5 321.8 %reduce-scatter.3.cloned.1.call-start = ((), (), s32[]{:S(2)}) async-start(), calls=%async_computation.14 | async-start | bytes 9437184 | tf_op jit(solution)/shard_map/reduce_scatter | solution.py:548
  271.2 37.0 %collective-permute-start.34 = (bf16[128,2048]{1,0:T(8,128)(2,1)S(1)}, bf16[128,2048]{1,0:T(8,128)(2,1)S(1)}, u32[]{:S(2)}, u32[]{:S(2)}) collective-permute-start(bf16[128,2048]{1,0:T(8,128)(2,1)S(1)} %get-tuple-element.292), channel_id=1, source_target_pairs={{0,2},{1,3},{2,0},{3,1},{4,6},{5,7},{6,4},{7,5},{8,10},{9,11},{10,... | collective-permute-start | bytes 1572872 | tf_op jit(solution)/shard_map/ppermute | solution.py:25
  273.6 34.6 %collective-permute-start.35 = (bf16[128,2048]{1,0:T(8,128)(2,1)S(1)}, bf16[128,2048]{1,0:T(8,128)(2,1)S(1)}, u32[]{:S(2)}, u32[]{:S(2)}) collective-permute-start(bf16[128,2048]{1,0:T(8,128)(2,1)S(1)} %get-tuple-element.292), channel_id=1, source_target_pairs={{0,3},{1,0},{2,1},{3,2},{4,7},{5,4},{6,5},{7,6},{8,11},{9,8},{10,9... | collective-permute-start | bytes 1572872 | tf_op jit(solution)/shard_map/ppermute | solution.py:25
  330.1 256.9 %reduce-scatter.5.cloned.1.call-start = ((), (), s32[]{:S(2)}) async-start(), calls=%async_computation.15 | async-start | bytes 9437184 | tf_op jit(solution)/shard_map/reduce_scatter | solution.py:547
  353.1 35.0 %collective-permute-start.37 = (bf16[128,2048]{1,0:T(8,128)(2,1)}, bf16[128,2048]{1,0:T(8,128)(2,1)}, u32[]{:S(2)}, u32[]{:S(2)}) collective-permute-start(bf16[128,2048]{1,0:T(8,128)(2,1)} %get-tuple-element.302), channel_id=1, source_target_pairs={{0,2},{1,3},{2,0},{3,1},{4,6},{5,7},{6,4},{7,5},{8,10},{9,11},{10,... | collective-permute-start | bytes 1572872 | tf_op jit(solution)/shard_map/ppermute | solution.py:48
  354.3 33.8 %collective-permute-start.38 = (bf16[128,2048]{1,0:T(8,128)(2,1)}, bf16[128,2048]{1,0:T(8,128)(2,1)}, u32[]{:S(2)}, u32[]{:S(2)}) collective-permute-start(bf16[128,2048]{1,0:T(8,128)(2,1)} %get-tuple-element.301), channel_id=1, source_target_pairs={{0,3},{1,0},{2,1},{3,2},{4,7},{5,4},{6,5},{7,6},{8,11},{9,8},{10,9... | collective-permute-start | bytes 1572872 | tf_op jit(solution)/shard_map/ppermute | solution.py:48
  444.9 49.4 %collective-permute-start.45 = (bf16[4,128,2048]{2,1,0:T(8,128)(2,1)}, bf16[4,128,2048]{2,1,0:T(8,128)(2,1)}, u32[]{:S(2)}, u32[]{:S(2)}) collective-permute-start(bf16[4,128,2048]{2,1,0:T(8,128)(2,1)} %pad_maximum_fusion.2), channel_id=1, source_target_pairs={{0,4},{4,0},{8,12},{12,8},{16,20},{20,16},{24,28},{28,24},{1,5},{5... | collective-permute-start | bytes 6291464 | tf_op jit(solution)/shard_map/ppermute | solution.py:67
  451.8 76.3 %collective-permute-start.50 = (bf16[128,2048]{1,0:T(8,128)(2,1)}, bf16[128,2048]{1,0:T(8,128)(2,1)}, u32[]{:S(2)}, u32[]{:S(2)}) collective-permute-start(bf16[128,2048]{1,0:T(8,128)(2,1)} %get-tuple-element.299), channel_id=1, source_target_pairs={{0,1},{1,2},{2,3},{3,0},{4,5},{5,6},{6,7},{7,4},{8,9},{9,10},{10,1... | collective-permute-start | bytes 1572872 | tf_op jit(solution)/shard_map/ppermute | solution.py:48
  465.0 63.2 %collective-permute-start.51 = (bf16[128,2048]{1,0:T(8,128)(2,1)}, bf16[128,2048]{1,0:T(8,128)(2,1)}, u32[]{:S(2)}, u32[]{:S(2)}) collective-permute-start(bf16[128,2048]{1,0:T(8,128)(2,1)} %get-tuple-element.298), channel_id=1, source_target_pairs={{0,2},{1,3},{2,0},{3,1},{4,6},{5,7},{6,4},{7,5},{8,10},{9,11},{10,... | collective-permute-start | bytes 1572872 | tf_op jit(solution)/shard_map/ppermute | solution.py:48
  494.3 33.9 %collective-permute-start.52 = (bf16[128,2048]{1,0:T(8,128)(2,1)}, bf16[128,2048]{1,0:T(8,128)(2,1)}, u32[]{:S(2)}, u32[]{:S(2)}) collective-permute-start(bf16[128,2048]{1,0:T(8,128)(2,1)} %get-tuple-element.297), channel_id=1, source_target_pairs={{0,3},{1,0},{2,1},{3,2},{4,7},{5,4},{6,5},{7,6},{8,11},{9,8},{10,9... | collective-permute-start | bytes 1572872 | tf_op jit(solution)/shard_map/ppermute | solution.py:48
  513.2 43.1 %all-to-all-start.6 = ((bf16[8,544,256]{2,1,0:T(8,128)(2,1)}), bf16[8,544,256]{2,1,0:T(8,128)(2,1)}, u32[]{:S(2)}, u32[]{:S(2)}) async-start(bf16[8,544,256]{2,1,0:T(8,128)(2,1)} %pad_maximum_fusion), calls=%async_computation.6 | async-start | bytes 4456448 | tf_op jit(solution)/shard_map/all_to_all | solution.py:58
  518.8 28.8 %collective-permute-start.48 = (bf16[1,512,128]{2,1,0:T(8,128)(2,1)S(1)}, bf16[1,512,128]{2,1,0:T(8,128)(2,1)S(1)}, u32[]{:S(2)}, u32[]{:S(2)}) collective-permute-start(bf16[1,512,128]{2,1,0:T(8,128)(2,1)S(1)} %fusion.33), channel_id=1, source_target_pairs={{0,8},{4,12},{8,0},{12,4},{16,24},{20,28},{24,16},{28,20},{1,9},{5... | collective-permute-start | bytes 393224 | tf_op jit(solution)/shard_map/ppermute | solution.py:67
  521.9 25.8 %collective-permute-start.49 = (bf16[1,512,128]{2,1,0:T(8,128)(2,1)S(1)}, bf16[1,512,128]{2,1,0:T(8,128)(2,1)S(1)}, u32[]{:S(2)}, u32[]{:S(2)}) collective-permute-start(bf16[1,512,128]{2,1,0:T(8,128)(2,1)S(1)} %fusion.32), channel_id=1, source_target_pairs={{0,16},{4,20},{8,24},{12,28},{16,0},{20,4},{24,8},{28,12},{1,17},{... | collective-permute-start | bytes 393224 | tf_op jit(solution)/shard_map/ppermute | solution.py:67
  575.0 59.6 %all-to-all-start.7 = ((bf16[8,400,256]{2,1,0:T(8,128)(2,1)}), bf16[8,400,256]{2,1,0:T(8,128)(2,1)}, u32[]{:S(2)}, u32[]{:S(2)}) async-start(bf16[8,400,256]{2,1,0:T(8,128)(2,1)} %concatenate.112), calls=%async_computation.7 | async-start | bytes 3276800 | tf_op jit(solution)/shard_map/all_to_all | solution.py:58
  581.7 48.4 %collective-permute-start.60 = (bf16[2,528,256]{2,1,0:T(8,128)(2,1)S(1)}, bf16[2,528,256]{2,1,0:T(8,128)(2,1)}, u32[]{:S(2)}, u32[]{:S(2)}) collective-permute-start(bf16[2,528,256]{2,1,0:T(8,128)(2,1)S(1)} %get-tuple-element.296), channel_id=1, source_target_pairs={{0,2},{1,3},{2,0},{3,1},{4,6},{5,7},{6,4},{7,5},{8,10},{9,11},{10,... | collective-permute-start | bytes 1622024 | tf_op jit(solution)/shard_map/ppermute | solution.py:48
  582.2 47.9 %collective-permute-start.59 = (bf16[2,528,256]{2,1,0:T(8,128)(2,1)S(1)}, bf16[2,528,256]{2,1,0:T(8,128)(2,1)}, u32[]{:S(2)}, u32[]{:S(2)}) collective-permute-start(bf16[2,528,256]{2,1,0:T(8,128)(2,1)S(1)} %get-tuple-element.294), channel_id=1, source_target_pairs={{0,1},{1,2},{2,3},{3,0},{4,5},{5,6},{6,7},{7,4},{8,9},{9,10},{10,1... | collective-permute-start | bytes 1622024 | tf_op jit(solution)/shard_map/ppermute | solution.py:48
  (116 other events, 1451.5 us)
Sparse Core Ops, SparseCore 0:
  37.5 60.4 all-gather.4
  100.5 70.3 all-gather.6
  195.5 66.8 all-gather.8
  264.2 55.8 all-gather.10
  330.2 84.8 reduce-scatter.2
  418.5 73.1 reduce-scatter.4

commit v2 on v1

--- a/solution.py
+++ b/solution.py
@@ -92,17 +92,15 @@
     )
 
 
-def row_gather(value):
+def row_gather(value, hold=list):
     half = value.shape[-1] // 2
     bits = chip_bits()
     orders = (bits, bits[::-1])
     held = [{0: value[..., :half]}, {0: value[..., half:]}]
     for step in range(len(bits)):
         keys = [sorted(h) for h in held]
-        got = yield [
-            swap(jnp.stack([h[k] for k in ks]), order[step])
-            for h, ks, order in zip(held, keys, orders)
-        ]
+        ready = hold([jnp.stack([h[k] for k in ks]) for h, ks in zip(held, keys)])
+        got = yield [swap(part, order[step]) for part, order in zip(ready, orders)]
         for h, ks, order, new in zip(held, keys, orders, got):
             h.update({k ^ order[step]: new[n] for n, k in enumerate(ks)})
     own = jnp.stack([jnp.concatenate([held[0][k], held[1][k]], -1) for k in sorted(held[0])])
@@ -461,38 +459,49 @@
     steps_x = row_gather(jnp.concatenate([inputs, padded(vectors, 32)], 0))
     fly_x = next(steps_x)
     kv_local = w_keyval.reshape(-1, query_cols)
+    local_rows = kv_local.shape[0]
+    bias_local = in_parts(b_query.reshape(heads_each, query_cols), 3).reshape(-1, query_cols)
+    bias_rows = bias_local.shape[0]
+    kv_local = jnp.concatenate([kv_local, padded(bias_local, 16)], 0)
     fly_kv = col_parts(kv_local)
-    fly_x, fly_kv = barrier(fly_x, fly_kv)
-
+    query_local = jnp.transpose(w_query.reshape(features, heads_each, query_cols), (1, 0, 2))
+    fly_x, fly_kv, query_local, w_up_late, w_out_late = barrier(
+        fly_x, fly_kv, query_local, w_up, w_out
+    )
+
+    w_up_all = lax.all_gather(w_up_late, "row", axis=0, tiled=True)
+    fly_q = col_parts(query_local)
+    fly_out = col_parts(w_out_late)
     fly_x = advance(steps_x, fly_x)
+    kv_join = col_join(kv_local, fly_kv)
     kv_strip = jnp.transpose(
-        col_join(kv_local, fly_kv).reshape(cols, features, kv_cols), (1, 0, 2)
+        kv_join[:, :local_rows].reshape(cols, features, kv_cols), (1, 0, 2)
     ).reshape(features, cols * kv_cols)
+    bias_parts = lax.dynamic_index_in_dim(
+        kv_join[:, local_rows : local_rows + bias_rows], row // heads_each, 0, keepdims=False
+    ).reshape(3, heads_each, query_cols)
+    bias_query = jnp.sum(
+        lax.dynamic_index_in_dim(bias_parts, row % heads_each, 1, keepdims=True).astype(F32), 0
+    )
     steps_kv = row_gather(kv_strip)
     fly_kv = next(steps_kv)
-    query_local = jnp.transpose(w_query.reshape(features, heads_each, query_cols), (1, 0, 2))
-    fly_q = col_parts(query_local)
-    bias_local = b_query.reshape(heads_each, query_cols)
-    fly_bias = col_parts(bias_local)
-    fly_x, fly_kv = barrier(fly_x, fly_kv)
-
-    w_up_late, _ = barrier(w_up, fly_x)
-    w_up_all = lax.all_gather(w_up_late, "row", axis=0, tiled=True)
-
+    fly_x, fly_kv, fly_q = barrier(fly_x, fly_kv, fly_q)
+
+    query_flat = col_join(query_local, fly_q).reshape(rows, features, query_cols)
+    w_query_row = exchange_rows(query_flat)
     fly_x = advance(steps_x, fly_x)
     fly_kv = advance(steps_kv, fly_kv)
-    w_out_late, _ = barrier(w_out, fly_bias)
-    fly_out = col_parts(w_out_late)
     fly_x, fly_kv = barrier(fly_x, fly_kv)
 
     fly_kv = advance(steps_kv, fly_kv)
-    cot_late, _ = barrier(cotangent, fly_x)
-    cot_own = lax.all_to_all(cot_late, "row", 0, 1, tiled=True)
     mine, theirs = finish(steps_x, fly_x)
     first_all, own_low, vectors = norm_gathered(mine, theirs, tokens_col, span)
     gain1, shift1, bias_out, gain2, shift2, bias_down = (vectors[k : k + 1] for k in range(6))
-    first_all, own_low, fly_kv, fly_q, fly_bias, cot_own = barrier(
-        first_all, own_low, fly_kv, fly_q, fly_bias, cot_own
+    first_all, own_low, fly_kv, w_query_row, fly_out, cot_late = barrier(
+        first_all, own_low, fly_kv, w_query_row, fly_out, cotangent
+    )
+    w_out_all = lax.all_gather(
+        col_join(w_out, fly_out).reshape(cols * head_cols, features), "row", axis=1, tiled=True
     )
 
     w_kv_all = in_row_order(jnp.concatenate(finish(steps_kv, fly_kv), 0), 0)
@@ -500,82 +509,86 @@
     first_low = lax.dynamic_slice_in_dim(first_all, row * span, span, 0)
     kv_own = dot_plain(first_low, w_kv_all).astype(BF16)
     fly_kv = col_parts(kv_own)
-    query_flat = col_join(query_local, fly_q).reshape(rows, features, query_cols)
-    w_query_row = exchange_rows(query_flat)
-    bias_query = lax.dynamic_slice(
-        col_join(bias_local, fly_bias), (row // heads_each, row % heads_each, 0), (1, 1, query_cols)
-    ).reshape(1, query_cols)
-    fly_kv, w_query_row = barrier(fly_kv, w_query_row)
+    cot_own = lax.all_to_all(cot_late, "row", 0, 1, tiled=True)
+    (fly_kv,) = barrier(fly_kv)
     steps_kv = row_gather(col_join(kv_own, fly_kv).reshape(cols * span, -1))
     fly_kv = next(steps_kv)
-    w_out_all = lax.all_gather(
-        col_join(w_out, fly_out).reshape(cols * head_cols, features), "row", axis=1, tiled=True
-    )
     queries = (dot_plain(first_all, w_query_row.reshape(width, query_cols)) + bias_query).astype(
         BF16
     )
-    fly_kv, queries = barrier(fly_kv, queries)
+    kv_all = jnp.concatenate(finish(steps_kv, fly_kv), 0)
+    queries, kv_all, cot_own, w_up_all = barrier(queries, kv_all, cot_own, w_up_all)
     fly_cot = col_parts(cot_own)
-    kv_all = jnp.concatenate(finish(steps_kv, advance(steps_kv, fly_kv)), 0)
-    queries, kv_all, w_up_all = barrier(queries, kv_all, w_up_all)
+    w_down_late, _ = barrier(w_down, queries)
+    w_down_all = lax.all_gather(w_down_late, "row", axis=1, tiled=True)
 
     attend, attend_back = attention_calls(seq_blocks, tokens_col, span, head_dim, query_cols)
     core_turned, logs, attn_low = attend(queries, kv_all, b_value[None, :])
     attn_own = lax.all_to_all(attn_low, "row", 0, 1, tiled=True)
     attn_own, w_out_all, fly_cot = barrier(attn_own, w_out_all, fly_cot)
-    w_down_late, _ = barrier(w_down, w_out_all)
-    w_down_all = lax.all_gather(w_down_late, "row", axis=1, tiled=True)
     middle = own + dot_plain(attn_own, w_out_all) + bias_out
 
     normed2, scale2 = norm_forward(middle)
     second_low = (normed2 * gain2 + shift2).astype(BF16)
     fly_second = col_parts(second_low)
     query_strip = jnp.transpose(query_flat, (1, 0, 2)).reshape(features, rows * query_cols)
-    query_strip, _ = barrier(query_strip, w_down_all)
+    query_strip, _ = barrier(query_strip, second_low)
     w_query_all = lax.all_gather(query_strip, "row", axis=0, tiled=True)
     cot_all = col_join(cot_own, fly_cot).reshape(cols * span, width)
-    fly_second, cot_all, w_down_all = barrier(fly_second, cot_all, w_down_all)
+    fly_second, cot_all = barrier(fly_second, cot_all)
     second_all = col_join(second_low, fly_second).reshape(cols * span, width)
+    pre = dot_plain(second_all, w_up_all) + b_up
     grad_hidden = dot_last(cot_all, w_down_all)
-    pre = dot_plain(second_all, w_up_all) + b_up
     gelu_value, gelu_back = jax.vjp(partial(jax.nn.gelu, approximate=True), pre)
     hidden = gelu_value.astype(BF16)
     grad_pre = gelu_back(grad_hidden)[0].astype(BF16)
-    fly_second = col_send(dot_last(grad_pre, w_up_all).reshape(cols, span, width))
+    second_part = dot_last(grad_pre, w_up_all).reshape(cols, span, width).astype(BF16)
+    second_part, hidden, grad_pre = barrier(second_part, hidden, grad_pre)
+    fly_second = col_send(second_part)
+    hidden_late, _ = barrier(hidden, fly_second[1])
+    up_part = dot_first(second_all, grad_pre).astype(BF16)
     down_part = dot_first(hidden, cot_all).astype(BF16)
-    up_part = dot_first(second_all, grad_pre).astype(BF16)
     grad_w_down = lax.psum_scatter(down_part, "row", scatter_dimension=1, tiled=True).astype(F32)
     grad_w_up = lax.psum_scatter(up_part, "row", scatter_dimension=0, tiled=True).astype(F32)
-    fly_second, _, _, w_query_all = barrier(fly_second, down_part, up_part, w_query_all)
+    out_part = dot_plain(hidden_late, w_down_all).astype(BF16)
+    fly_second, _, _, out_part = barrier(fly_second, down_part, up_part, out_part)
+    fly_block = col_send(out_part.reshape(cols, span, width))
 
     grad_in2, gain2_part, shift2_part = norm_backward(add_up(fly_second), normed2, scale2, gain2)
     grad_middle = cot_own.astype(F32) + grad_in2
     mid_low = grad_middle.astype(BF16)
+    late = {}
+
+    def hold(ready):
+        if "grad_attn" in late:
+            ready, late["grad_attn"] = barrier(ready, late["grad_attn"])
+        return list(ready)
+
+    steps_mid = row_gather(mid_low, hold)
+    fly_mid = next(steps_mid)
     grad_attn_own = dot_last(mid_low, w_out_all).astype(BF16)
-    grad_attn = lax.all_to_all(grad_attn_own, "row", 1, 0, tiled=True)
-    steps_mid = row_gather(mid_low)
-    fly_mid = next(steps_mid)
-    late_hidden, _ = barrier(hidden, mid_low)
-    out_part = dot_plain(late_hidden, w_down_all).astype(BF16)
-    grad_attn, fly_mid, out_part = barrier(grad_attn, fly_mid, out_part)
+    fly_mid, grad_attn_own = barrier(fly_mid, grad_attn_own)
+    late["grad_attn"] = lax.all_to_all(grad_attn_own, "row", 1, 0, tiled=True)
     fly_mid = advance(steps_mid, fly_mid)
-    fly_block = col_send(out_part.reshape(cols, span, width))
+    grad_attn = late.pop("grad_attn")
 
     grad_queries, key_mine, key_theirs, value_mine, value_theirs = attend_back(
         queries, grad_attn, core_turned, logs, kv_all
     )
-    grad_queries, key_theirs, value_theirs, fly_mid = barrier(
-        grad_queries, key_theirs, value_theirs, fly_mid
-    )
-
+    grad_queries, key_theirs, value_theirs, fly_mid, fly_block = barrier(
+        grad_queries, key_theirs, value_theirs, fly_mid, fly_block
+    )
+
+    queries_own = lax.all_to_all(grad_queries, "row", 0, 1, tiled=True)
     steps_kv = row_scatter([key_mine, value_mine], [key_theirs, value_theirs])
     fly_kv = next(steps_kv)
-    queries_own = lax.all_to_all(grad_queries, "row", 0, 1, tiled=True)
     fly_mid = advance(steps_mid, fly_mid)
     query_part = dot_first(first_all, grad_queries).astype(BF16)
-    fly_kv, fly_mid, query_part = barrier(fly_kv, fly_mid, query_part)
-    fly_kv = advance(steps_kv, fly_kv)
-    mid_mine, mid_theirs = finish(steps_mid, fly_mid)
+    query_bias = padded(in_parts(jnp.sum(grad_queries.astype(F32), 0), 2), 16)
+    up_bias = in_parts(jnp.sum(grad_pre.astype(F32), 0), 2).reshape(-1, query_cols)
+    up_rows = up_bias.shape[0]
+    extra = jnp.concatenate([query_bias, padded(up_bias, 16)], 0)
+    out_own = (middle + add_up(fly_block) + bias_down).astype(BF16)
     attn_tokens = attn_low.reshape(rows, span, query_cols)
     apart = [2 * k for k in range(rows // 2)]
 
@@ -588,39 +601,32 @@
             0,
         )
 
-    out_part = (
-        dot_first(mid_mine.reshape(-1, width), attn_rows(0))
-        + dot_first(mid_theirs.reshape(-1, width), attn_rows(1))
+    attn_mine, attn_theirs = attn_rows(0), attn_rows(1)
+    fly_kv, fly_mid, queries_own, attn_mine, attn_theirs = barrier(
+        fly_kv, fly_mid, queries_own, attn_mine, attn_theirs
+    )
+    fly_kv = advance(steps_kv, fly_kv)
+    mid_mine, mid_theirs = finish(steps_mid, fly_mid)
+    out_weights = (
+        dot_first(mid_mine.reshape(-1, width), attn_mine)
+        + dot_first(mid_theirs.reshape(-1, width), attn_theirs)
     ).astype(BF16)
-    query_bias = padded(in_parts(jnp.sum(grad_queries.astype(F32), 0), 2), 16)
-    up_bias = in_parts(jnp.sum(grad_pre.astype(F32), 0), 2).reshape(-1, query_cols)
-    up_rows = up_bias.shape[0]
-    extra = jnp.concatenate([query_bias, padded(up_bias, 16)], 0)
-    fly_kv, queries_own, out_part = barrier(fly_kv, queries_own, out_part)
-    fly_kv = advance(steps_kv, fly_kv)
-    first_part = dot_last(queries_own, w_query_all)
-    weights = exchange_rows(
-        jnp.concatenate(
-            [
-                query_part.reshape(rows, features, query_cols),
-                out_part.reshape(rows, features, query_cols),
-                jnp.broadcast_to(extra[None], (rows,) + extra.shape),
-            ],
-            1,
-        )
-    )
-    fly_kv, fly_block, first_part = barrier(fly_kv, fly_block, first_part)
+    pieces = jnp.concatenate(
+        [
+            jnp.transpose(out_own.reshape(span, rows, features), (1, 0, 2)),
+            out_weights.reshape(rows, features, query_cols),
+            query_part.reshape(rows, features, query_cols),
+            jnp.broadcast_to(extra[None], (rows,) + extra.shape),
+        ],
+        1,
+    )
     kv_group = jnp.concatenate(finish(steps_kv, fly_kv), -1)
+
+    pieces, kv_group = barrier(pieces, kv_group)
     fly_kv = col_send(kv_group.reshape(cols, span, -1))
-    out_own = (middle + add_up(fly_block) + bias_down).astype(BF16)
-    fly_kv, weights = barrier(fly_kv, weights)
-
-    both = 2 * features + 16
-    fly_weights = col_send(weights[:, :both].reshape(cols, heads_each, both, query_cols))
-    up_total = total(weights[:, both : both + up_rows]).reshape(2, up_cols)
+    sent = exchange_rows(pieces)
     kv_mine = add_up(fly_kv).astype(BF16)
-    grad_first = first_part + dot_last(kv_mine, w_kv_all)
-    kv_part = dot_first(first_low, kv_mine).astype(BF16)
+    grad_first = dot_last(queries_own, w_query_all) + dot_last(kv_mine, w_kv_all)
     normed1, scale1 = norm_forward(own)
     grad_in1, gain1_part, shift1_part = norm_backward(grad_first, normed1, scale1, gain1)
     feature_parts = jnp.stack(
@@ -634,43 +640,47 @@
         ]
     )
     value_part = jnp.sum(grad_attn_own.astype(F32).reshape(-1, head_dim), 0)
-    value_rows = jnp.broadcast_to(
-        jnp.pad(in_parts(value_part, 2), ((0, 0), (0, features - head_dim)))[None],
-        (rows, 2, features),
-    )
-    feature_rows = jnp.transpose(
-        in_parts(feature_parts, 2).reshape(12, rows, features), (1, 0, 2)
-    )
-    grad_low = jnp.transpose(
-        (grad_middle + grad_in1).astype(BF16).reshape(span, rows, features), (1, 0, 2)
-    )
-    kv_wide = kv_part.reshape(rows, -1, features)
-    kv_rows = kv_wide.shape[1]
-    last = exchange_rows(
+    value_rows = jnp.tile(
+        jnp.pad(in_parts(value_part, 2), ((0, 0), (0, features - head_dim))), (1, rows)
+    )
+    stacked = jnp.concatenate(
+        [
+            (grad_middle + grad_in1).astype(BF16),
+            padded(jnp.concatenate([in_parts(feature_parts, 2).reshape(12, width), value_rows], 0), 16),
+        ],
+        0,
+    )
+    stacked, kv_mine, sent = barrier(stacked, kv_mine, sent)
+    block_output = sent[:, :span].reshape(tokens_col, features)
+    last_row = span + 2 * features + 16
+    fly_weights = col_send(
+        sent[:, span:last_row].reshape(cols, heads_each, 2 * features + 16, query_cols)
+    )
+    up_total = total(sent[:, last_row : last_row + up_rows]).reshape(2, up_cols)
+    last = lax.all_to_all(stacked, "row", 1, 0, tiled=True).reshape(rows, -1, features)
+    steps_kv = row_gather(kv_mine)
+    kv_tokens = in_row_order(jnp.concatenate(finish(steps_kv, next(steps_kv)), 0), 0)
+    first_mine = lax.dynamic_slice_in_dim(first_all, row * features, features, 1)
+    kv_sum = dot_first(kv_tokens, first_mine).reshape(cols, kv_cols, features)
+    last, kv_sum, grad_w_down, grad_w_up = barrier(last, kv_sum, grad_w_down, grad_w_up)
+    grad_inputs = last[:, :span].reshape(tokens_col, features).astype(F32)
+    sums = in_parts(total(last[:, -16:]), 2).reshape(32, features)
+    fly_sums = col_send(
         jnp.concatenate(
-            [
-                grad_low,
-                kv_wide,
-                feature_rows,
-                value_rows,
-                jnp.zeros((rows, 2, features), BF16),
-            ],
-            1,
+            [kv_sum.astype(BF16), jnp.broadcast_to(sums[None], (cols, 32, features))], 1
         )
     )
-    block_output = lax.all_to_all(out_own, "row", 1, 0, tiled=True)
-    grad_inputs = last[:, :span].reshape(tokens_col, features).astype(F32)
-    kv_sum = total(last[:, span : span + kv_rows]).reshape(features, cols, kv_cols)
-    grad_w_keyval = add_up(col_send(jnp.transpose(kv_sum, (1, 0, 2))))
-    sums = total(last[:, span + kv_rows : span + kv_rows + 16])
-    sums = add_up([sums] + col_parts(sums))
+    fly_weights, fly_sums = barrier(fly_weights, fly_sums)
+    sums = add_up(fly_sums)
+    grad_w_keyval = jnp.transpose(sums[:kv_cols])
+    sums = sums[kv_cols : kv_cols + 16] + sums[kv_cols + 16 :]
     by_feature = sums[0:6] + sums[6:12]
     grad_b_value = (sums[12] + sums[13])[:head_dim]
 
     weights = add_up(fly_weights)
-    grad_w_query = jnp.transpose(weights[:, :features], (1, 0, 2)).reshape(features, head_cols)
-    grad_w_out = jnp.transpose(weights[:, features : 2 * features], (0, 2, 1)).reshape(
-        head_cols, features
+    grad_w_out = jnp.transpose(weights[:, :features], (0, 2, 1)).reshape(head_cols, features)
+    grad_w_query = jnp.transpose(weights[:, features : 2 * features], (1, 0, 2)).reshape(
+        features, head_cols
     )
     grad_b_query = (weights[:, 2 * features] + weights[:, 2 * features + 1]).reshape(head_cols)
     return (

time: 671 us -> 607 us (0.905)
  waiting for transfers between devices: 268 us -> 206 us
  matrix products: 76.6 us -> 94.3 us
  starting transfers between devices: 164 us -> 149 us
  other arithmetic: 52.1 us -> 43.1 us
    all_gather x1, waiting for transfers between devices: 64.8 us -> 0.01 us  [body(): w_down_all = lax.all_gather(w_down_late, 'row', axis=1, tiled=True)]
    ppermute x24 -> x18, waiting for transfers between devices: 67.5 us -> 50.5 us  [col_parts(): lax.ppermute(value, 'col', [(i, (i + step) % count) for i in range(count)])]
    ppermute x15, waiting for transfers between devices: 68.4 us -> 54.1 us  [col_send(): lax.ppermute(part, 'col', [(i, (i + step) % count) for i in range(count)])]
    all_to_all x1, waiting for transfers between devices: 0.01 us -> 13.1 us  [body(): attn_own = lax.all_to_all(attn_low, 'row', 0, 1, tiled=True)]
    all_to_all x1, waiting for transfers between devices: 0.01 us -> 9.66 us  [body(): queries_own = lax.all_to_all(grad_queries, 'row', 0, 1, tiled=True)]
    dot_general x5, matrix products: 28.7 us -> 36.7 us  [dot_last(): lax.dot_general(left, right, (((1,), (1,)), ((), ())), preferred_element_...]
    concatenate x2, local copies, waits for them, and re-layouts: 9.27 us -> 1.32 us  [the longest x1 1.3 us: body(): kv_all = jnp.concatenate(finish(steps_kv, fly_kv), 0)]
    ppermute x15, starting transfers between devices: 57.1 us -> 49.7 us  [col_send(): lax.ppermute(part, 'col', [(i, (i + step) % count) for i in range(count)])]
  transfers between devices with their start and end apart: 79 -> 77, of which waited for: 32 -> 34; matrix products, arithmetic and copies ran while one was open for 26% -> 31% of each run, Pallas kernels for 4% -> 5%
where the time goes in v2:
time: 607 us; the launch traced here: 597 us
  waiting for transfers between devices  206 us (34%)
  starting transfers between devices  149 us (25%)
  matrix products  94.3 us (16%)
  local copies, waits for them, and re-layouts  58.8 us (10%)
  other arithmetic  43.1 us (7%)
  Pallas kernels  29 us (5%)
  between operations  16.1 us (3%)
    ppermute x15, waiting for transfers between devices, col_send(): lax.ppermute(part, 'col', [(i, (i + step) % count) for i in range(count)])  54.1 us
    ppermute x18, waiting for transfers between devices, col_parts(): lax.ppermute(value, 'col', [(i, (i + step) % count) for i in range(count)])  50.5 us
    ppermute x15, starting transfers between devices, col_send(): lax.ppermute(part, 'col', [(i, (i + step) % count) for i in range(count)])  49.7 us
    ppermute x31, waiting for transfers between devices, swap(): return lax.ppermute(value, 'row', [(i, i ^ bit) for i in range(count)])  47.1 us
    ppermute x18, starting transfers between devices, col_parts(): lax.ppermute(value, 'col', [(i, (i + step) % count) for i in range(count)])  40.5 us
    dot_general x5, matrix products, dot_last(): lax.dot_general(left, right, (((1,), (1,)), ((), ())), preferred_element_...  36.7 us
    ppermute x31, starting transfers between devices, swap(): return lax.ppermute(value, 'row', [(i, i ^ bit) for i in range(count)])  31.8 us
    dot_general x5, matrix products, dot_plain(): lax.dot_general(left, right, (((1,), (0,)), ((), ())), preferred_element_...  31.7 us
  transfers between devices with their start and end apart: 77, of which 34 were waited for; matrix products, arithmetic and copies ran while one was open for 31% of the time, Pallas kernels for 5%

profile of v2, /device:TPU:0, one launch (start us, length us, event | category | flops | bytes accessed | tf_op | source)
XLA Modules:
  0.0 596.8 jit_solution(12002184944268972700)
XLA Ops:
  28.8 17.0 %collective-permute-done.7 = bf16[1,256,128]{1,2,0:T(8,128)(2,1)S(1)} collective-permute-done((bf16[1,256,128]{1,2,0:T(8,128)(2,1)S(1)}, bf16[1,256,128]{1,2,0:T(8,128)(2,1)S(1)}, u32[]{:S(2)}, u32[]{:S(2)}) %collective-permute-start.7) | collective-permute-done | bytes 65568 | tf_op jit(solution)/shard_map/ppermute | solution.py:67
  78.6 8.1 %norm_gathered.1 = (bf16[1024,2048]{1,0:T(8,128)(2,1)}, bf16[128,2048]{1,0:T(8,128)(2,1)}, f32[8,2048]{1,0:T(8,128)}) custom-call(s32[1]{0:T(128)} %bitcast.me_ref, bf16[4,1056,256]{2,1,0:T(8,128)(2,1)} %copy-done, bf16[4,1056,256]{2,1,0:T(8,128)(2,1)} %collective-permute-done.12.theirs_ref.theirs_vec.theirs_own, bf16[4,1056,256]{2,1,0:T(8,128)(2,1)} %copy-done, ...), custom_call_target="tpu_custom_call" | custom-call | tf_op jit(solution)/shard_map/norm_gathered/pallas_call | solution.py:203
  86.7 9.0 %collective-permute-done.17 = bf16[512,256]{1,0:T(8,128)(2,1)S(1)} collective-permute-done((bf16[512,256]{1,0:T(8,128)(2,1)S(1)}, bf16[512,256]{1,0:T(8,128)(2,1)S(1)}, u32[]{:S(2)}, u32[]{:S(2)}) %collective-permute-start.17) | collective-permute-done | bytes 262176 | tf_op jit(solution)/shard_map/ppermute | solution.py:25
  143.7 10.9 %all-to-all-done.1 = bf16[8,128,256]{2,1,0:T(8,128)(2,1)S(1)} async-done(((bf16[8,128,256]{2,1,0:T(8,128)(2,1)}), bf16[8,128,256]{2,1,0:T(8,128)(2,1)S(1)}, u32[]{:S(2)}, u32[]{:S(2)}) %all-to-all-start.1) | async-done | bytes 524320 | tf_op jit(solution)/shard_map/all_to_all | solution.py:512
  166.1 8.9 %attend_forward.1 = (f32[4,128,512]{2,1,0:T(8,128)}, f32[4,1,512]{2,1,0:T(1,128)}, bf16[1024,256]{1,0:T(8,128)(2,1)}) custom-call(s32[4]{0:T(128)} %select_reduce_fusion.low_ref, s32[4]{0:T(128)} %get-tuple-element.363.high_ref, s32[1]{0:T(128)} %bitcast.me_ref, bf16[1024,256]{1,0:T(8,128)(2,1)} %fusion.9.q_ref, bf16[8,512,256]{2,1,0:T(8,128)(2,1)} %copy-done.2, ...), custom_call_target="tpu_custom_call" | custom-call | tf_op jit(solution)/shard_map/attend_forward/pallas_call | solution.py:362
  183.1 13.1 %all-to-all-done.2 = bf16[8,128,256]{1,2,0:T(8,128)(2,1)S(1)} async-done(((bf16[8,128,256]{1,2,0:T(8,128)(2,1)}), bf16[8,128,256]{1,2,0:T(8,128)(2,1)S(1)}, u32[]{:S(2)}, u32[]{:S(2)}) %all-to-all-start.2) | async-done | bytes 524320 | tf_op jit(solution)/shard_map/all_to_all | solution.py:527
  206.6 11.1 %collective-permute-start.30 = (bf16[128,2048]{1,0:T(8,128)(2,1)}, bf16[128,2048]{1,0:T(8,128)(2,1)S(1)}, u32[]{:S(2)}, u32[]{:S(2)}) collective-permute-start(bf16[128,2048]{1,0:T(8,128)(2,1)} %get-tuple-element.259), channel_id=1, source_target_pairs={{0,1},{1,2},{2,3},{3,0},{4,5},{5,6},{6,7},{7,4},{8,9},{9,10},{10,1... | collective-permute-start | bytes 1572872 | tf_op jit(solution)/shard_map/ppermute | solution.py:25
  224.8 7.0 %collective-permute-done.30 = bf16[128,2048]{1,0:T(8,128)(2,1)S(1)} collective-permute-done((bf16[128,2048]{1,0:T(8,128)(2,1)}, bf16[128,2048]{1,0:T(8,128)(2,1)S(1)}, u32[]{:S(2)}, u32[]{:S(2)}) %collective-permute-start.30) | collective-permute-done | bytes 524320 | tf_op jit(solution)/shard_map/ppermute | solution.py:25
  231.8 18.0 %collective-permute-done.31 = bf16[128,2048]{1,0:T(8,128)(2,1)S(1)} collective-permute-done((bf16[128,2048]{1,0:T(8,128)(2,1)}, bf16[128,2048]{1,0:T(8,128)(2,1)S(1)}, u32[]{:S(2)}, u32[]{:S(2)}) %collective-permute-start.31) | collective-permute-done | bytes 524320 | tf_op jit(solution)/shard_map/ppermute | solution.py:25
  254.4 10.5 %fusion.86 = f32[512,2048]{1,0:T(8,128)} fusion(bf16[512,2048]{1,0:T(8,128)(2,1)} %bitcast.99, bf16[2048,2048]{1,0:T(8,128)(2,1)} %all-gather.5.cloned.1.call-done), kind=kOutput, calls=%fused_computation.340 | convolution fusion | flops 4294967296 | bytes 14680064 | tf_op jit(solution)/shard_map/dot_general | solution.py:238
  264.9 11.7 %multiply_convert_fusion = (bf16[512,2048]{1,0:T(8,128)(2,1)}, bf16[512,2048]{1,0:T(8,128)(2,1)S(1)}) fusion(f32[512,2048]{1,0:T(8,128)} %fusion.86, f32[2048]{0:T(1024)S(1)} %copy-done.52, bf16[512,2048]{1,0:T(8,128)(2,1)} %bitcast.94, bf16[2048,2048]{1,0:T(8,128)(2,1)} %all-gather.9.cloned.1.call-done), kind=kOutput, calls=%fused_computation.12 | convolution fusion | flops 4319084544 | bytes 18882560 | tf_op jit(solution)/shard_map/dot_general | solution.py:230
  276.7 9.9 %convolution_convert_fusion.3 = bf16[512,2048]{1,0:T(8,128)(2,1)} fusion(bf16[512,2048]{1,0:T(8,128)(2,1)S(1)} %get-tuple-element.183, bf16[2048,2048]{1,0:T(8,128)(2,1)} %all-gather.5.cloned.1.call-done), kind=kOutput, calls=%fused_computation.14 | convolution fusion | flops 4296015872 | bytes 12582912 | tf_op jit(solution)/shard_map/dot_general | solution.py:230
  286.5 8.4 %convolution_convert_fusion = bf16[2048,2048]{1,0:T(8,128)(2,1)} fusion(bf16[512,2048]{1,0:T(8,128)(2,1)} %bitcast.99, bf16[512,2048]{1,0:T(8,128)(2,1)S(1)} %get-tuple-element.183), kind=kOutput, calls=%fused_computation | convolution fusion | flops 4299161600 | bytes 12582912 | tf_op jit(solution)/shard_map/dot_general | solution.py:234
  298.0 12.0 %collective-permute-start.33 = (bf16[128,2048]{1,0:T(8,128)(2,1)}, bf16[128,2048]{1,0:T(8,128)(2,1)S(1)}, u32[]{:S(2)}, u32[]{:S(2)}) collective-permute-start(bf16[128,2048]{1,0:T(8,128)(2,1)} %get-tuple-element.272), channel_id=1, source_target_pairs={{0,1},{1,2},{2,3},{3,0},{4,5},{5,6},{6,7},{7,4},{8,9},{9,10},{10,1... | collective-permute-start | bytes 1572872 | tf_op jit(solution)/shard_map/ppermute | solution.py:48
  310.0 8.7 %convolution_convert_fusion.1 = bf16[2048,2048]{1,0:T(8,128)(2,1)} fusion(bf16[512,2048]{1,0:T(8,128)(2,1)S(1)} %copy-done.54, bf16[512,2048]{1,0:T(8,128)(2,1)} %bitcast.94), kind=kOutput, calls=%fused_computation.1 | convolution fusion | flops 4299161600 | bytes 12582912 | tf_op jit(solution)/shard_map/dot_general | solution.py:234
  325.7 9.8 %convolution_convert_fusion.2 = bf16[512,2048]{1,0:T(8,128)(2,1)} fusion(bf16[512,2048]{1,0:T(8,128)(2,1)} %get-tuple-element.184, bf16[2048,2048]{1,0:T(8,128)(2,1)} %all-gather.9.cloned.1.call-done), kind=kOutput, calls=%fused_computation.13 | convolution fusion | flops 4296015872 | bytes 12582912 | tf_op jit(solution)/shard_map/dot_general | solution.py:238
  335.5 11.5 %collective-permute-done.34 = bf16[128,2048]{1,0:T(8,128)(2,1)S(1)} collective-permute-done((bf16[128,2048]{1,0:T(8,128)(2,1)}, bf16[128,2048]{1,0:T(8,128)(2,1)S(1)}, u32[]{:S(2)}, u32[]{:S(2)}) %collective-permute-start.34) | collective-permute-done | bytes 524320 | tf_op jit(solution)/shard_map/ppermute | solution.py:48
  370.0 13.9 %collective-permute-start.40 = (bf16[128,2048]{1,0:T(8,128)(2,1)}, bf16[128,2048]{1,0:T(8,128)(2,1)}, u32[]{:S(2)}, u32[]{:S(2)}) collective-permute-start(bf16[128,2048]{1,0:T(8,128)(2,1)} %get-tuple-element.268), channel_id=1, source_target_pairs={{0,1},{1,2},{2,3},{3,0},{4,5},{5,6},{6,7},{7,4},{8,9},{9,10},{10,1... | collective-permute-start | bytes 1572872 | tf_op jit(solution)/shard_map/ppermute | solution.py:48
  393.6 12.1 %attend_backward.1 = (bf16[1024,256]{1,0:T(8,128)(2,1)}, f32[4,512,128]{2,1,0:T(8,128)}, bf16[4,512,128]{2,1,0:T(8,128)(2,1)}, f32[4,512,128]{2,1,0:T(8,128)}, bf16[4,512,128]{2,1,0:T(8,128)(2,1)}) custom-call(s32[4]{0:T(128)} %select_reduce_fusion.low_ref, s32[4]{0:T(128)} %get-tuple-element.363.high_ref, s32[1]{0:T(128)} %bitcast.me_ref, ...), custom_call_target="tpu_custom_call" | custom-call | tf_op jit(solution)/shard_map/attend_backward/pallas_call | solution.py:384
  405.7 11.4 %collective-permute-done.41 = bf16[128,2048]{1,0:T(8,128)(2,1)} collective-permute-done((bf16[128,2048]{1,0:T(8,128)(2,1)}, bf16[128,2048]{1,0:T(8,128)(2,1)}, u32[]{:S(2)}, u32[]{:S(2)}) %collective-permute-start.41) | collective-permute-done | bytes 524320 | tf_op jit(solution)/shard_map/ppermute | solution.py:48
  436.9 9.7 %all-to-all-done.4 = bf16[8,128,256]{1,2,0:T(8,128)(2,1)S(1)} async-done(((bf16[8,128,256]{1,2,0:T(8,128)(2,1)}), bf16[8,128,256]{1,2,0:T(8,128)(2,1)S(1)}, u32[]{:S(2)}, u32[]{:S(2)}) %all-to-all-start.4) | async-done | bytes 524320 | tf_op jit(solution)/shard_map/all_to_all | solution.py:582
  498.0 20.6 %all-to-all-done.5 = bf16[8,672,256]{2,1,0:T(8,128)(2,1)S(1)} async-done(((bf16[8,672,256]{2,1,0:T(8,128)(2,1)}), bf16[8,672,256]{2,1,0:T(8,128)(2,1)S(1)}, u32[]{:S(2)}, u32[]{:S(2)}) %all-to-all-start.5) | async-done | bytes 2752544 | tf_op jit(solution)/shard_map/all_to_all | solution.py:58
  559.1 11.7 %collective-permute-done.59 = bf16[2,528,256]{2,0,1:T(2,128)(2,1)S(1)} collective-permute-done((bf16[2,528,256]{2,0,1:T(2,128)(2,1)S(1)}, bf16[2,528,256]{2,0,1:T(2,128)(2,1)S(1)}, u32[]{:S(2)}, u32[]{:S(2)}) %collective-permute-start.59) | collective-permute-done | bytes 540704 | tf_op jit(solution)/shard_map/ppermute | solution.py:48
  571.8 13.1 %collective-permute-done.62 = bf16[96,256]{1,0:T(8,128)(2,1)S(1)} collective-permute-done((bf16[96,256]{1,0:T(8,128)(2,1)S(1)}, bf16[96,256]{1,0:T(8,128)(2,1)S(1)}, u32[]{:S(2)}, u32[]{:S(2)}) %collective-permute-start.62) | collective-permute-done | bytes 49184 | tf_op jit(solution)/shard_map/ppermute | solution.py:48
  (492 shorter events, 302.6 us)
Async XLA Ops:
  7.2 151.6 %all-gather.5.cloned.1.call-start = ((), (), s32[]{:S(2)}) async-start(), calls=%async_computation.9 | async-start | bytes 9437184 | tf_op jit(solution)/shard_map/all_gather | solution.py:472
  23.5 32.7 %collective-permute-start.6 = (bf16[2,1056,128]{2,1,0:T(8,128)(2,1)S(1)}, bf16[2,1056,128]{2,1,0:T(8,128)(2,1)S(1)}, u32[]{:S(2)}, u32[]{:S(2)}) collective-permute-start(bf16[2,1056,128]{2,1,0:T(8,128)(2,1)S(1)} %pad_maximum_fusion.6), channel_id=1, source_target_pairs={{0,8},{4,12},{8,0},{12,4},{16,24},{20,28},{24,16},{28,20},{1,9},{5... | collective-permute-start | bytes 1622024 | tf_op jit(solution)/shard_map/ppermute | solution.py:67
  24.2 32.7 %collective-permute-start.5 = (bf16[2,1056,128]{2,1,0:T(8,128)(2,1)S(1)}, bf16[2,1056,128]{2,1,0:T(8,128)(2,1)S(1)}, u32[]{:S(2)}, u32[]{:S(2)}) collective-permute-start(bf16[2,1056,128]{2,1,0:T(8,128)(2,1)S(1)} %pad_maximum_fusion.5), channel_id=1, source_target_pairs={{0,16},{4,20},{8,24},{12,28},{16,0},{20,4},{24,8},{28,12},{1,17},{... | collective-permute-start | bytes 1622024 | tf_op jit(solution)/shard_map/ppermute | solution.py:67
  66.0 29.6 %all-to-all-start = ((bf16[8,256,256]{2,1,0:T(8,128)(2,1)}), bf16[8,256,256]{2,1,0:T(8,128)(2,1)}, u32[]{:S(2)}, u32[]{:S(2)}) async-start(bf16[8,256,256]{2,1,0:T(8,128)(2,1)} %bitcast.47), calls=%async_computation | async-start | bytes 2097152 | tf_op jit(solution)/shard_map/all_to_all | solution.py:58
  70.4 125.9 %all-gather.7.cloned.1.call-start = ((), (), s32[]{:S(2)}) async-start(), calls=%async_computation.10 | async-start | bytes 9437184 | tf_op jit(solution)/shard_map/all_gather | solution.py:503
  138.9 126.0 %all-gather.9.cloned.1.call-start = ((), (), s32[]{:S(2)}) async-start(), calls=%async_computation.11 | async-start | bytes 9437184 | tf_op jit(solution)/shard_map/all_gather | solution.py:523
  160.0 36.2 %collective-permute-start.27 = (bf16[128,2048]{1,0:T(8,128)(2,1)S(1)}, bf16[128,2048]{1,0:T(8,128)(2,1)S(1)}, u32[]{:S(2)}, u32[]{:S(2)}) collective-permute-start(bf16[128,2048]{1,0:T(8,128)(2,1)S(1)} %bitcast.426), channel_id=1, source_target_pairs={{0,1},{1,2},{2,3},{3,0},{4,5},{5,6},{6,7},{7,4},{8,9},{9,10},{10,1... | collective-permute-start | bytes 1572872 | tf_op jit(solution)/shard_map/ppermute | solution.py:25
  161.5 34.7 %collective-permute-start.28 = (bf16[128,2048]{1,0:T(8,128)(2,1)S(1)}, bf16[128,2048]{1,0:T(8,128)(2,1)}, u32[]{:S(2)}, u32[]{:S(2)}) collective-permute-start(bf16[128,2048]{1,0:T(8,128)(2,1)S(1)} %bitcast.427), channel_id=1, source_target_pairs={{0,2},{1,3},{2,0},{3,1},{4,6},{5,7},{6,4},{7,5},{8,10},{9,11},{10,... | collective-permute-start | bytes 1572872 | tf_op jit(solution)/shard_map/ppermute | solution.py:25
  163.9 32.3 %collective-permute-start.29 = (bf16[128,2048]{1,0:T(8,128)(2,1)S(1)}, bf16[128,2048]{1,0:T(8,128)(2,1)}, u32[]{:S(2)}, u32[]{:S(2)}) collective-permute-start(bf16[128,2048]{1,0:T(8,128)(2,1)S(1)} %bitcast.428), channel_id=1, source_target_pairs={{0,3},{1,0},{2,1},{3,2},{4,7},{5,4},{6,5},{7,6},{8,11},{9,8},{10,9... | collective-permute-start | bytes 1572872 | tf_op jit(solution)/shard_map/ppermute | solution.py:25
  180.5 308.0 %all-gather.11.cloned.1.call-start = ((), (), s32[]{:S(2)}) async-start(), calls=%async_computation.12 | async-start | bytes 9437184 | tf_op jit(solution)/shard_map/all_gather | solution.py:536
  204.1 341.9 %reduce-scatter.5.cloned.1.call-start = ((), (), s32[]{:S(2)}) async-start(), calls=%async_computation.14 | async-start | bytes 9437184 | tf_op jit(solution)/shard_map/reduce_scatter | solution.py:552
  217.7 32.1 %collective-permute-start.31 = (bf16[128,2048]{1,0:T(8,128)(2,1)}, bf16[128,2048]{1,0:T(8,128)(2,1)S(1)}, u32[]{:S(2)}, u32[]{:S(2)}) collective-permute-start(bf16[128,2048]{1,0:T(8,128)(2,1)} %get-tuple-element.259), channel_id=1, source_target_pairs={{0,2},{1,3},{2,0},{3,1},{4,6},{5,7},{6,4},{7,5},{8,10},{9,11},{10,... | collective-permute-start | bytes 1572872 | tf_op jit(solution)/shard_map/ppermute | solution.py:25
  219.2 32.7 %collective-permute-start.32 = (bf16[128,2048]{1,0:T(8,128)(2,1)}, bf16[128,2048]{1,0:T(8,128)(2,1)S(1)}, u32[]{:S(2)}, u32[]{:S(2)}) collective-permute-start(bf16[128,2048]{1,0:T(8,128)(2,1)} %get-tuple-element.259), channel_id=1, source_target_pairs={{0,3},{1,0},{2,1},{3,2},{4,7},{5,4},{6,5},{7,6},{8,11},{9,8},{10,9... | collective-permute-start | bytes 1572872 | tf_op jit(solution)/shard_map/ppermute | solution.py:25
  366.9 181.9 %reduce-scatter.3.cloned.1.call-start = ((), (), s32[]{:S(2)}) async-start(), calls=%async_computation.13 | async-start | bytes 9437184 | tf_op jit(solution)/shard_map/reduce_scatter | solution.py:551
  370.0 35.7 %collective-permute-start.40 = (bf16[128,2048]{1,0:T(8,128)(2,1)}, bf16[128,2048]{1,0:T(8,128)(2,1)}, u32[]{:S(2)}, u32[]{:S(2)}) collective-permute-start(bf16[128,2048]{1,0:T(8,128)(2,1)} %get-tuple-element.268), channel_id=1, source_target_pairs={{0,1},{1,2},{2,3},{3,0},{4,5},{5,6},{6,7},{7,4},{8,9},{9,10},{10,1... | collective-permute-start | bytes 1572872 | tf_op jit(solution)/shard_map/ppermute | solution.py:48
  384.0 33.1 %collective-permute-start.41 = (bf16[128,2048]{1,0:T(8,128)(2,1)}, bf16[128,2048]{1,0:T(8,128)(2,1)}, u32[]{:S(2)}, u32[]{:S(2)}) collective-permute-start(bf16[128,2048]{1,0:T(8,128)(2,1)} %get-tuple-element.267), channel_id=1, source_target_pairs={{0,2},{1,3},{2,0},{3,1},{4,6},{5,7},{6,4},{7,5},{8,10},{9,11},{10,... | collective-permute-start | bytes 1572872 | tf_op jit(solution)/shard_map/ppermute | solution.py:48
  384.0 34.6 %collective-permute-start.42 = (bf16[128,2048]{1,0:T(8,128)(2,1)}, bf16[128,2048]{1,0:T(8,128)(2,1)}, u32[]{:S(2)}, u32[]{:S(2)}) collective-permute-start(bf16[128,2048]{1,0:T(8,128)(2,1)} %get-tuple-element.266), channel_id=1, source_target_pairs={{0,3},{1,0},{2,1},{3,2},{4,7},{5,4},{6,5},{7,6},{8,11},{9,8},{10,9... | collective-permute-start | bytes 1572872 | tf_op jit(solution)/shard_map/ppermute | solution.py:48
  388.2 30.4 %collective-permute-start.38 = (bf16[2,128,1024]{2,1,0:T(8,128)(2,1)}, bf16[2,128,1024]{2,1,0:T(8,128)(2,1)}, u32[]{:S(2)}, u32[]{:S(2)}) collective-permute-start(bf16[2,128,1024]{2,1,0:T(8,128)(2,1)} %pad_maximum_fusion.8), channel_id=1, source_target_pairs={{0,16},{4,20},{8,24},{12,28},{16,0},{20,4},{24,8},{28,12},{1,17},{... | collective-permute-start | bytes 1572872 | tf_op jit(solution)/shard_map/ppermute | solution.py:67
  481.4 37.2 %all-to-all-start.5 = ((bf16[8,672,256]{2,1,0:T(8,128)(2,1)}), bf16[8,672,256]{2,1,0:T(8,128)(2,1)S(1)}, u32[]{:S(2)}, u32[]{:S(2)}) async-start(bf16[8,672,256]{2,1,0:T(8,128)(2,1)} %pad_maximum_fusion), calls=%async_computation.5 | async-start | bytes 5505024 | tf_op jit(solution)/shard_map/all_to_all | solution.py:58
  522.9 28.6 %all-to-all-start.6 = ((bf16[144,8,256]{2,0,1:T(8,128)(2,1)}), bf16[144,8,256]{2,0,1:T(8,128)(2,1)}, u32[]{:S(2)}, u32[]{:S(2)}) async-start(bf16[144,8,256]{2,0,1:T(8,128)(2,1)} %bitcast.441), calls=%async_computation.6 | async-start | bytes 1179648 | tf_op jit(solution)/shard_map/all_to_all | solution.py:660
  532.7 38.1 %collective-permute-start.59 = (bf16[2,528,256]{2,0,1:T(2,128)(2,1)S(1)}, bf16[2,528,256]{2,0,1:T(2,128)(2,1)S(1)}, u32[]{:S(2)}, u32[]{:S(2)}) collective-permute-start(bf16[2,528,256]{2,0,1:T(2,128)(2,1)S(1)} %bitcast.482), channel_id=1, source_target_pairs={{0,2},{1,3},{2,0},{3,1},{4,6},{5,7},{6,4},{7,5},{8,10},{9,11},{10,... | collective-permute-start | bytes 1622024 | tf_op jit(solution)/shard_map/ppermute | solution.py:48
  534.0 36.8 %collective-permute-start.60 = (bf16[2,528,256]{2,0,1:T(2,128)(2,1)}, bf16[2,528,256]{2,0,1:T(2,128)(2,1)S(1)}, u32[]{:S(2)}, u32[]{:S(2)}) collective-permute-start(bf16[2,528,256]{2,0,1:T(2,128)(2,1)} %bitcast.412), channel_id=1, source_target_pairs={{0,3},{1,0},{2,1},{3,2},{4,7},{5,4},{6,5},{7,6},{8,11},{9,8},{10,9... | collective-permute-start | bytes 1622024 | tf_op jit(solution)/shard_map/ppermute | solution.py:48
  553.6 31.3 %collective-permute-start.62 = (bf16[96,256]{1,0:T(8,128)(2,1)S(1)}, bf16[96,256]{1,0:T(8,128)(2,1)S(1)}, u32[]{:S(2)}, u32[]{:S(2)}) collective-permute-start(bf16[96,256]{1,0:T(8,128)(2,1)S(1)} %get-tuple-element.313), channel_id=1, source_target_pairs={{0,2},{1,3},{2,0},{3,1},{4,6},{5,7},{6,4},{7,5},{8,10},{9,11},{10,... | collective-permute-start | bytes 147464 | tf_op jit(solution)/shard_map/ppermute | solution.py:48
  556.2 28.7 %collective-permute-start.63 = (bf16[96,256]{1,0:T(8,128)(2,1)S(1)}, bf16[96,256]{1,0:T(8,128)(2,1)S(1)}, u32[]{:S(2)}, u32[]{:S(2)}) collective-permute-start(bf16[96,256]{1,0:T(8,128)(2,1)S(1)} %get-tuple-element.310), channel_id=1, source_target_pairs={{0,3},{1,0},{2,1},{3,2},{4,7},{5,4},{6,5},{7,6},{8,11},{9,8},{10,9... | collective-permute-start | bytes 147464 | tf_op jit(solution)/shard_map/ppermute | solution.py:48
  (108 other events, 1151.2 us)
Sparse Core Ops, SparseCore 0:
  22.5 69.3 all-gather.4
  97.9 71.5 all-gather.6
  171.3 59.7 all-gather.8
  232.8 55.8 all-gather.10
  295.1 89.7 reduce-scatter.4
  393.7 77.7 reduce-scatter.2

commit v3 on v2

--- a/solution.py
+++ b/solution.py
@@ -497,11 +497,8 @@
     mine, theirs = finish(steps_x, fly_x)
     first_all, own_low, vectors = norm_gathered(mine, theirs, tokens_col, span)
     gain1, shift1, bias_out, gain2, shift2, bias_down = (vectors[k : k + 1] for k in range(6))
-    first_all, own_low, fly_kv, w_query_row, fly_out, cot_late = barrier(
-        first_all, own_low, fly_kv, w_query_row, fly_out, cotangent
-    )
-    w_out_all = lax.all_gather(
-        col_join(w_out, fly_out).reshape(cols * head_cols, features), "row", axis=1, tiled=True
+    first_all, own_low, fly_kv, w_query_row, cot_late = barrier(
+        first_all, own_low, fly_kv, w_query_row, cotangent
     )
 
     w_kv_all = in_row_order(jnp.concatenate(finish(steps_kv, fly_kv), 0), 0)
@@ -510,14 +507,17 @@
     kv_own = dot_plain(first_low, w_kv_all).astype(BF16)
     fly_kv = col_parts(kv_own)
     cot_own = lax.all_to_all(cot_late, "row", 0, 1, tiled=True)
-    (fly_kv,) = barrier(fly_kv)
+    fly_kv, fly_out, cot_own = barrier(fly_kv, fly_out, cot_own)
+    w_out_all = lax.all_gather(
+        col_join(w_out, fly_out).reshape(cols * head_cols, features), "row", axis=1, tiled=True
+    )
     steps_kv = row_gather(col_join(kv_own, fly_kv).reshape(cols * span, -1))
     fly_kv = next(steps_kv)
     queries = (dot_plain(first_all, w_query_row.reshape(width, query_cols)) + bias_query).astype(
         BF16
     )
     kv_all = jnp.concatenate(finish(steps_kv, fly_kv), 0)
-    queries, kv_all, cot_own, w_up_all = barrier(queries, kv_all, cot_own, w_up_all)
+    queries, kv_all, w_up_all = barrier(queries, kv_all, w_up_all)
     fly_cot = col_parts(cot_own)
     w_down_late, _ = barrier(w_down, queries)
     w_down_all = lax.all_gather(w_down_late, "row", axis=1, tiled=True)
@@ -588,7 +588,6 @@
     up_bias = in_parts(jnp.sum(grad_pre.astype(F32), 0), 2).reshape(-1, query_cols)
     up_rows = up_bias.shape[0]
     extra = jnp.concatenate([query_bias, padded(up_bias, 16)], 0)
-    out_own = (middle + add_up(fly_block) + bias_down).astype(BF16)
     attn_tokens = attn_low.reshape(rows, span, query_cols)
     apart = [2 * k for k in range(rows // 2)]
 
@@ -605,6 +604,7 @@
     fly_kv, fly_mid, queries_own, attn_mine, attn_theirs = barrier(
         fly_kv, fly_mid, queries_own, attn_mine, attn_theirs
     )
+    out_own = (middle + add_up(fly_block) + bias_down).astype(BF16)
     fly_kv = advance(steps_kv, fly_kv)
     mid_mine, mid_theirs = finish(steps_mid, fly_mid)
     out_weights = (

time: 607 us -> 593 us (0.977)
    all_to_all x1, waiting for transfers between devices: 13.1 us -> 0.01 us  [body(): attn_own = lax.all_to_all(attn_low, 'row', 0, 1, tiled=True)]
    all_to_all x1, waiting for transfers between devices: 10.9 us -> 1.35 us  [body(): cot_own = lax.all_to_all(cot_late, 'row', 0, 1, tiled=True)]
    ppermute x18, waiting for transfers between devices: 50.5 us -> 59.3 us  [col_parts(): lax.ppermute(value, 'col', [(i, (i + step) % count) for i in range(count)])]
    all_to_all x2, waiting for transfers between devices: 20.6 us -> 27.9 us  [exchange_rows(): return lax.all_to_all(pieces.astype(BF16), 'row', 0, 0)]
  transfers between devices with their start and end apart: 77 -> 77, of which waited for: 34 -> 33; matrix products, arithmetic and copies ran while one was open for 31% -> 32% of each run, Pallas kernels for 5% -> 4%
where the time goes in v3:
time: 593 us; the launch traced here: 582 us
  waiting for transfers between devices  200 us (34%)
  starting transfers between devices  144 us (24%)
  matrix products  95.6 us (16%)
  local copies, waits for them, and re-layouts  61.5 us (10%)
  other arithmetic  40.5 us (7%)
  Pallas kernels  24.1 us (4%)
  between operations  16.1 us (3%)
    ppermute x18, waiting for transfers between devices, col_parts(): lax.ppermute(value, 'col', [(i, (i + step) % count) for i in range(count)])  59.3 us
    ppermute x15, waiting for transfers between devices, col_send(): lax.ppermute(part, 'col', [(i, (i + step) % count) for i in range(count)])  54.9 us
    ppermute x31, waiting for transfers between devices, swap(): return lax.ppermute(value, 'row', [(i, i ^ bit) for i in range(count)])  46.4 us
    ppermute x15, starting transfers between devices, col_send(): lax.ppermute(part, 'col', [(i, (i + step) % count) for i in range(count)])  46 us
    ppermute x18, starting transfers between devices, col_parts(): lax.ppermute(value, 'col', [(i, (i + step) % count) for i in range(count)])  37.5 us
    dot_general x5, matrix products, dot_last(): lax.dot_general(left, right, (((1,), (1,)), ((), ())), preferred_element_...  37 us
    ppermute x31, starting transfers between devices, swap(): return lax.ppermute(value, 'row', [(i, i ^ bit) for i in range(count)])  32.8 us
    dot_general x5, matrix products, dot_plain(): lax.dot_general(left, right, (((1,), (0,)), ((), ())), preferred_element_...  32.4 us
  transfers between devices with their start and end apart: 77, of which 33 were waited for; matrix products, arithmetic and copies ran while one was open for 32% of the time, Pallas kernels for 4%

profile of v3, /device:TPU:0, one launch (start us, length us, event | category | flops | bytes accessed | tf_op | source)
XLA Modules:
  0.0 581.8 jit_solution(12125058934081364521)
XLA Ops:
  28.8 17.0 %collective-permute-done.7 = bf16[1,256,128]{1,2,0:T(8,128)(2,1)S(1)} collective-permute-done((bf16[1,256,128]{1,2,0:T(8,128)(2,1)S(1)}, bf16[1,256,128]{1,2,0:T(8,128)(2,1)S(1)}, u32[]{:S(2)}, u32[]{:S(2)}) %collective-permute-start.7) | collective-permute-done | bytes 65568 | tf_op jit(solution)/shard_map/ppermute | solution.py:67
  78.5 8.0 %norm_gathered.1 = (bf16[1024,2048]{1,0:T(8,128)(2,1)}, bf16[128,2048]{1,0:T(8,128)(2,1)}, f32[8,2048]{1,0:T(8,128)}) custom-call(s32[1]{0:T(128)} %bitcast.me_ref, bf16[4,1056,256]{2,1,0:T(8,128)(2,1)} %copy-done, bf16[4,1056,256]{2,1,0:T(8,128)(2,1)} %collective-permute-done.12.theirs_ref.theirs_vec.theirs_own, bf16[4,1056,256]{2,1,0:T(8,128)(2,1)} %copy-done, ...), custom_call_target="tpu_custom_call" | custom-call | tf_op jit(solution)/shard_map/norm_gathered/pallas_call | solution.py:203
  86.5 7.2 %all-to-all-done = bf16[8,256,256]{2,1,0:T(8,128)(2,1)} async-done(((bf16[8,256,256]{2,1,0:T(8,128)(2,1)}), bf16[8,256,256]{2,1,0:T(8,128)(2,1)}, u32[]{:S(2)}, u32[]{:S(2)}) %all-to-all-start) | async-done | bytes 1048608 | tf_op jit(solution)/shard_map/all_to_all | solution.py:58
  122.4 9.5 %collective-permute-done.25 = bf16[2,512,128]{2,1,0:T(8,128)(2,1)S(1)} collective-permute-done((bf16[2,512,128]{2,1,0:T(8,128)(2,1)S(1)}, bf16[2,512,128]{2,1,0:T(8,128)(2,1)S(1)}, u32[]{:S(2)}, u32[]{:S(2)}) %collective-permute-start.25) | collective-permute-done | bytes 262176 | tf_op jit(solution)/shard_map/ppermute | solution.py:67
  147.7 6.6 %attend_forward.1 = (f32[4,128,512]{2,1,0:T(8,128)}, f32[4,1,512]{2,1,0:T(1,128)}, bf16[1024,256]{1,0:T(8,128)(2,1)}) custom-call(s32[4]{0:T(128)} %select_reduce_fusion.low_ref, s32[4]{0:T(128)} %get-tuple-element.363.high_ref, s32[1]{0:T(128)} %bitcast.me_ref, bf16[1024,256]{1,0:T(8,128)(2,1)} %fusion.9.q_ref, bf16[8,512,256]{2,1,0:T(8,128)(2,1)} %copy-done.2, ...), custom_call_target="tpu_custom_call" | custom-call | tf_op jit(solution)/shard_map/attend_forward/pallas_call | solution.py:362
  163.2 17.7 %collective-permute-done.28 = bf16[128,2048]{1,0:T(8,128)(2,1)} collective-permute-done((bf16[128,2048]{1,0:T(8,128)(2,1)S(1)}, bf16[128,2048]{1,0:T(8,128)(2,1)}, u32[]{:S(2)}, u32[]{:S(2)}) %collective-permute-start.28) | collective-permute-done | bytes 524320 | tf_op jit(solution)/shard_map/ppermute | solution.py:25
  191.3 11.7 %collective-permute-start.30 = (bf16[128,2048]{1,0:T(8,128)(2,1)}, bf16[128,2048]{1,0:T(8,128)(2,1)S(1)}, u32[]{:S(2)}, u32[]{:S(2)}) collective-permute-start(bf16[128,2048]{1,0:T(8,128)(2,1)} %get-tuple-element.259), channel_id=1, source_target_pairs={{0,1},{1,2},{2,3},{3,0},{4,5},{5,6},{6,7},{7,4},{8,9},{9,10},{10,1... | collective-permute-start | bytes 1572872 | tf_op jit(solution)/shard_map/ppermute | solution.py:25
  210.1 6.9 %collective-permute-done.30 = bf16[128,2048]{1,0:T(8,128)(2,1)S(1)} collective-permute-done((bf16[128,2048]{1,0:T(8,128)(2,1)}, bf16[128,2048]{1,0:T(8,128)(2,1)S(1)}, u32[]{:S(2)}, u32[]{:S(2)}) %collective-permute-start.30) | collective-permute-done | bytes 524320 | tf_op jit(solution)/shard_map/ppermute | solution.py:25
  216.9 21.7 %collective-permute-done.31 = bf16[128,2048]{1,0:T(8,128)(2,1)S(1)} collective-permute-done((bf16[128,2048]{1,0:T(8,128)(2,1)}, bf16[128,2048]{1,0:T(8,128)(2,1)S(1)}, u32[]{:S(2)}, u32[]{:S(2)}) %collective-permute-start.31) | collective-permute-done | bytes 524320 | tf_op jit(solution)/shard_map/ppermute | solution.py:25
  241.1 11.4 %fusion.86 = f32[512,2048]{1,0:T(8,128)} fusion(bf16[512,2048]{1,0:T(8,128)(2,1)} %bitcast.99, bf16[2048,2048]{1,0:T(8,128)(2,1)} %all-gather.5.cloned.1.call-done), kind=kOutput, calls=%fused_computation.340 | convolution fusion | flops 4294967296 | bytes 14680064 | tf_op jit(solution)/shard_map/dot_general | solution.py:238
  252.5 11.7 %multiply_convert_fusion = (bf16[512,2048]{1,0:T(8,128)(2,1)}, bf16[512,2048]{1,0:T(8,128)(2,1)S(1)}) fusion(f32[512,2048]{1,0:T(8,128)} %fusion.86, f32[2048]{0:T(1024)S(1)} %copy-done.52, bf16[512,2048]{1,0:T(8,128)(2,1)} %bitcast.94, bf16[2048,2048]{1,0:T(8,128)(2,1)} %all-gather.9.cloned.1.call-done), kind=kOutput, calls=%fused_computation.12 | convolution fusion | flops 4319084544 | bytes 18882560 | tf_op jit(solution)/shard_map/dot_general | solution.py:230
  264.2 10.2 %convolution_convert_fusion.3 = bf16[512,2048]{1,0:T(8,128)(2,1)} fusion(bf16[512,2048]{1,0:T(8,128)(2,1)S(1)} %get-tuple-element.183, bf16[2048,2048]{1,0:T(8,128)(2,1)} %all-gather.5.cloned.1.call-done), kind=kOutput, calls=%fused_computation.14 | convolution fusion | flops 4296015872 | bytes 12582912 | tf_op jit(solution)/shard_map/dot_general | solution.py:230
  274.4 8.4 %convolution_convert_fusion = bf16[2048,2048]{1,0:T(8,128)(2,1)} fusion(bf16[512,2048]{1,0:T(8,128)(2,1)} %bitcast.99, bf16[512,2048]{1,0:T(8,128)(2,1)S(1)} %get-tuple-element.183), kind=kOutput, calls=%fused_computation | convolution fusion | flops 4299161600 | bytes 12582912 | tf_op jit(solution)/shard_map/dot_general | solution.py:234
  285.9 11.9 %collective-permute-start.33 = (bf16[128,2048]{1,0:T(8,128)(2,1)}, bf16[128,2048]{1,0:T(8,128)(2,1)S(1)}, u32[]{:S(2)}, u32[]{:S(2)}) collective-permute-start(bf16[128,2048]{1,0:T(8,128)(2,1)} %get-tuple-element.272), channel_id=1, source_target_pairs={{0,1},{1,2},{2,3},{3,0},{4,5},{5,6},{6,7},{7,4},{8,9},{9,10},{10,1... | collective-permute-start | bytes 1572872 | tf_op jit(solution)/shard_map/ppermute | solution.py:48
  297.8 8.6 %convolution_convert_fusion.1 = bf16[2048,2048]{1,0:T(8,128)(2,1)} fusion(bf16[512,2048]{1,0:T(8,128)(2,1)S(1)} %copy-done.54, bf16[512,2048]{1,0:T(8,128)(2,1)} %bitcast.94), kind=kOutput, calls=%fused_computation.1 | convolution fusion | flops 4299161600 | bytes 12582912 | tf_op jit(solution)/shard_map/dot_general | solution.py:234
  310.4 10.1 %convolution_convert_fusion.2 = bf16[512,2048]{1,0:T(8,128)(2,1)} fusion(bf16[512,2048]{1,0:T(8,128)(2,1)} %get-tuple-element.184, bf16[2048,2048]{1,0:T(8,128)(2,1)} %all-gather.9.cloned.1.call-done), kind=kOutput, calls=%fused_computation.13 | convolution fusion | flops 4296015872 | bytes 12582912 | tf_op jit(solution)/shard_map/dot_general | solution.py:238
  320.6 12.5 %collective-permute-done.34 = bf16[128,2048]{1,0:T(8,128)(2,1)S(1)} collective-permute-done((bf16[128,2048]{1,0:T(8,128)(2,1)}, bf16[128,2048]{1,0:T(8,128)(2,1)S(1)}, u32[]{:S(2)}, u32[]{:S(2)}) %collective-permute-start.34) | collective-permute-done | bytes 524320 | tf_op jit(solution)/shard_map/ppermute | solution.py:48
  358.1 10.8 %collective-permute-start.40 = (bf16[128,2048]{1,0:T(8,128)(2,1)}, bf16[128,2048]{1,0:T(8,128)(2,1)}, u32[]{:S(2)}, u32[]{:S(2)}) collective-permute-start(bf16[128,2048]{1,0:T(8,128)(2,1)} %get-tuple-element.268), channel_id=1, source_target_pairs={{0,1},{1,2},{2,3},{3,0},{4,5},{5,6},{6,7},{7,4},{8,9},{9,10},{10,1... | collective-permute-start | bytes 1572872 | tf_op jit(solution)/shard_map/ppermute | solution.py:48
  378.6 9.5 %attend_backward.1 = (bf16[1024,256]{1,0:T(8,128)(2,1)}, f32[4,512,128]{2,1,0:T(8,128)}, bf16[4,512,128]{2,1,0:T(8,128)(2,1)}, f32[4,512,128]{2,1,0:T(8,128)}, bf16[4,512,128]{2,1,0:T(8,128)(2,1)}) custom-call(s32[4]{0:T(128)} %select_reduce_fusion.low_ref, s32[4]{0:T(128)} %get-tuple-element.363.high_ref, s32[1]{0:T(128)} %bitcast.me_ref, ...), custom_call_target="tpu_custom_call" | custom-call | tf_op jit(solution)/shard_map/attend_backward/pallas_call | solution.py:384
  388.2 15.6 %collective-permute-done.41 = bf16[128,2048]{1,0:T(8,128)(2,1)} collective-permute-done((bf16[128,2048]{1,0:T(8,128)(2,1)}, bf16[128,2048]{1,0:T(8,128)(2,1)}, u32[]{:S(2)}, u32[]{:S(2)}) %collective-permute-start.41) | collective-permute-done | bytes 524320 | tf_op jit(solution)/shard_map/ppermute | solution.py:48
  422.1 9.7 %all-to-all-done.4 = bf16[8,128,256]{1,2,0:T(8,128)(2,1)S(1)} async-done(((bf16[8,128,256]{1,2,0:T(8,128)(2,1)}), bf16[8,128,256]{1,2,0:T(8,128)(2,1)S(1)}, u32[]{:S(2)}, u32[]{:S(2)}) %all-to-all-start.4) | async-done | bytes 524320 | tf_op jit(solution)/shard_map/all_to_all | solution.py:582
  482.9 20.7 %all-to-all-done.5 = bf16[8,672,256]{2,1,0:T(8,128)(2,1)S(1)} async-done(((bf16[8,672,256]{2,1,0:T(8,128)(2,1)}), bf16[8,672,256]{2,1,0:T(8,128)(2,1)S(1)}, u32[]{:S(2)}, u32[]{:S(2)}) %all-to-all-start.5) | async-done | bytes 2752544 | tf_op jit(solution)/shard_map/all_to_all | solution.py:58
  544.1 11.7 %collective-permute-done.59 = bf16[2,528,256]{2,0,1:T(2,128)(2,1)S(1)} collective-permute-done((bf16[2,528,256]{2,0,1:T(2,128)(2,1)S(1)}, bf16[2,528,256]{2,0,1:T(2,128)(2,1)S(1)}, u32[]{:S(2)}, u32[]{:S(2)}) %collective-permute-start.59) | collective-permute-done | bytes 540704 | tf_op jit(solution)/shard_map/ppermute | solution.py:48
  556.8 13.1 %collective-permute-done.62 = bf16[96,256]{1,0:T(8,128)(2,1)S(1)} collective-permute-done((bf16[96,256]{1,0:T(8,128)(2,1)S(1)}, bf16[96,256]{1,0:T(8,128)(2,1)S(1)}, u32[]{:S(2)}, u32[]{:S(2)}) %collective-permute-start.62) | collective-permute-done | bytes 49184 | tf_op jit(solution)/shard_map/ppermute | solution.py:48
  (492 shorter events, 283.5 us)
Async XLA Ops:
  7.2 133.7 %all-gather.5.cloned.1.call-start = ((), (), s32[]{:S(2)}) async-start(), calls=%async_computation.9 | async-start | bytes 9437184 | tf_op jit(solution)/shard_map/all_gather | solution.py:472
  23.5 32.7 %collective-permute-start.6 = (bf16[2,1056,128]{2,1,0:T(8,128)(2,1)S(1)}, bf16[2,1056,128]{2,1,0:T(8,128)(2,1)S(1)}, u32[]{:S(2)}, u32[]{:S(2)}) collective-permute-start(bf16[2,1056,128]{2,1,0:T(8,128)(2,1)S(1)} %pad_maximum_fusion.6), channel_id=1, source_target_pairs={{0,8},{4,12},{8,0},{12,4},{16,24},{20,28},{24,16},{28,20},{1,9},{5... | collective-permute-start | bytes 1622024 | tf_op jit(solution)/shard_map/ppermute | solution.py:67
  24.2 32.7 %collective-permute-start.5 = (bf16[2,1056,128]{2,1,0:T(8,128)(2,1)S(1)}, bf16[2,1056,128]{2,1,0:T(8,128)(2,1)S(1)}, u32[]{:S(2)}, u32[]{:S(2)}) collective-permute-start(bf16[2,1056,128]{2,1,0:T(8,128)(2,1)S(1)} %pad_maximum_fusion.5), channel_id=1, source_target_pairs={{0,16},{4,20},{8,24},{12,28},{16,0},{20,4},{24,8},{28,12},{1,17},{... | collective-permute-start | bytes 1622024 | tf_op jit(solution)/shard_map/ppermute | solution.py:67
  74.1 29.9 %collective-permute-start.19 = (bf16[512,256]{1,0:T(8,128)(2,1)S(1)}, bf16[512,256]{1,0:T(8,128)(2,1)S(1)}, u32[]{:S(2)}, u32[]{:S(2)}) collective-permute-start(bf16[512,256]{1,0:T(8,128)(2,1)S(1)} %copy-done.31), channel_id=1, source_target_pairs={{0,1},{1,2},{2,3},{3,0},{4,5},{5,6},{6,7},{7,4},{8,9},{9,10},{10,1... | collective-permute-start | bytes 786440 | tf_op jit(solution)/shard_map/ppermute | solution.py:25
  75.2 31.8 %collective-permute-start.20 = (bf16[512,256]{1,0:T(8,128)(2,1)S(1)}, bf16[512,256]{1,0:T(8,128)(2,1)}, u32[]{:S(2)}, u32[]{:S(2)}) collective-permute-start(bf16[512,256]{1,0:T(8,128)(2,1)S(1)} %copy-done.31), channel_id=1, source_target_pairs={{0,2},{1,3},{2,0},{3,1},{4,6},{5,7},{6,4},{7,5},{8,10},{9,11},{10,... | collective-permute-start | bytes 786440 | tf_op jit(solution)/shard_map/ppermute | solution.py:25
  77.4 29.5 %collective-permute-start.21 = (bf16[512,256]{1,0:T(8,128)(2,1)S(1)}, bf16[512,256]{1,0:T(8,128)(2,1)}, u32[]{:S(2)}, u32[]{:S(2)}) collective-permute-start(bf16[512,256]{1,0:T(8,128)(2,1)S(1)} %copy-done.31), channel_id=1, source_target_pairs={{0,3},{1,0},{2,1},{3,2},{4,7},{5,4},{6,5},{7,6},{8,11},{9,8},{10,9... | collective-permute-start | bytes 786440 | tf_op jit(solution)/shard_map/ppermute | solution.py:25
  97.3 83.7 %all-gather.7.cloned.1.call-start = ((), (), s32[]{:S(2)}) async-start(), calls=%async_computation.10 | async-start | bytes 9437184 | tf_op jit(solution)/shard_map/all_gather | solution.py:511
  113.3 139.2 %all-gather.9.cloned.1.call-start = ((), (), s32[]{:S(2)}) async-start(), calls=%async_computation.11 | async-start | bytes 9437184 | tf_op jit(solution)/shard_map/all_gather | solution.py:523
  144.6 36.3 %collective-permute-start.28 = (bf16[128,2048]{1,0:T(8,128)(2,1)S(1)}, bf16[128,2048]{1,0:T(8,128)(2,1)}, u32[]{:S(2)}, u32[]{:S(2)}) collective-permute-start(bf16[128,2048]{1,0:T(8,128)(2,1)S(1)} %bitcast.427), channel_id=1, source_target_pairs={{0,2},{1,3},{2,0},{3,1},{4,6},{5,7},{6,4},{7,5},{8,10},{9,11},{10,... | collective-permute-start | bytes 1572872 | tf_op jit(solution)/shard_map/ppermute | solution.py:25
  144.7 36.3 %collective-permute-start.29 = (bf16[128,2048]{1,0:T(8,128)(2,1)S(1)}, bf16[128,2048]{1,0:T(8,128)(2,1)}, u32[]{:S(2)}, u32[]{:S(2)}) collective-permute-start(bf16[128,2048]{1,0:T(8,128)(2,1)S(1)} %bitcast.428), channel_id=1, source_target_pairs={{0,3},{1,0},{2,1},{3,2},{4,7},{5,4},{6,5},{7,6},{8,11},{9,8},{10,9... | collective-permute-start | bytes 1572872 | tf_op jit(solution)/shard_map/ppermute | solution.py:25
  160.7 312.7 %all-gather.11.cloned.1.call-start = ((), (), s32[]{:S(2)}) async-start(), calls=%async_computation.12 | async-start | bytes 9437184 | tf_op jit(solution)/shard_map/all_gather | solution.py:536
  188.8 342.2 %reduce-scatter.5.cloned.1.call-start = ((), (), s32[]{:S(2)}) async-start(), calls=%async_computation.14 | async-start | bytes 9437184 | tf_op jit(solution)/shard_map/reduce_scatter | solution.py:552
  203.0 35.6 %collective-permute-start.31 = (bf16[128,2048]{1,0:T(8,128)(2,1)}, bf16[128,2048]{1,0:T(8,128)(2,1)S(1)}, u32[]{:S(2)}, u32[]{:S(2)}) collective-permute-start(bf16[128,2048]{1,0:T(8,128)(2,1)} %get-tuple-element.259), channel_id=1, source_target_pairs={{0,2},{1,3},{2,0},{3,1},{4,6},{5,7},{6,4},{7,5},{8,10},{9,11},{10,... | collective-permute-start | bytes 1572872 | tf_op jit(solution)/shard_map/ppermute | solution.py:25
  204.4 34.3 %collective-permute-start.32 = (bf16[128,2048]{1,0:T(8,128)(2,1)}, bf16[128,2048]{1,0:T(8,128)(2,1)S(1)}, u32[]{:S(2)}, u32[]{:S(2)}) collective-permute-start(bf16[128,2048]{1,0:T(8,128)(2,1)} %get-tuple-element.259), channel_id=1, source_target_pairs={{0,3},{1,0},{2,1},{3,2},{4,7},{5,4},{6,5},{7,6},{8,11},{9,8},{10,9... | collective-permute-start | bytes 1572872 | tf_op jit(solution)/shard_map/ppermute | solution.py:25
  355.0 178.8 %reduce-scatter.3.cloned.1.call-start = ((), (), s32[]{:S(2)}) async-start(), calls=%async_computation.13 | async-start | bytes 9437184 | tf_op jit(solution)/shard_map/reduce_scatter | solution.py:551
  358.1 30.1 %collective-permute-start.40 = (bf16[128,2048]{1,0:T(8,128)(2,1)}, bf16[128,2048]{1,0:T(8,128)(2,1)}, u32[]{:S(2)}, u32[]{:S(2)}) collective-permute-start(bf16[128,2048]{1,0:T(8,128)(2,1)} %get-tuple-element.268), channel_id=1, source_target_pairs={{0,1},{1,2},{2,3},{3,0},{4,5},{5,6},{6,7},{7,4},{8,9},{9,10},{10,1... | collective-permute-start | bytes 1572872 | tf_op jit(solution)/shard_map/ppermute | solution.py:48
  368.9 34.8 %collective-permute-start.41 = (bf16[128,2048]{1,0:T(8,128)(2,1)}, bf16[128,2048]{1,0:T(8,128)(2,1)}, u32[]{:S(2)}, u32[]{:S(2)}) collective-permute-start(bf16[128,2048]{1,0:T(8,128)(2,1)} %get-tuple-element.267), channel_id=1, source_target_pairs={{0,2},{1,3},{2,0},{3,1},{4,6},{5,7},{6,4},{7,5},{8,10},{9,11},{10,... | collective-permute-start | bytes 1572872 | tf_op jit(solution)/shard_map/ppermute | solution.py:48
  369.0 34.8 %collective-permute-start.42 = (bf16[128,2048]{1,0:T(8,128)(2,1)}, bf16[128,2048]{1,0:T(8,128)(2,1)}, u32[]{:S(2)}, u32[]{:S(2)}) collective-permute-start(bf16[128,2048]{1,0:T(8,128)(2,1)} %get-tuple-element.266), channel_id=1, source_target_pairs={{0,3},{1,0},{2,1},{3,2},{4,7},{5,4},{6,5},{7,6},{8,11},{9,8},{10,9... | collective-permute-start | bytes 1572872 | tf_op jit(solution)/shard_map/ppermute | solution.py:48
  373.2 30.6 %collective-permute-start.38 = (bf16[2,128,1024]{2,1,0:T(8,128)(2,1)}, bf16[2,128,1024]{2,1,0:T(8,128)(2,1)}, u32[]{:S(2)}, u32[]{:S(2)}) collective-permute-start(bf16[2,128,1024]{2,1,0:T(8,128)(2,1)} %pad_maximum_fusion.8), channel_id=1, source_target_pairs={{0,16},{4,20},{8,24},{12,28},{16,0},{20,4},{24,8},{28,12},{1,17},{... | collective-permute-start | bytes 1572872 | tf_op jit(solution)/shard_map/ppermute | solution.py:67
  466.3 37.3 %all-to-all-start.5 = ((bf16[8,672,256]{2,1,0:T(8,128)(2,1)}), bf16[8,672,256]{2,1,0:T(8,128)(2,1)S(1)}, u32[]{:S(2)}, u32[]{:S(2)}) async-start(bf16[8,672,256]{2,1,0:T(8,128)(2,1)} %pad_maximum_fusion), calls=%async_computation.5 | async-start | bytes 5505024 | tf_op jit(solution)/shard_map/all_to_all | solution.py:58
  517.7 38.1 %collective-permute-start.59 = (bf16[2,528,256]{2,0,1:T(2,128)(2,1)S(1)}, bf16[2,528,256]{2,0,1:T(2,128)(2,1)S(1)}, u32[]{:S(2)}, u32[]{:S(2)}) collective-permute-start(bf16[2,528,256]{2,0,1:T(2,128)(2,1)S(1)} %bitcast.482), channel_id=1, source_target_pairs={{0,2},{1,3},{2,0},{3,1},{4,6},{5,7},{6,4},{7,5},{8,10},{9,11},{10,... | collective-permute-start | bytes 1622024 | tf_op jit(solution)/shard_map/ppermute | solution.py:48
  519.0 36.8 %collective-permute-start.60 = (bf16[2,528,256]{2,0,1:T(2,128)(2,1)}, bf16[2,528,256]{2,0,1:T(2,128)(2,1)S(1)}, u32[]{:S(2)}, u32[]{:S(2)}) collective-permute-start(bf16[2,528,256]{2,0,1:T(2,128)(2,1)} %bitcast.412), channel_id=1, source_target_pairs={{0,3},{1,0},{2,1},{3,2},{4,7},{5,4},{6,5},{7,6},{8,11},{9,8},{10,9... | collective-permute-start | bytes 1622024 | tf_op jit(solution)/shard_map/ppermute | solution.py:48
  538.6 31.3 %collective-permute-start.62 = (bf16[96,256]{1,0:T(8,128)(2,1)S(1)}, bf16[96,256]{1,0:T(8,128)(2,1)S(1)}, u32[]{:S(2)}, u32[]{:S(2)}) collective-permute-start(bf16[96,256]{1,0:T(8,128)(2,1)S(1)} %get-tuple-element.313), channel_id=1, source_target_pairs={{0,2},{1,3},{2,0},{3,1},{4,6},{5,7},{6,4},{7,5},{8,10},{9,11},{10,... | collective-permute-start | bytes 147464 | tf_op jit(solution)/shard_map/ppermute | solution.py:48
  541.2 28.7 %collective-permute-start.63 = (bf16[96,256]{1,0:T(8,128)(2,1)S(1)}, bf16[96,256]{1,0:T(8,128)(2,1)S(1)}, u32[]{:S(2)}, u32[]{:S(2)}) collective-permute-start(bf16[96,256]{1,0:T(8,128)(2,1)S(1)} %get-tuple-element.310), channel_id=1, source_target_pairs={{0,3},{1,0},{2,1},{3,2},{4,7},{5,4},{6,5},{7,6},{8,11},{9,8},{10,9... | collective-permute-start | bytes 147464 | tf_op jit(solution)/shard_map/ppermute | solution.py:48
  (108 other events, 1118.2 us)
Sparse Core Ops, SparseCore 0:
  22.5 69.3 all-gather.4
  113.5 63.2 all-gather.6
  178.6 55.4 all-gather.8
  235.8 55.8 all-gather.10
  295.0 79.0 reduce-scatter.4
  378.7 77.9 reduce-scatter.2

commit v4 on v3

--- a/solution.py
+++ b/solution.py
@@ -465,11 +465,8 @@
     kv_local = jnp.concatenate([kv_local, padded(bias_local, 16)], 0)
     fly_kv = col_parts(kv_local)
     query_local = jnp.transpose(w_query.reshape(features, heads_each, query_cols), (1, 0, 2))
-    fly_x, fly_kv, query_local, w_up_late, w_out_late = barrier(
-        fly_x, fly_kv, query_local, w_up, w_out
-    )
-
-    w_up_all = lax.all_gather(w_up_late, "row", axis=0, tiled=True)
+    fly_x, fly_kv, query_local, w_out_late = barrier(fly_x, fly_kv, query_local, w_out)
+
     fly_q = col_parts(query_local)
     fly_out = col_parts(w_out_late)
     fly_x = advance(steps_x, fly_x)
@@ -485,8 +482,9 @@
     )
     steps_kv = row_gather(kv_strip)
     fly_kv = next(steps_kv)
-    fly_x, fly_kv, fly_q = barrier(fly_x, fly_kv, fly_q)
-
+    fly_x, fly_kv, fly_q, w_up_late = barrier(fly_x, fly_kv, fly_q, w_up)
+
+    w_up_all = lax.all_gather(w_up_late, "row", axis=0, tiled=True)
     query_flat = col_join(query_local, fly_q).reshape(rows, features, query_cols)
     w_query_row = exchange_rows(query_flat)
     fly_x = advance(steps_x, fly_x)

time: 593 us -> 594 us (level)
  starting transfers between devices: 144 us -> 134 us
  waiting for transfers between devices: 200 us -> 209 us
    ppermute x18, starting transfers between devices: 37.5 us -> 29.1 us  [col_parts(): lax.ppermute(value, 'col', [(i, (i + step) % count) for i in range(count)])]
    all_gather x1, waiting for transfers between devices: 0.01 us -> 8.18 us  [body(): lax.all_gather(col_join(w_out, fly_out).reshape(cols * head_cols, feature...]
    all_to_all x1, waiting for transfers between devices: 1.35 us -> 8.72 us  [body(): cot_own = lax.all_to_all(cot_late, 'row', 0, 1, tiled=True)]
    unnamed x139 -> x141, local copies, waits for them, and re-layouts: 12 us -> 12.9 us
where the time goes in v4:
time: 594 us; the launch traced here: 584 us
  waiting for transfers between devices  209 us (35%)
  starting transfers between devices  134 us (23%)
  matrix products  96.5 us (16%)
  local copies, waits for them, and re-layouts  63.7 us (11%)
  other arithmetic  40.5 us (7%)
  Pallas kernels  23.7 us (4%)
  between operations  16.1 us (3%)
    ppermute x18, waiting for transfers between devices, col_parts(): lax.ppermute(value, 'col', [(i, (i + step) % count) for i in range(count)])  59.9 us
    ppermute x15, waiting for transfers between devices, col_send(): lax.ppermute(part, 'col', [(i, (i + step) % count) for i in range(count)])  56.3 us
    ppermute x15, starting transfers between devices, col_send(): lax.ppermute(part, 'col', [(i, (i + step) % count) for i in range(count)])  50.1 us
    ppermute x31, waiting for transfers between devices, swap(): return lax.ppermute(value, 'row', [(i, i ^ bit) for i in range(count)])  44.2 us
    dot_general x5, matrix products, dot_last(): lax.dot_general(left, right, (((1,), (1,)), ((), ())), preferred_element_...  37.6 us
    dot_general x5, matrix products, dot_plain(): lax.dot_general(left, right, (((1,), (0,)), ((), ())), preferred_element_...  33.2 us
    ppermute x18, starting transfers between devices, col_parts(): lax.ppermute(value, 'col', [(i, (i + step) % count) for i in range(count)])  29.1 us
    ppermute x31, starting transfers between devices, swap(): return lax.ppermute(value, 'row', [(i, i ^ bit) for i in range(count)])  27.7 us
  transfers between devices with their start and end apart: 77, of which 33 were waited for; matrix products, arithmetic and copies ran while one was open for 32% of the time, Pallas kernels for 4%

profile of v4, /device:TPU:0, one launch (start us, length us, event | category | flops | bytes accessed | tf_op | source)
XLA Modules:
  0.0 583.7 jit_solution(15242182331843832551)
XLA Ops:
  28.7 8.8 %collective-permute-done.7 = bf16[1,256,128]{1,2,0:T(8,128)(2,1)S(1)} collective-permute-done((bf16[1,256,128]{1,2,0:T(8,128)(2,1)S(1)}, bf16[1,256,128]{1,2,0:T(8,128)(2,1)S(1)}, u32[]{:S(2)}, u32[]{:S(2)}) %collective-permute-start.7) | collective-permute-done | bytes 65568 | tf_op jit(solution)/shard_map/ppermute | solution.py:67
  40.7 10.4 %collective-permute-done.11 = bf16[2,256,256]{1,2,0:T(8,128)(2,1)S(1)} collective-permute-done((bf16[2,256,256]{1,2,0:T(8,128)(2,1)S(1)}, bf16[2,256,256]{1,2,0:T(8,128)(2,1)S(1)}, u32[]{:S(2)}, u32[]{:S(2)}) %collective-permute-start.11) | collective-permute-done | bytes 262176 | tf_op jit(solution)/shard_map/ppermute | solution.py:25
  76.0 8.0 %norm_gathered.1 = (bf16[1024,2048]{1,0:T(8,128)(2,1)}, bf16[128,2048]{1,0:T(8,128)(2,1)}, f32[8,2048]{1,0:T(8,128)}) custom-call(s32[1]{0:T(128)} %bitcast.me_ref, bf16[4,1056,256]{2,1,0:T(8,128)(2,1)} %copy-done, bf16[4,1056,256]{2,1,0:T(8,128)(2,1)} %collective-permute-done.12.theirs_ref.theirs_vec.theirs_own, bf16[4,1056,256]{2,1,0:T(8,128)(2,1)} %copy-done, ...), custom_call_target="tpu_custom_call" | custom-call | tf_op jit(solution)/shard_map/norm_gathered/pallas_call | solution.py:203
  98.4 8.7 %all-to-all-done.1 = bf16[8,128,256]{2,1,0:T(8,128)(2,1)S(1)} async-done(((bf16[8,128,256]{2,1,0:T(8,128)(2,1)}), bf16[8,128,256]{2,1,0:T(8,128)(2,1)S(1)}, u32[]{:S(2)}, u32[]{:S(2)}) %all-to-all-start.1) | async-done | bytes 524320 | tf_op jit(solution)/shard_map/all_to_all | solution.py:507
  157.5 17.9 %collective-permute-done.28 = bf16[128,2048]{1,0:T(8,128)(2,1)} collective-permute-done((bf16[128,2048]{1,0:T(8,128)(2,1)S(1)}, bf16[128,2048]{1,0:T(8,128)(2,1)}, u32[]{:S(2)}, u32[]{:S(2)}) %collective-permute-start.28) | collective-permute-done | bytes 524320 | tf_op jit(solution)/shard_map/ppermute | solution.py:25
  175.4 8.2 %all-gather.7.cloned.1.call-done = bf16[2048,2048]{1,0:T(8,128)(2,1)} async-done(((bf16[2048,256]{1,0:T(8,128)(2,1)}), bf16[2048,2048]{1,0:T(8,128)(2,1)}) %all-gather.7.cloned.1.call-update) | async-done | bytes 8388624 | tf_op jit(solution)/shard_map/all_gather | solution.py:509
  204.5 7.1 %collective-permute-done.30 = bf16[128,2048]{1,0:T(8,128)(2,1)S(1)} collective-permute-done((bf16[128,2048]{1,0:T(8,128)(2,1)}, bf16[128,2048]{1,0:T(8,128)(2,1)S(1)}, u32[]{:S(2)}, u32[]{:S(2)}) %collective-permute-start.30) | collective-permute-done | bytes 524320 | tf_op jit(solution)/shard_map/ppermute | solution.py:25
  211.6 21.4 %collective-permute-done.31 = bf16[128,2048]{1,0:T(8,128)(2,1)S(1)} collective-permute-done((bf16[128,2048]{1,0:T(8,128)(2,1)}, bf16[128,2048]{1,0:T(8,128)(2,1)S(1)}, u32[]{:S(2)}, u32[]{:S(2)}) %collective-permute-start.31) | collective-permute-done | bytes 524320 | tf_op jit(solution)/shard_map/ppermute | solution.py:25
  235.5 11.1 %fusion.86 = f32[512,2048]{1,0:T(8,128)} fusion(bf16[512,2048]{1,0:T(8,128)(2,1)} %bitcast.99, bf16[2048,2048]{1,0:T(8,128)(2,1)} %all-gather.5.cloned.1.call-done), kind=kOutput, calls=%fused_computation.340 | convolution fusion | flops 4294967296 | bytes 14680064 | tf_op jit(solution)/shard_map/dot_general | solution.py:238
  246.5 12.3 %multiply_convert_fusion = (bf16[512,2048]{1,0:T(8,128)(2,1)}, bf16[512,2048]{1,0:T(8,128)(2,1)S(1)}) fusion(f32[512,2048]{1,0:T(8,128)} %fusion.86, f32[2048]{0:T(1024)S(1)} %copy-done.53, bf16[512,2048]{1,0:T(8,128)(2,1)} %bitcast.94, bf16[2048,2048]{1,0:T(8,128)(2,1)} %all-gather.9.cloned.1.call-done), kind=kOutput, calls=%fused_computation.12 | convolution fusion | flops 4319084544 | bytes 18882560 | tf_op jit(solution)/shard_map/dot_general | solution.py:230
  258.8 9.9 %convolution_convert_fusion.3 = bf16[512,2048]{1,0:T(8,128)(2,1)} fusion(bf16[512,2048]{1,0:T(8,128)(2,1)S(1)} %get-tuple-element.183, bf16[2048,2048]{1,0:T(8,128)(2,1)} %all-gather.5.cloned.1.call-done), kind=kOutput, calls=%fused_computation.14 | convolution fusion | flops 4296015872 | bytes 12582912 | tf_op jit(solution)/shard_map/dot_general | solution.py:230
  268.7 8.7 %convolution_convert_fusion = bf16[2048,2048]{1,0:T(8,128)(2,1)} fusion(bf16[512,2048]{1,0:T(8,128)(2,1)} %bitcast.99, bf16[512,2048]{1,0:T(8,128)(2,1)S(1)} %get-tuple-element.183), kind=kOutput, calls=%fused_computation | convolution fusion | flops 4299161600 | bytes 12582912 | tf_op jit(solution)/shard_map/dot_general | solution.py:234
  280.4 12.1 %collective-permute-start.33 = (bf16[128,2048]{1,0:T(8,128)(2,1)}, bf16[128,2048]{1,0:T(8,128)(2,1)S(1)}, u32[]{:S(2)}, u32[]{:S(2)}) collective-permute-start(bf16[128,2048]{1,0:T(8,128)(2,1)} %get-tuple-element.272), channel_id=1, source_target_pairs={{0,1},{1,2},{2,3},{3,0},{4,5},{5,6},{6,7},{7,4},{8,9},{9,10},{10,1... | collective-permute-start | bytes 1572872 | tf_op jit(solution)/shard_map/ppermute | solution.py:48
  292.5 8.4 %convolution_convert_fusion.1 = bf16[2048,2048]{1,0:T(8,128)(2,1)} fusion(bf16[512,2048]{1,0:T(8,128)(2,1)S(1)} %copy-done.55, bf16[512,2048]{1,0:T(8,128)(2,1)} %bitcast.94), kind=kOutput, calls=%fused_computation.1 | convolution fusion | flops 4299161600 | bytes 12582912 | tf_op jit(solution)/shard_map/dot_general | solution.py:234
  305.2 10.9 %convolution_convert_fusion.2 = bf16[512,2048]{1,0:T(8,128)(2,1)} fusion(bf16[512,2048]{1,0:T(8,128)(2,1)} %get-tuple-element.184, bf16[2048,2048]{1,0:T(8,128)(2,1)} %all-gather.9.cloned.1.call-done), kind=kOutput, calls=%fused_computation.13 | convolution fusion | flops 4296015872 | bytes 12582912 | tf_op jit(solution)/shard_map/dot_general | solution.py:238
  316.1 11.0 %collective-permute-done.34 = bf16[128,2048]{1,0:T(8,128)(2,1)S(1)} collective-permute-done((bf16[128,2048]{1,0:T(8,128)(2,1)}, bf16[128,2048]{1,0:T(8,128)(2,1)S(1)}, u32[]{:S(2)}, u32[]{:S(2)}) %collective-permute-start.34) | collective-permute-done | bytes 524320 | tf_op jit(solution)/shard_map/ppermute | solution.py:48
  353.3 11.6 %collective-permute-start.40 = (bf16[128,2048]{1,0:T(8,128)(2,1)}, bf16[128,2048]{1,0:T(8,128)(2,1)}, u32[]{:S(2)}, u32[]{:S(2)}) collective-permute-start(bf16[128,2048]{1,0:T(8,128)(2,1)} %get-tuple-element.268), channel_id=1, source_target_pairs={{0,1},{1,2},{2,3},{3,0},{4,5},{5,6},{6,7},{7,4},{8,9},{9,10},{10,1... | collective-permute-start | bytes 1572872 | tf_op jit(solution)/shard_map/ppermute | solution.py:48
  374.9 9.2 %attend_backward.1 = (bf16[1024,256]{1,0:T(8,128)(2,1)}, f32[4,512,128]{2,1,0:T(8,128)}, bf16[4,512,128]{2,1,0:T(8,128)(2,1)}, f32[4,512,128]{2,1,0:T(8,128)}, bf16[4,512,128]{2,1,0:T(8,128)(2,1)}) custom-call(s32[4]{0:T(128)} %select_reduce_fusion.low_ref, s32[4]{0:T(128)} %get-tuple-element.363.high_ref, s32[1]{0:T(128)} %bitcast.me_ref, ...), custom_call_target="tpu_custom_call" | custom-call | tf_op jit(solution)/shard_map/attend_backward/pallas_call | solution.py:384
  384.1 18.3 %collective-permute-done.41 = bf16[128,2048]{1,0:T(8,128)(2,1)} collective-permute-done((bf16[128,2048]{1,0:T(8,128)(2,1)}, bf16[128,2048]{1,0:T(8,128)(2,1)}, u32[]{:S(2)}, u32[]{:S(2)}) %collective-permute-start.41) | collective-permute-done | bytes 524320 | tf_op jit(solution)/shard_map/ppermute | solution.py:48
  421.0 7.0 %all-to-all-done.4 = bf16[8,128,256]{1,2,0:T(8,128)(2,1)S(1)} async-done(((bf16[8,128,256]{1,2,0:T(8,128)(2,1)}), bf16[8,128,256]{1,2,0:T(8,128)(2,1)S(1)}, u32[]{:S(2)}, u32[]{:S(2)}) %all-to-all-start.4) | async-done | bytes 524320 | tf_op jit(solution)/shard_map/all_to_all | solution.py:580
  455.9 8.6 %collective-permute-start.50 = (bf16[128,256]{1,0:T(8,128)(2,1)}, bf16[128,256]{1,0:T(8,128)(2,1)S(1)}, u32[]{:S(2)}, u32[]{:S(2)}) collective-permute-start(bf16[128,256]{1,0:T(8,128)(2,1)} %get-tuple-element.301), channel_id=1, source_target_pairs={{0,1},{1,2},{2,3},{3,0},{4,5},{5,6},{6,7},{7,4},{8,9},{9,10},{10,1... | collective-permute-start | bytes 196616 | tf_op jit(solution)/shard_map/ppermute | solution.py:48
  484.8 20.6 %all-to-all-done.5 = bf16[8,672,256]{2,1,0:T(8,128)(2,1)S(1)} async-done(((bf16[8,672,256]{2,1,0:T(8,128)(2,1)}), bf16[8,672,256]{2,1,0:T(8,128)(2,1)S(1)}, u32[]{:S(2)}, u32[]{:S(2)}) %all-to-all-start.5) | async-done | bytes 2752544 | tf_op jit(solution)/shard_map/all_to_all | solution.py:58
  546.1 11.5 %collective-permute-done.59 = bf16[2,528,256]{2,0,1:T(2,128)(2,1)S(1)} collective-permute-done((bf16[2,528,256]{2,0,1:T(2,128)(2,1)S(1)}, bf16[2,528,256]{2,0,1:T(2,128)(2,1)S(1)}, u32[]{:S(2)}, u32[]{:S(2)}) %collective-permute-start.59) | collective-permute-done | bytes 540704 | tf_op jit(solution)/shard_map/ppermute | solution.py:48
  558.7 13.1 %collective-permute-done.62 = bf16[96,256]{1,0:T(8,128)(2,1)S(1)} collective-permute-done((bf16[96,256]{1,0:T(8,128)(2,1)S(1)}, bf16[96,256]{1,0:T(8,128)(2,1)S(1)}, u32[]{:S(2)}, u32[]{:S(2)}) %collective-permute-start.62) | collective-permute-done | bytes 49184 | tf_op jit(solution)/shard_map/ppermute | solution.py:48
  (494 shorter events, 293.1 us)
Async XLA Ops:
  7.2 128.2 %all-gather.5.cloned.1.call-start = ((), (), s32[]{:S(2)}) async-start(), calls=%async_computation.9 | async-start | bytes 9437184 | tf_op jit(solution)/shard_map/all_gather | solution.py:487
  24.1 28.4 %collective-permute-start.5 = (bf16[2,1056,128]{2,1,0:T(8,128)(2,1)S(1)}, bf16[2,1056,128]{2,1,0:T(8,128)(2,1)S(1)}, u32[]{:S(2)}, u32[]{:S(2)}) collective-permute-start(bf16[2,1056,128]{2,1,0:T(8,128)(2,1)S(1)} %pad_maximum_fusion.5), channel_id=1, source_target_pairs={{0,16},{4,20},{8,24},{12,28},{16,0},{20,4},{24,8},{28,12},{1,17},{... | collective-permute-start | bytes 1622024 | tf_op jit(solution)/shard_map/ppermute | solution.py:67
  71.7 35.4 %collective-permute-start.20 = (bf16[512,256]{1,0:T(8,128)(2,1)S(1)}, bf16[512,256]{1,0:T(8,128)(2,1)}, u32[]{:S(2)}, u32[]{:S(2)}) collective-permute-start(bf16[512,256]{1,0:T(8,128)(2,1)S(1)} %copy-done.32), channel_id=1, source_target_pairs={{0,2},{1,3},{2,0},{3,1},{4,6},{5,7},{6,4},{7,5},{8,10},{9,11},{10,... | collective-permute-start | bytes 786440 | tf_op jit(solution)/shard_map/ppermute | solution.py:25
  74.5 32.6 %collective-permute-start.21 = (bf16[512,256]{1,0:T(8,128)(2,1)S(1)}, bf16[512,256]{1,0:T(8,128)(2,1)}, u32[]{:S(2)}, u32[]{:S(2)}) collective-permute-start(bf16[512,256]{1,0:T(8,128)(2,1)S(1)} %copy-done.32), channel_id=1, source_target_pairs={{0,3},{1,0},{2,1},{3,2},{4,7},{5,4},{6,5},{7,6},{8,11},{9,8},{10,9... | collective-permute-start | bytes 786440 | tf_op jit(solution)/shard_map/ppermute | solution.py:25
  91.4 92.2 %all-gather.7.cloned.1.call-start = ((), (), s32[]{:S(2)}) async-start(), calls=%async_computation.10 | async-start | bytes 9437184 | tf_op jit(solution)/shard_map/all_gather | solution.py:509
  111.2 135.4 %all-gather.9.cloned.1.call-start = ((), (), s32[]{:S(2)}) async-start(), calls=%async_computation.11 | async-start | bytes 9437184 | tf_op jit(solution)/shard_map/all_gather | solution.py:521
  138.2 37.2 %collective-permute-start.28 = (bf16[128,2048]{1,0:T(8,128)(2,1)S(1)}, bf16[128,2048]{1,0:T(8,128)(2,1)}, u32[]{:S(2)}, u32[]{:S(2)}) collective-permute-start(bf16[128,2048]{1,0:T(8,128)(2,1)S(1)} %bitcast.427), channel_id=1, source_target_pairs={{0,2},{1,3},{2,0},{3,1},{4,6},{5,7},{6,4},{7,5},{8,10},{9,11},{10,... | collective-permute-start | bytes 1572872 | tf_op jit(solution)/shard_map/ppermute | solution.py:25
  140.6 34.8 %collective-permute-start.29 = (bf16[128,2048]{1,0:T(8,128)(2,1)S(1)}, bf16[128,2048]{1,0:T(8,128)(2,1)}, u32[]{:S(2)}, u32[]{:S(2)}) collective-permute-start(bf16[128,2048]{1,0:T(8,128)(2,1)S(1)} %bitcast.428), channel_id=1, source_target_pairs={{0,3},{1,0},{2,1},{3,2},{4,7},{5,4},{6,5},{7,6},{8,11},{9,8},{10,9... | collective-permute-start | bytes 1572872 | tf_op jit(solution)/shard_map/ppermute | solution.py:25
  155.0 320.3 %all-gather.11.cloned.1.call-start = ((), (), s32[]{:S(2)}) async-start(), calls=%async_computation.12 | async-start | bytes 9437184 | tf_op jit(solution)/shard_map/all_gather | solution.py:534
  191.4 342.2 %reduce-scatter.5.cloned.1.call-start = ((), (), s32[]{:S(2)}) async-start(), calls=%async_computation.14 | async-start | bytes 9437184 | tf_op jit(solution)/shard_map/reduce_scatter | solution.py:550
  197.5 35.5 %collective-permute-start.31 = (bf16[128,2048]{1,0:T(8,128)(2,1)}, bf16[128,2048]{1,0:T(8,128)(2,1)S(1)}, u32[]{:S(2)}, u32[]{:S(2)}) collective-permute-start(bf16[128,2048]{1,0:T(8,128)(2,1)} %get-tuple-element.259), channel_id=1, source_target_pairs={{0,2},{1,3},{2,0},{3,1},{4,6},{5,7},{6,4},{7,5},{8,10},{9,11},{10,... | collective-permute-start | bytes 1572872 | tf_op jit(solution)/shard_map/ppermute | solution.py:25
  199.1 33.9 %collective-permute-start.32 = (bf16[128,2048]{1,0:T(8,128)(2,1)}, bf16[128,2048]{1,0:T(8,128)(2,1)S(1)}, u32[]{:S(2)}, u32[]{:S(2)}) collective-permute-start(bf16[128,2048]{1,0:T(8,128)(2,1)} %get-tuple-element.259), channel_id=1, source_target_pairs={{0,3},{1,0},{2,1},{3,2},{4,7},{5,4},{6,5},{7,6},{8,11},{9,8},{10,9... | collective-permute-start | bytes 1572872 | tf_op jit(solution)/shard_map/ppermute | solution.py:25
  350.2 186.2 %reduce-scatter.3.cloned.1.call-start = ((), (), s32[]{:S(2)}) async-start(), calls=%async_computation.13 | async-start | bytes 9437184 | tf_op jit(solution)/shard_map/reduce_scatter | solution.py:549
  353.3 30.8 %collective-permute-start.40 = (bf16[128,2048]{1,0:T(8,128)(2,1)}, bf16[128,2048]{1,0:T(8,128)(2,1)}, u32[]{:S(2)}, u32[]{:S(2)}) collective-permute-start(bf16[128,2048]{1,0:T(8,128)(2,1)} %get-tuple-element.268), channel_id=1, source_target_pairs={{0,1},{1,2},{2,3},{3,0},{4,5},{5,6},{6,7},{7,4},{8,9},{9,10},{10,1... | collective-permute-start | bytes 1572872 | tf_op jit(solution)/shard_map/ppermute | solution.py:48
  364.9 37.5 %collective-permute-start.41 = (bf16[128,2048]{1,0:T(8,128)(2,1)}, bf16[128,2048]{1,0:T(8,128)(2,1)}, u32[]{:S(2)}, u32[]{:S(2)}) collective-permute-start(bf16[128,2048]{1,0:T(8,128)(2,1)} %get-tuple-element.267), channel_id=1, source_target_pairs={{0,2},{1,3},{2,0},{3,1},{4,6},{5,7},{6,4},{7,5},{8,10},{9,11},{10,... | collective-permute-start | bytes 1572872 | tf_op jit(solution)/shard_map/ppermute | solution.py:48
  367.6 34.8 %collective-permute-start.42 = (bf16[128,2048]{1,0:T(8,128)(2,1)}, bf16[128,2048]{1,0:T(8,128)(2,1)}, u32[]{:S(2)}, u32[]{:S(2)}) collective-permute-start(bf16[128,2048]{1,0:T(8,128)(2,1)} %get-tuple-element.266), channel_id=1, source_target_pairs={{0,3},{1,0},{2,1},{3,2},{4,7},{5,4},{6,5},{7,6},{8,11},{9,8},{10,9... | collective-permute-start | bytes 1572872 | tf_op jit(solution)/shard_map/ppermute | solution.py:48
  369.4 32.9 %collective-permute-start.38 = (bf16[2,128,1024]{2,1,0:T(8,128)(2,1)}, bf16[2,128,1024]{2,1,0:T(8,128)(2,1)}, u32[]{:S(2)}, u32[]{:S(2)}) collective-permute-start(bf16[2,128,1024]{2,1,0:T(8,128)(2,1)} %pad_maximum_fusion.8), channel_id=1, source_target_pairs={{0,16},{4,20},{8,24},{12,28},{16,0},{20,4},{24,8},{28,12},{1,17},{... | collective-permute-start | bytes 1572872 | tf_op jit(solution)/shard_map/ppermute | solution.py:67
  371.3 31.0 %collective-permute-start.39 = (bf16[2,128,1024]{2,1,0:T(8,128)(2,1)}, bf16[2,128,1024]{2,1,0:T(8,128)(2,1)}, u32[]{:S(2)}, u32[]{:S(2)}) collective-permute-start(bf16[2,128,1024]{2,1,0:T(8,128)(2,1)} %pad_maximum_fusion.9), channel_id=1, source_target_pairs={{0,8},{4,12},{8,0},{12,4},{16,24},{20,28},{24,16},{28,20},{1,9},{5... | collective-permute-start | bytes 1572872 | tf_op jit(solution)/shard_map/ppermute | solution.py:67
  468.0 37.5 %all-to-all-start.5 = ((bf16[8,672,256]{2,1,0:T(8,128)(2,1)}), bf16[8,672,256]{2,1,0:T(8,128)(2,1)S(1)}, u32[]{:S(2)}, u32[]{:S(2)}) async-start(bf16[8,672,256]{2,1,0:T(8,128)(2,1)} %pad_maximum_fusion), calls=%async_computation.5 | async-start | bytes 5505024 | tf_op jit(solution)/shard_map/all_to_all | solution.py:58
  509.8 29.4 %all-to-all-start.6 = ((bf16[144,8,256]{2,0,1:T(8,128)(2,1)}), bf16[144,8,256]{2,0,1:T(8,128)(2,1)}, u32[]{:S(2)}, u32[]{:S(2)}) async-start(bf16[144,8,256]{2,0,1:T(8,128)(2,1)} %bitcast.441), calls=%async_computation.6 | async-start | bytes 1179648 | tf_op jit(solution)/shard_map/all_to_all | solution.py:658
  518.9 38.8 %collective-permute-start.59 = (bf16[2,528,256]{2,0,1:T(2,128)(2,1)S(1)}, bf16[2,528,256]{2,0,1:T(2,128)(2,1)S(1)}, u32[]{:S(2)}, u32[]{:S(2)}) collective-permute-start(bf16[2,528,256]{2,0,1:T(2,128)(2,1)S(1)} %bitcast.482), channel_id=1, source_target_pairs={{0,2},{1,3},{2,0},{3,1},{4,6},{5,7},{6,4},{7,5},{8,10},{9,11},{10,... | collective-permute-start | bytes 1622024 | tf_op jit(solution)/shard_map/ppermute | solution.py:48
  522.5 35.1 %collective-permute-start.60 = (bf16[2,528,256]{2,0,1:T(2,128)(2,1)}, bf16[2,528,256]{2,0,1:T(2,128)(2,1)S(1)}, u32[]{:S(2)}, u32[]{:S(2)}) collective-permute-start(bf16[2,528,256]{2,0,1:T(2,128)(2,1)} %bitcast.412), channel_id=1, source_target_pairs={{0,3},{1,0},{2,1},{3,2},{4,7},{5,4},{6,5},{7,6},{8,11},{9,8},{10,9... | collective-permute-start | bytes 1622024 | tf_op jit(solution)/shard_map/ppermute | solution.py:48
  541.8 30.0 %collective-permute-start.62 = (bf16[96,256]{1,0:T(8,128)(2,1)S(1)}, bf16[96,256]{1,0:T(8,128)(2,1)S(1)}, u32[]{:S(2)}, u32[]{:S(2)}) collective-permute-start(bf16[96,256]{1,0:T(8,128)(2,1)S(1)} %get-tuple-element.313), channel_id=1, source_target_pairs={{0,2},{1,3},{2,0},{3,1},{4,6},{5,7},{6,4},{7,5},{8,10},{9,11},{10,... | collective-permute-start | bytes 147464 | tf_op jit(solution)/shard_map/ppermute | solution.py:48
  542.3 29.5 %collective-permute-start.63 = (bf16[96,256]{1,0:T(8,128)(2,1)S(1)}, bf16[96,256]{1,0:T(8,128)(2,1)S(1)}, u32[]{:S(2)}, u32[]{:S(2)}) collective-permute-start(bf16[96,256]{1,0:T(8,128)(2,1)S(1)} %get-tuple-element.310), channel_id=1, source_target_pairs={{0,3},{1,0},{2,1},{3,2},{4,7},{5,4},{6,5},{7,6},{8,11},{9,8},{10,9... | collective-permute-start | bytes 147464 | tf_op jit(solution)/shard_map/ppermute | solution.py:48
  (109 other events, 1142.0 us)
Sparse Core Ops, SparseCore 0:
  52.7 67.3 all-gather.4
  121.9 61.6 all-gather.6
  185.5 54.9 all-gather.8
  242.2 55.8 all-gather.10
  301.4 87.6 reduce-scatter.4
  392.3 83.9 reduce-scatter.2

commit v5 on v4

--- a/solution.py
+++ b/solution.py
@@ -549,7 +549,8 @@
     grad_w_down = lax.psum_scatter(down_part, "row", scatter_dimension=1, tiled=True).astype(F32)
     grad_w_up = lax.psum_scatter(up_part, "row", scatter_dimension=0, tiled=True).astype(F32)
     out_part = dot_plain(hidden_late, w_down_all).astype(BF16)
-    fly_second, _, _, out_part = barrier(fly_second, down_part, up_part, out_part)
+    up_sum = jnp.sum(grad_pre.astype(F32), 0)
+    fly_second, _, _, out_part, up_sum = barrier(fly_second, down_part, up_part, out_part, up_sum)
     fly_block = col_send(out_part.reshape(cols, span, width))
 
     grad_in2, gain2_part, shift2_part = norm_backward(add_up(fly_second), normed2, scale2, gain2)
@@ -583,7 +584,7 @@
     fly_mid = advance(steps_mid, fly_mid)
     query_part = dot_first(first_all, grad_queries).astype(BF16)
     query_bias = padded(in_parts(jnp.sum(grad_queries.astype(F32), 0), 2), 16)
-    up_bias = in_parts(jnp.sum(grad_pre.astype(F32), 0), 2).reshape(-1, query_cols)
+    up_bias = in_parts(up_sum, 2).reshape(-1, query_cols)
     up_rows = up_bias.shape[0]
     extra = jnp.concatenate([query_bias, padded(up_bias, 16)], 0)
     attn_tokens = attn_low.reshape(rows, span, query_cols)
@@ -620,7 +621,7 @@
     )
     kv_group = jnp.concatenate(finish(steps_kv, fly_kv), -1)
 
-    pieces, kv_group = barrier(pieces, kv_group)
+    pieces, kv_group, grad_attn_own = barrier(pieces, kv_group, grad_attn_own)
     fly_kv = col_send(kv_group.reshape(cols, span, -1))
     sent = exchange_rows(pieces)
     kv_mine = add_up(fly_kv).astype(BF16)

time: 594 us -> 612 us (1.030)
  starting transfers between devices: 134 us -> 148 us
    ppermute x15, starting transfers between devices: 50.1 us -> 65.4 us  [col_send(): lax.ppermute(part, 'col', [(i, (i + step) % count) for i in range(count)])]
    all_to_all x2, waiting for transfers between devices: 24.5 us -> 32.7 us  [exchange_rows(): return lax.all_to_all(pieces.astype(BF16), 'row', 0, 0)]
    unnamed x141 -> x139, local copies, waits for them, and re-layouts: 12.9 us -> 13.4 us
  transfers between devices with their start and end apart: 77 -> 77, of which waited for: 33 -> 31; matrix products, arithmetic and copies ran while one was open for 32% -> 31% of each run, Pallas kernels for 4% -> 4%
where the time goes in v5:
time: 612 us; the launch traced here: 602 us
  waiting for transfers between devices  211 us (34%)
  starting transfers between devices  148 us (24%)
  matrix products  95.2 us (16%)
  local copies, waits for them, and re-layouts  67.1 us (11%)
  other arithmetic  40.7 us (7%)
  Pallas kernels  23.6 us (4%)
  between operations  16.3 us (3%)
    ppermute x15, starting transfers between devices, col_send(): lax.ppermute(part, 'col', [(i, (i + step) % count) for i in range(count)])  65.4 us
    ppermute x18, waiting for transfers between devices, col_parts(): lax.ppermute(value, 'col', [(i, (i + step) % count) for i in range(count)])  60.6 us
    ppermute x15, waiting for transfers between devices, col_send(): lax.ppermute(part, 'col', [(i, (i + step) % count) for i in range(count)])  53.4 us
    ppermute x31, waiting for transfers between devices, swap(): return lax.ppermute(value, 'row', [(i, i ^ bit) for i in range(count)])  39.6 us
    dot_general x5, matrix products, dot_last(): lax.dot_general(left, right, (((1,), (1,)), ((), ())), preferred_element_...  36.8 us
    all_to_all x2, waiting for transfers between devices, exchange_rows(): return lax.all_to_all(pieces.astype(BF16), 'row', 0, 0)  32.7 us
    dot_general x5, matrix products, dot_plain(): lax.dot_general(left, right, (((1,), (0,)), ((), ())), preferred_element_...  32.1 us
    ppermute x18, starting transfers between devices, col_parts(): lax.ppermute(value, 'col', [(i, (i + step) % count) for i in range(count)])  28.6 us
  transfers between devices with their start and end apart: 77, of which 31 were waited for; matrix products, arithmetic and copies ran while one was open for 31% of the time, Pallas kernels for 4%

profile of v5, /device:TPU:0, one launch (start us, length us, event | category | flops | bytes accessed | tf_op | source)
XLA Modules:
  0.0 602.5 jit_solution(3532247894157032457)
XLA Ops:
  28.7 8.8 %collective-permute-done.7 = bf16[1,256,128]{1,2,0:T(8,128)(2,1)S(1)} collective-permute-done((bf16[1,256,128]{1,2,0:T(8,128)(2,1)S(1)}, bf16[1,256,128]{1,2,0:T(8,128)(2,1)S(1)}, u32[]{:S(2)}, u32[]{:S(2)}) %collective-permute-start.7) | collective-permute-done | bytes 65568 | tf_op jit(solution)/shard_map/ppermute | solution.py:67
  40.7 10.4 %collective-permute-done.11 = bf16[2,256,256]{1,2,0:T(8,128)(2,1)S(1)} collective-permute-done((bf16[2,256,256]{1,2,0:T(8,128)(2,1)S(1)}, bf16[2,256,256]{1,2,0:T(8,128)(2,1)S(1)}, u32[]{:S(2)}, u32[]{:S(2)}) %collective-permute-start.11) | collective-permute-done | bytes 262176 | tf_op jit(solution)/shard_map/ppermute | solution.py:25
  76.0 7.9 %norm_gathered.1 = (bf16[1024,2048]{1,0:T(8,128)(2,1)}, bf16[128,2048]{1,0:T(8,128)(2,1)}, f32[8,2048]{1,0:T(8,128)}) custom-call(s32[1]{0:T(128)} %bitcast.me_ref, bf16[4,1056,256]{2,1,0:T(8,128)(2,1)} %copy-done, bf16[4,1056,256]{2,1,0:T(8,128)(2,1)} %collective-permute-done.12.theirs_ref.theirs_vec.theirs_own, bf16[4,1056,256]{2,1,0:T(8,128)(2,1)} %copy-done, ...), custom_call_target="tpu_custom_call" | custom-call | tf_op jit(solution)/shard_map/norm_gathered/pallas_call | solution.py:203
  97.8 8.4 %all-to-all-done.1 = bf16[8,128,256]{2,1,0:T(8,128)(2,1)S(1)} async-done(((bf16[8,128,256]{2,1,0:T(8,128)(2,1)}), bf16[8,128,256]{2,1,0:T(8,128)(2,1)S(1)}, u32[]{:S(2)}, u32[]{:S(2)}) %all-to-all-start.1) | async-done | bytes 524320 | tf_op jit(solution)/shard_map/all_to_all | solution.py:507
  111.7 6.6 %collective-permute-done.22 = bf16[1,512,128]{2,1,0:T(8,128)(2,1)S(1)} collective-permute-done((bf16[1,512,128]{2,1,0:T(8,128)(2,1)S(1)}, bf16[1,512,128]{2,1,0:T(8,128)(2,1)S(1)}, u32[]{:S(2)}, u32[]{:S(2)}) %collective-permute-start.22) | collective-permute-done | bytes 131104 | tf_op jit(solution)/shard_map/ppermute | solution.py:67
  121.4 8.7 %collective-permute-done.25 = bf16[2,512,128]{2,1,0:T(8,128)(2,1)S(1)} collective-permute-done((bf16[2,512,128]{2,1,0:T(8,128)(2,1)S(1)}, bf16[2,512,128]{2,1,0:T(8,128)(2,1)S(1)}, u32[]{:S(2)}, u32[]{:S(2)}) %collective-permute-start.25) | collective-permute-done | bytes 262176 | tf_op jit(solution)/shard_map/ppermute | solution.py:67
  160.4 18.6 %collective-permute-done.28 = bf16[128,2048]{1,0:T(8,128)(2,1)} collective-permute-done((bf16[128,2048]{1,0:T(8,128)(2,1)S(1)}, bf16[128,2048]{1,0:T(8,128)(2,1)}, u32[]{:S(2)}, u32[]{:S(2)}) %collective-permute-start.28) | collective-permute-done | bytes 524320 | tf_op jit(solution)/shard_map/ppermute | solution.py:25
  179.0 13.0 %all-gather.7.cloned.1.call-done = bf16[2048,2048]{1,0:T(8,128)(2,1)} async-done(((bf16[2048,256]{1,0:T(8,128)(2,1)}), bf16[2048,2048]{1,0:T(8,128)(2,1)}) %all-gather.7.cloned.1.call-update) | async-done | bytes 8388624 | tf_op jit(solution)/shard_map/all_gather | solution.py:509
  220.1 22.0 %collective-permute-done.31 = bf16[128,2048]{1,0:T(8,128)(2,1)S(1)} collective-permute-done((bf16[128,2048]{1,0:T(8,128)(2,1)}, bf16[128,2048]{1,0:T(8,128)(2,1)S(1)}, u32[]{:S(2)}, u32[]{:S(2)}) %collective-permute-start.31) | collective-permute-done | bytes 524320 | tf_op jit(solution)/shard_map/ppermute | solution.py:25
  244.6 10.5 %fusion.86 = f32[512,2048]{1,0:T(8,128)} fusion(bf16[512,2048]{1,0:T(8,128)(2,1)} %bitcast.99, bf16[2048,2048]{1,0:T(8,128)(2,1)} %all-gather.5.cloned.1.call-done), kind=kOutput, calls=%fused_computation.340 | convolution fusion | flops 4294967296 | bytes 14680064 | tf_op jit(solution)/shard_map/dot_general | solution.py:238
  255.1 11.7 %multiply_convert_fusion = (bf16[512,2048]{1,0:T(8,128)(2,1)}, bf16[512,2048]{1,0:T(8,128)(2,1)S(1)}) fusion(f32[512,2048]{1,0:T(8,128)} %fusion.86, f32[2048]{0:T(1024)S(1)} %copy-done.51, bf16[512,2048]{1,0:T(8,128)(2,1)} %bitcast.94, bf16[2048,2048]{1,0:T(8,128)(2,1)} %all-gather.9.cloned.1.call-done), kind=kOutput, calls=%fused_computation.12 | convolution fusion | flops 4319084544 | bytes 18882560 | tf_op jit(solution)/shard_map/dot_general | solution.py:230
  266.9 9.9 %convolution_convert_fusion.3 = bf16[512,2048]{1,0:T(8,128)(2,1)} fusion(bf16[512,2048]{1,0:T(8,128)(2,1)S(1)} %get-tuple-element.185, bf16[2048,2048]{1,0:T(8,128)(2,1)} %all-gather.5.cloned.1.call-done), kind=kOutput, calls=%fused_computation.14 | convolution fusion | flops 4296015872 | bytes 12582912 | tf_op jit(solution)/shard_map/dot_general | solution.py:230
  276.7 8.4 %convolution_convert_fusion = bf16[2048,2048]{1,0:T(8,128)(2,1)} fusion(bf16[512,2048]{1,0:T(8,128)(2,1)} %bitcast.99, bf16[512,2048]{1,0:T(8,128)(2,1)S(1)} %get-tuple-element.185), kind=kOutput, calls=%fused_computation | convolution fusion | flops 4299161600 | bytes 12582912 | tf_op jit(solution)/shard_map/dot_general | solution.py:234
  288.3 20.2 %collective-permute-start.33 = (bf16[128,2048]{1,0:T(8,128)(2,1)}, bf16[128,2048]{1,0:T(8,128)(2,1)S(1)}, u32[]{:S(2)}, u32[]{:S(2)}) collective-permute-start(bf16[128,2048]{1,0:T(8,128)(2,1)} %get-tuple-element.276), channel_id=1, source_target_pairs={{0,1},{1,2},{2,3},{3,0},{4,5},{5,6},{6,7},{7,4},{8,9},{9,10},{10,1... | collective-permute-start | bytes 1572872 | tf_op jit(solution)/shard_map/ppermute | solution.py:48
  308.5 8.4 %convolution_convert_fusion.1 = bf16[2048,2048]{1,0:T(8,128)(2,1)} fusion(bf16[512,2048]{1,0:T(8,128)(2,1)S(1)} %copy-done.53, bf16[512,2048]{1,0:T(8,128)(2,1)} %bitcast.94), kind=kOutput, calls=%fused_computation.1 | convolution fusion | flops 4299161600 | bytes 12582912 | tf_op jit(solution)/shard_map/dot_general | solution.py:234
  322.6 10.6 %convolution_convert_fusion.2 = bf16[512,2048]{1,0:T(8,128)(2,1)} fusion(bf16[512,2048]{1,0:T(8,128)(2,1)S(1)} %copy-done.54, bf16[2048,2048]{1,0:T(8,128)(2,1)} %all-gather.9.cloned.1.call-done), kind=kOutput, calls=%fused_computation.13 | convolution fusion | flops 4296015872 | bytes 12582912 | tf_op jit(solution)/shard_map/dot_general | solution.py:238
  333.2 10.7 %collective-permute-done.34 = bf16[128,2048]{1,0:T(8,128)(2,1)S(1)} collective-permute-done((bf16[128,2048]{1,0:T(8,128)(2,1)}, bf16[128,2048]{1,0:T(8,128)(2,1)S(1)}, u32[]{:S(2)}, u32[]{:S(2)}) %collective-permute-start.34) | collective-permute-done | bytes 524320 | tf_op jit(solution)/shard_map/ppermute | solution.py:48
  388.2 9.2 %attend_backward.1 = (bf16[1024,256]{1,0:T(8,128)(2,1)}, f32[4,512,128]{2,1,0:T(8,128)}, bf16[4,512,128]{2,1,0:T(8,128)(2,1)}, f32[4,512,128]{2,1,0:T(8,128)}, bf16[4,512,128]{2,1,0:T(8,128)(2,1)}) custom-call(s32[4]{0:T(128)} %select_reduce_fusion.low_ref, s32[4]{0:T(128)} %get-tuple-element.367.high_ref, s32[1]{0:T(128)} %bitcast.me_ref, ...), custom_call_target="tpu_custom_call" | custom-call | tf_op jit(solution)/shard_map/attend_backward/pallas_call | solution.py:384
  397.4 16.7 %collective-permute-done.41 = bf16[128,2048]{1,0:T(8,128)(2,1)} collective-permute-done((bf16[128,2048]{1,0:T(8,128)(2,1)}, bf16[128,2048]{1,0:T(8,128)(2,1)}, u32[]{:S(2)}, u32[]{:S(2)}) %collective-permute-start.41) | collective-permute-done | bytes 524320 | tf_op jit(solution)/shard_map/ppermute | solution.py:48
  453.7 15.8 %collective-permute-start.50 = (bf16[128,256]{1,0:T(8,128)(2,1)}, bf16[128,256]{1,0:T(8,128)(2,1)S(1)}, u32[]{:S(2)}, u32[]{:S(2)}) collective-permute-start(bf16[128,256]{1,0:T(8,128)(2,1)} %get-tuple-element.305), channel_id=1, source_target_pairs={{0,1},{1,2},{2,3},{3,0},{4,5},{5,6},{6,7},{7,4},{8,9},{9,10},{10,1... | collective-permute-start | bytes 196616 | tf_op jit(solution)/shard_map/ppermute | solution.py:48
  489.6 29.4 %all-to-all-done.5 = bf16[8,672,256]{2,1,0:T(8,128)(2,1)S(1)} async-done(((bf16[8,672,256]{2,1,0:T(8,128)(2,1)}), bf16[8,672,256]{2,1,0:T(8,128)(2,1)S(1)}, u32[]{:S(2)}, u32[]{:S(2)}) %all-to-all-start.5) | async-done | bytes 2752544 | tf_op jit(solution)/shard_map/all_to_all | solution.py:58
  530.4 7.0 %collective-permute-start.58 = (bf16[2,528,256]{2,0,1:T(2,128)(2,1)}, bf16[2,528,256]{2,0,1:T(2,128)(2,1)S(1)}, u32[]{:S(2)}, u32[]{:S(2)}) collective-permute-start(bf16[2,528,256]{2,0,1:T(2,128)(2,1)} %bitcast.413), channel_id=1, source_target_pairs={{0,1},{1,2},{2,3},{3,0},{4,5},{5,6},{6,7},{7,4},{8,9},{9,10},{10,1... | collective-permute-start | bytes 1622024 | tf_op jit(solution)/shard_map/ppermute | solution.py:48
  564.7 11.2 %collective-permute-done.59 = bf16[2,528,256]{2,0,1:T(2,128)(2,1)S(1)} collective-permute-done((bf16[2,528,256]{2,0,1:T(2,128)(2,1)S(1)}, bf16[2,528,256]{2,0,1:T(2,128)(2,1)S(1)}, u32[]{:S(2)}, u32[]{:S(2)}) %collective-permute-start.59) | collective-permute-done | bytes 540704 | tf_op jit(solution)/shard_map/ppermute | solution.py:48
  577.0 13.4 %collective-permute-done.62 = bf16[96,256]{1,0:T(8,128)(2,1)S(1)} collective-permute-done((bf16[96,256]{1,0:T(8,128)(2,1)S(1)}, bf16[96,256]{1,0:T(8,128)(2,1)S(1)}, u32[]{:S(2)}, u32[]{:S(2)}) %collective-permute-start.62) | collective-permute-done | bytes 49184 | tf_op jit(solution)/shard_map/ppermute | solution.py:48
  (494 shorter events, 288.7 us)
Async XLA Ops:
  7.2 131.7 %all-gather.5.cloned.1.call-start = ((), (), s32[]{:S(2)}) async-start(), calls=%async_computation.9 | async-start | bytes 9437184 | tf_op jit(solution)/shard_map/all_gather | solution.py:487
  71.7 34.6 %collective-permute-start.20 = (bf16[512,256]{1,0:T(8,128)(2,1)S(1)}, bf16[512,256]{1,0:T(8,128)(2,1)}, u32[]{:S(2)}, u32[]{:S(2)}) collective-permute-start(bf16[512,256]{1,0:T(8,128)(2,1)S(1)} %copy-done.27), channel_id=1, source_target_pairs={{0,2},{1,3},{2,0},{3,1},{4,6},{5,7},{6,4},{7,5},{8,10},{9,11},{10,... | collective-permute-start | bytes 786440 | tf_op jit(solution)/shard_map/ppermute | solution.py:25
  74.5 31.8 %collective-permute-start.21 = (bf16[512,256]{1,0:T(8,128)(2,1)S(1)}, bf16[512,256]{1,0:T(8,128)(2,1)}, u32[]{:S(2)}, u32[]{:S(2)}) collective-permute-start(bf16[512,256]{1,0:T(8,128)(2,1)S(1)} %copy-done.27), channel_id=1, source_target_pairs={{0,3},{1,0},{2,1},{3,2},{4,7},{5,4},{6,5},{7,6},{8,11},{9,8},{10,9... | collective-permute-start | bytes 786440 | tf_op jit(solution)/shard_map/ppermute | solution.py:25
  90.8 101.2 %all-gather.7.cloned.1.call-start = ((), (), s32[]{:S(2)}) async-start(), calls=%async_computation.10 | async-start | bytes 9437184 | tf_op jit(solution)/shard_map/all_gather | solution.py:509
  110.3 144.8 %all-gather.9.cloned.1.call-start = ((), (), s32[]{:S(2)}) async-start(), calls=%async_computation.11 | async-start | bytes 9437184 | tf_op jit(solution)/shard_map/all_gather | solution.py:521
  140.9 38.0 %collective-permute-start.28 = (bf16[128,2048]{1,0:T(8,128)(2,1)S(1)}, bf16[128,2048]{1,0:T(8,128)(2,1)}, u32[]{:S(2)}, u32[]{:S(2)}) collective-permute-start(bf16[128,2048]{1,0:T(8,128)(2,1)S(1)} %bitcast.426), channel_id=1, source_target_pairs={{0,2},{1,3},{2,0},{3,1},{4,6},{5,7},{6,4},{7,5},{8,10},{9,11},{10,... | collective-permute-start | bytes 1572872 | tf_op jit(solution)/shard_map/ppermute | solution.py:25
  142.9 36.1 %collective-permute-start.29 = (bf16[128,2048]{1,0:T(8,128)(2,1)S(1)}, bf16[128,2048]{1,0:T(8,128)(2,1)}, u32[]{:S(2)}, u32[]{:S(2)}) collective-permute-start(bf16[128,2048]{1,0:T(8,128)(2,1)S(1)} %bitcast.427), channel_id=1, source_target_pairs={{0,3},{1,0},{2,1},{3,2},{4,7},{5,4},{6,5},{7,6},{8,11},{9,8},{10,9... | collective-permute-start | bytes 1572872 | tf_op jit(solution)/shard_map/ppermute | solution.py:25
  157.2 322.9 %all-gather.11.cloned.1.call-start = ((), (), s32[]{:S(2)}) async-start(), calls=%async_computation.12 | async-start | bytes 9437184 | tf_op jit(solution)/shard_map/all_gather | solution.py:534
  199.9 352.4 %reduce-scatter.5.cloned.1.call-start = ((), (), s32[]{:S(2)}) async-start(), calls=%async_computation.14 | async-start | bytes 9437184 | tf_op jit(solution)/shard_map/reduce_scatter | solution.py:550
  205.1 37.0 %collective-permute-start.31 = (bf16[128,2048]{1,0:T(8,128)(2,1)}, bf16[128,2048]{1,0:T(8,128)(2,1)S(1)}, u32[]{:S(2)}, u32[]{:S(2)}) collective-permute-start(bf16[128,2048]{1,0:T(8,128)(2,1)} %get-tuple-element.263), channel_id=1, source_target_pairs={{0,2},{1,3},{2,0},{3,1},{4,6},{5,7},{6,4},{7,5},{8,10},{9,11},{10,... | collective-permute-start | bytes 1572872 | tf_op jit(solution)/shard_map/ppermute | solution.py:25
  207.5 34.6 %collective-permute-start.32 = (bf16[128,2048]{1,0:T(8,128)(2,1)}, bf16[128,2048]{1,0:T(8,128)(2,1)S(1)}, u32[]{:S(2)}, u32[]{:S(2)}) collective-permute-start(bf16[128,2048]{1,0:T(8,128)(2,1)} %get-tuple-element.263), channel_id=1, source_target_pairs={{0,3},{1,0},{2,1},{3,2},{4,7},{5,4},{6,5},{7,6},{8,11},{9,8},{10,9... | collective-permute-start | bytes 1572872 | tf_op jit(solution)/shard_map/ppermute | solution.py:25
  288.3 34.4 %collective-permute-start.33 = (bf16[128,2048]{1,0:T(8,128)(2,1)}, bf16[128,2048]{1,0:T(8,128)(2,1)S(1)}, u32[]{:S(2)}, u32[]{:S(2)}) collective-permute-start(bf16[128,2048]{1,0:T(8,128)(2,1)} %get-tuple-element.276), channel_id=1, source_target_pairs={{0,1},{1,2},{2,3},{3,0},{4,5},{5,6},{6,7},{7,4},{8,9},{9,10},{10,1... | collective-permute-start | bytes 1572872 | tf_op jit(solution)/shard_map/ppermute | solution.py:48
  367.5 187.5 %reduce-scatter.3.cloned.1.call-start = ((), (), s32[]{:S(2)}) async-start(), calls=%async_computation.13 | async-start | bytes 9437184 | tf_op jit(solution)/shard_map/reduce_scatter | solution.py:549
  377.0 37.1 %collective-permute-start.41 = (bf16[128,2048]{1,0:T(8,128)(2,1)}, bf16[128,2048]{1,0:T(8,128)(2,1)}, u32[]{:S(2)}, u32[]{:S(2)}) collective-permute-start(bf16[128,2048]{1,0:T(8,128)(2,1)} %get-tuple-element.271), channel_id=1, source_target_pairs={{0,2},{1,3},{2,0},{3,1},{4,6},{5,7},{6,4},{7,5},{8,10},{9,11},{10,... | collective-permute-start | bytes 1572872 | tf_op jit(solution)/shard_map/ppermute | solution.py:48
  379.4 34.7 %collective-permute-start.42 = (bf16[128,2048]{1,0:T(8,128)(2,1)}, bf16[128,2048]{1,0:T(8,128)(2,1)}, u32[]{:S(2)}, u32[]{:S(2)}) collective-permute-start(bf16[128,2048]{1,0:T(8,128)(2,1)} %get-tuple-element.270), channel_id=1, source_target_pairs={{0,3},{1,0},{2,1},{3,2},{4,7},{5,4},{6,5},{7,6},{8,11},{9,8},{10,9... | collective-permute-start | bytes 1572872 | tf_op jit(solution)/shard_map/ppermute | solution.py:48
  382.6 31.5 %collective-permute-start.38 = (bf16[2,128,1024]{2,1,0:T(8,128)(2,1)}, bf16[2,128,1024]{2,1,0:T(8,128)(2,1)}, u32[]{:S(2)}, u32[]{:S(2)}) collective-permute-start(bf16[2,128,1024]{2,1,0:T(8,128)(2,1)} %pad_maximum_fusion.8), channel_id=1, source_target_pairs={{0,16},{4,20},{8,24},{12,28},{16,0},{20,4},{24,8},{28,12},{1,17},{... | collective-permute-start | bytes 1572872 | tf_op jit(solution)/shard_map/ppermute | solution.py:67
  384.2 29.9 %collective-permute-start.39 = (bf16[2,128,1024]{2,1,0:T(8,128)(2,1)}, bf16[2,128,1024]{2,1,0:T(8,128)(2,1)}, u32[]{:S(2)}, u32[]{:S(2)}) collective-permute-start(bf16[2,128,1024]{2,1,0:T(8,128)(2,1)} %pad_maximum_fusion.9), channel_id=1, source_target_pairs={{0,8},{4,12},{8,0},{12,4},{16,24},{20,28},{24,16},{28,20},{1,9},{5... | collective-permute-start | bytes 1572872 | tf_op jit(solution)/shard_map/ppermute | solution.py:67
  473.0 46.0 %all-to-all-start.5 = ((bf16[8,672,256]{2,1,0:T(8,128)(2,1)}), bf16[8,672,256]{2,1,0:T(8,128)(2,1)S(1)}, u32[]{:S(2)}, u32[]{:S(2)}) async-start(bf16[8,672,256]{2,1,0:T(8,128)(2,1)} %pad_maximum_fusion), calls=%async_computation.5 | async-start | bytes 5505024 | tf_op jit(solution)/shard_map/all_to_all | solution.py:58
  523.2 34.5 %all-to-all-start.6 = ((bf16[144,8,256]{2,0,1:T(8,128)(2,1)}), bf16[144,8,256]{2,0,1:T(8,128)(2,1)}, u32[]{:S(2)}, u32[]{:S(2)}) async-start(bf16[144,8,256]{2,0,1:T(8,128)(2,1)} %bitcast.440), calls=%async_computation.6 | async-start | bytes 1179648 | tf_op jit(solution)/shard_map/all_to_all | solution.py:659
  530.4 31.1 %collective-permute-start.58 = (bf16[2,528,256]{2,0,1:T(2,128)(2,1)}, bf16[2,528,256]{2,0,1:T(2,128)(2,1)S(1)}, u32[]{:S(2)}, u32[]{:S(2)}) collective-permute-start(bf16[2,528,256]{2,0,1:T(2,128)(2,1)} %bitcast.413), channel_id=1, source_target_pairs={{0,1},{1,2},{2,3},{3,0},{4,5},{5,6},{6,7},{7,4},{8,9},{9,10},{10,1... | collective-permute-start | bytes 1622024 | tf_op jit(solution)/shard_map/ppermute | solution.py:48
  537.8 38.1 %collective-permute-start.59 = (bf16[2,528,256]{2,0,1:T(2,128)(2,1)S(1)}, bf16[2,528,256]{2,0,1:T(2,128)(2,1)S(1)}, u32[]{:S(2)}, u32[]{:S(2)}) collective-permute-start(bf16[2,528,256]{2,0,1:T(2,128)(2,1)S(1)} %bitcast.481), channel_id=1, source_target_pairs={{0,2},{1,3},{2,0},{3,1},{4,6},{5,7},{6,4},{7,5},{8,10},{9,11},{10,... | collective-permute-start | bytes 1622024 | tf_op jit(solution)/shard_map/ppermute | solution.py:48
  541.5 34.4 %collective-permute-start.60 = (bf16[2,528,256]{2,0,1:T(2,128)(2,1)}, bf16[2,528,256]{2,0,1:T(2,128)(2,1)S(1)}, u32[]{:S(2)}, u32[]{:S(2)}) collective-permute-start(bf16[2,528,256]{2,0,1:T(2,128)(2,1)} %bitcast.411), channel_id=1, source_target_pairs={{0,3},{1,0},{2,1},{3,2},{4,7},{5,4},{6,5},{7,6},{8,11},{9,8},{10,9... | collective-permute-start | bytes 1622024 | tf_op jit(solution)/shard_map/ppermute | solution.py:48
  561.0 29.4 %collective-permute-start.62 = (bf16[96,256]{1,0:T(8,128)(2,1)S(1)}, bf16[96,256]{1,0:T(8,128)(2,1)S(1)}, u32[]{:S(2)}, u32[]{:S(2)}) collective-permute-start(bf16[96,256]{1,0:T(8,128)(2,1)S(1)} %get-tuple-element.317), channel_id=1, source_target_pairs={{0,2},{1,3},{2,0},{3,1},{4,6},{5,7},{6,4},{7,5},{8,10},{9,11},{10,... | collective-permute-start | bytes 147464 | tf_op jit(solution)/shard_map/ppermute | solution.py:48
  561.5 28.8 %collective-permute-start.63 = (bf16[96,256]{1,0:T(8,128)(2,1)S(1)}, bf16[96,256]{1,0:T(8,128)(2,1)S(1)}, u32[]{:S(2)}, u32[]{:S(2)}) collective-permute-start(bf16[96,256]{1,0:T(8,128)(2,1)S(1)} %get-tuple-element.314), channel_id=1, source_target_pairs={{0,3},{1,0},{2,1},{3,2},{4,7},{5,4},{6,5},{7,6},{8,11},{9,8},{10,9... | collective-permute-start | bytes 147464 | tf_op jit(solution)/shard_map/ppermute | solution.py:48
  (108 other events, 1224.8 us)
Sparse Core Ops, SparseCore 0:
  52.7 77.8 all-gather.4
  132.4 59.5 all-gather.6
  193.9 57.0 all-gather.8
  252.8 55.8 all-gather.10
  312.0 79.1 reduce-scatter.4
  419.8 102.5 reduce-scatter.2
